TPU v7x, 32 devices: a whole 2x2x4 slice. The times are simulated.
32 devices in a mesh: lat: 4 (over y, x), lon: 8 (over z, core).
Axes of the slice: x: 2, y: 2, z: 4, core: 2. Of those that a mesh axis runs over, the one named last changes fastest.
Arguments:
- temp: float32 [40, 64, 1024], P(None, 'lat', 'lon'), may hold values from -6 to 6
- uvel: float32 [40, 64, 1024], P(None, 'lat', 'lon'), may hold values from -3 to 3
- vvel: float32 [40, 64, 1024], P(None, 'lat', 'lon'), may hold values from -3 to 3
- vert_mixing: float32 [40, 64, 1024], P(None, 'lat', 'lon'), may hold values from 0.1 to 10
- inv_dx: float32 [64, 1024], P('lat', 'lon'), may hold values from 0.5 to 2
- inv_dy: float32 [64, 1024], P('lat', 'lon'), may hold values from 0.5 to 2
- horiz_mixing: float32 [64, 1024], P('lat', 'lon'), may hold values from 0.02 to 0.1
- coriolis: float32 [64, 1024], P('lat', 'lon'), may hold values from -0.5 to 0.5
- wet_mask: int32 [40, 64, 1024], P(None, 'lat', 'lon'), may hold values from 0 to 1, as said below
- levels: int32 [64, 1024], P('lat', 'lon'), may hold values from 0 to 40, as said below
Outputs:
- temp_new: float32 [40, 64, 1024], P(None, 'lat', 'lon')
- uvel_new: float32 [40, 64, 1024], P(None, 'lat', 'lon')
- vvel_new: float32 [40, 64, 1024], P(None, 'lat', 'lon')
Inputs may be any that keep to these rules, and one draw needn't show every extreme that they name: `levels`: the number of active levels of each column; 0 marks land; some column has 40. `wet_mask`: zero at every level k with k >= levels of its column.
All inputs are finite; a program needn't handle non-finite values.
Results may differ from a plain program's by a relative error of at most 0.00002.
Values sent between devices are 32-bit elements; how exact they have to be, the bound alone decides.
No kernel may reach another device: no remote copies, remote signals or barrier semaphores. Data moves between devices by JAX's collectives and lax.ppermute only.
A program may use at most 64 MiB of HBM per device.

v0:
```python
import jax
import jax.numpy as jnp
from jax import lax
from jax.sharding import PartitionSpec as P


def partner(block, axis, bit):
    count = lax.axis_size(axis)
    route = []
    for low in range(count):
        high = low | 1 << bit
        if high != low and high < count:
            route += [(low, high), (high, low)]
    return lax.ppermute(block, axis, route)


def padded(block, sides, width, periodic):
    for axis, dim in sides:
        count = lax.axis_size(axis)
        forward = [(i, i + 1) for i in range(count - 1)]
        if periodic:
            forward.append((count - 1, 0))
        backward = [(target, source) for source, target in forward]
        low = lax.ppermute(
            lax.slice_in_dim(block, block.shape[dim] - width, None, axis=dim), axis, forward
        )
        high = lax.ppermute(lax.slice_in_dim(block, 0, width, axis=dim), axis, backward)
        block = jnp.concatenate([low, block, high], axis=dim)
    return block


def flux_difference(part, direction_axis, length, inverse_width, mixing, speed_index):
    far_left = lax.slice_in_dim(part, 0, length + 1, axis=direction_axis)
    near_left = lax.slice_in_dim(part, 1, length + 2, axis=direction_axis)
    near_right = lax.slice_in_dim(part, 2, length + 3, axis=direction_axis)
    far_right = lax.slice_in_dim(part, 3, length + 4, axis=direction_axis)
    face_mask = near_left[3] * near_right[3]
    speed = 0.5 * (near_left[speed_index] + near_right[speed_index])
    value = (7.0 * (near_left[:3] + near_right[:3]) - (far_left[:3] + far_right[:3])) / 12.0
    advect = face_mask * speed * value
    spread = face_mask * (near_right[:3] - near_left[:3])
    advect_diff = lax.slice_in_dim(advect, 1, length + 1, axis=direction_axis) - lax.slice_in_dim(
        advect, 0, length, axis=direction_axis
    )
    spread_diff = lax.slice_in_dim(spread, 1, length + 1, axis=direction_axis) - lax.slice_in_dim(
        spread, 0, length, axis=direction_axis
    )
    return -inverse_width * advect_diff + mixing * inverse_width * inverse_width * spread_diff


def horizontal_step(extended, inv_dx, inv_dy, horiz_mixing, coriolis):
    rows_in = extended.shape[2] - 4
    cols_in = extended.shape[3] - 4
    zonal_part = extended[:, :, 2 : rows_in + 2, :]
    merid_part = extended[:, :, :, 2 : cols_in + 2]
    center = extended[:, :, 2 : rows_in + 2, 2 : cols_in + 2]
    tendency = flux_difference(zonal_part, 3, cols_in, inv_dx, horiz_mixing, 1)
    tendency = tendency + flux_difference(merid_part, 2, rows_in, inv_dy, horiz_mixing, 2)
    rotation = jnp.stack([jnp.zeros_like(center[0]), coriolis * center[2], -coriolis * center[1]])
    return center[:3] + center[3] * (tendency + rotation)


def column_solve(provisional, vert_mixing, levels):
    depth = vert_mixing.shape[0]
    level_index = jnp.arange(depth, dtype=jnp.int32)[:, None, None]
    mixing_next = jnp.concatenate([vert_mixing[1:], jnp.zeros_like(vert_mixing[:1])], axis=0)
    lower = jnp.where(
        (level_index >= 1) & (level_index < levels[None]), vert_mixing, jnp.zeros_like(vert_mixing)
    )
    upper = jnp.where(level_index + 1 < levels[None], mixing_next, jnp.zeros_like(vert_mixing))
    diagonal = 1.0 + lower + upper
    gains = []
    values = []
    gain_prev = jnp.zeros_like(diagonal[0])
    value_prev = jnp.zeros_like(provisional[:, 0])
    for level in range(depth):
        denom = diagonal[level] - lower[level] * gain_prev
        gain_prev = upper[level] / denom
        value_prev = (provisional[:, level] + lower[level] * value_prev) / denom
        gains.append(gain_prev)
        values.append(value_prev)
    result = [None] * depth
    below = values[depth - 1]
    result[depth - 1] = below
    for level in range(depth - 2, -1, -1):
        below = values[level] + gains[level] * below
        result[level] = below
    return jnp.stack(result, axis=1)


def fold_rows(extended, parity):
    source = jnp.flip(extended[:, :, -4:-2], axis=2)
    lon_count = lax.axis_size("lon")
    for bit_number in range(lon_count.bit_length() - 1):
        source = partner(source, "lon", bit_number)
    mirrored = jnp.flip(source, axis=3) * parity
    top_row = lax.axis_index("lat") == lax.axis_size("lat") - 1
    north_rows = jnp.where(top_row, mirrored, extended[:, :, -2:])
    return jnp.concatenate([extended[:, :, :-2], north_rows], axis=2)


def per_device(
    temp, uvel, vvel, vert_mixing, inv_dx, inv_dy, horiz_mixing, coriolis, wet_mask, levels
):
    fields = jnp.stack([temp, uvel, vvel, wet_mask.astype(jnp.float32)])
    parity = jnp.array([1.0, -1.0, -1.0, 1.0], dtype=jnp.float32)[:, None, None, None]
    widened = padded(fields, (("lon", 3),), 2, True)
    extended = padded(widened, (("lat", 2),), 2, False)
    extended = fold_rows(extended, parity)
    provisional = horizontal_step(extended, inv_dx, inv_dy, horiz_mixing, coriolis)
    solved = column_solve(provisional, vert_mixing, levels)
    return (solved[0], solved[1], solved[2])


def solution(mesh):
    placed = (
        P(None, "lat", "lon"),
        P(None, "lat", "lon"),
        P(None, "lat", "lon"),
        P(None, "lat", "lon"),
        P("lat", "lon"),
        P("lat", "lon"),
        P("lat", "lon"),
        P("lat", "lon"),
        P(None, "lat", "lon"),
        P("lat", "lon"),
    )
    return jax.shard_map(
        per_device,
        mesh=mesh,
        in_specs=placed,
        out_specs=(P(None, "lat", "lon"), P(None, "lat", "lon"), P(None, "lat", "lon")),
        check_vma=False,
    )
```

profile of v0, /device:TPU:4, one launch (start us, length us, event | category | flops | bytes accessed | tf_op | source)
XLA Modules:
  0.0 93.3 jit_solution(3804811998291196239)
XLA Ops:
  0.6 1.7 %fusion.133 = (f32[40,16,128]{2,1,0:T(8,128)}, f32[1,40,16,128]{3,2,1,0:T(8,128)S(1)}) fusion(s32[40,16,128]{2,1,0:T(8,128)} %param.19), kind=kLoop, calls=%fused_computation.388 | loop fusion | flops 81920 | bytes 983040 | tf_op jit(solution)/shard_map/convert_element_type | solution.py:105
  2.4 0.7 copy-done.6
  3.1 1.3 %pad_maximum_fusion.2 = f32[4,40,16,128]{3,2,1,0:T(8,128)S(1)} fusion(f32[1,40,16,128]{3,2,1,0:T(8,128)S(1)} %get-tuple-element.189, f32[1,40,16,128]{3,2,1,0:T(8,128)} %bitcast.225, f32[1,40,16,128]{3,2,1,0:T(8,128)} %bitcast.228, f32[1,40,16,128]{3,2,1,0:T(8,128)} %bitcast.231), kind=kLoop, calls=%fused_computation.15 | loop fusion | flops 983040 | bytes 2621440 | tf_op jit(solution)/shard_map/stack | solution.py:105
  4.4 1.5 %fusion.132 = (f32[4,40,16,2]{3,2,1,0:T(8,128)}, f32[4,40,16,2]{3,2,1,0:T(8,128)S(1)}) fusion(f32[4,40,16,128]{3,2,1,0:T(8,128)S(1)} %pad_maximum_fusion.2), kind=kLoop, calls=%fused_computation.387 | loop fusion | bytes 81920 | tf_op jit(solution)/shard_map/slice | solution.py:25
  5.9 2.6 %copy.161 = f32[4,40,16,2]{1,2,3,0:T(8,128)} copy(f32[4,40,16,2]{3,2,1,0:T(8,128)} %get-tuple-element.121) | data formatting | bytes 40960
  8.5 1.2 %copy.162 = f32[4,40,16,2]{1,2,3,0:T(8,128)} copy(f32[4,40,16,2]{3,2,1,0:T(8,128)S(1)} %get-tuple-element.122) | data formatting | bytes 40960
  9.7 3.5 %collective-permute-start.1 = (f32[4,40,16,2]{1,2,3,0:T(8,128)}, f32[4,40,16,2]{1,2,3,0:T(8,128)S(1)}, u32[]{:S(2)}, u32[]{:S(2)}) collective-permute-start(f32[4,40,16,2]{1,2,3,0:T(8,128)} %copy.162), channel_id=1, source_target_pairs={{1,0},{2,1},{3,2},{4,3},{5,4},{6,5},{7,6},{0,7},{9,8},{10,9},{11,1... | collective-permute-start | bytes 61448 | tf_op jit(solution)/shard_map/ppermute | solution.py:27
  13.3 0.9 multiply_bitcast_fusion
  14.4 0.6 fusion.74
  16.3 0.7 fusion.80
  17.0 0.6 fusion.82
  17.6 0.6 fusion.84
  18.2 0.6 fusion.86
  18.8 0.6 fusion.88
  19.5 0.6 fusion.90
  20.2 0.6 fusion.92
  20.8 0.6 fusion.94
  21.5 0.6 fusion.96
  22.1 0.6 fusion.98
  22.7 0.6 fusion.100
  23.4 0.6 fusion.102
  24.0 0.6 fusion.104
  24.6 0.7 fusion.106
  25.3 0.6 fusion.68
  26.0 0.7 fusion.107
  26.7 0.6 fusion.134
  28.7 1.6 %copy.154 = f32[4,40,16,2]{3,1,2,0:T(8,128)} copy(f32[4,40,16,2]{1,2,3,0:T(8,128)S(1)} %collective-permute-done.1) | data formatting | bytes 40960 | tf_op jit(solution)/shard_map/ppermute | solution.py:27
  30.4 2.1 %pad_maximum_fusion.6 = (f32[4,40,2,132]{3,1,2,0:T(8,128)}, f32[4,40,2,132]{3,1,2,0:T(8,128)}) fusion(f32[4,40,16,2]{3,1,2,0:T(8,128)} %copy.154, f32[4,40,16,128]{3,1,2,0:T(8,128)S(1)} %copy.153, f32[4,40,16,2]{3,1,2,0:T(8,128)S(1)} %copy.152), kind=kLoop, calls=%fused_computation.49 | loop fusion | flops 168960 | bytes 1689600 | tf_op jit(solution)/shard_map/concatenate | solution.py:28
  32.5 1.7 %rev.8 = f32[4,40,2,132]{3,1,2,0:T(8,128)} reverse(f32[4,40,2,132]{3,1,2,0:T(8,128)} %get-tuple-element.112), dimensions={2} | reverse | bytes 337920 | tf_op jit(solution)/shard_map/jit(_flip)/rev | solution.py:92
  34.2 3.4 %collective-permute-start.2 = (f32[4,40,2,132]{3,1,2,0:T(8,128)}, f32[4,40,2,132]{3,1,2,0:T(8,128)}, u32[]{:S(2)}, u32[]{:S(2)}) collective-permute-start(f32[4,40,2,132]{3,1,2,0:T(8,128)} %get-tuple-element.112), channel_id=1, source_target_pairs={{0,8},{8,16},{16,24},{1,9},{9,17},{17,25},{2,10},{10,18},{18,26},{... | collective-permute-start | bytes 506888 | tf_op jit(solution)/shard_map/ppermute | solution.py:24
  37.7 3.5 %collective-permute-start.6 = (f32[4,40,2,132]{3,1,2,0:T(8,128)}, f32[4,40,2,132]{3,1,2,0:T(8,128)}, u32[]{:S(2)}, u32[]{:S(2)}) collective-permute-start(f32[4,40,2,132]{3,1,2,0:T(8,128)} %get-tuple-element.111), channel_id=1, source_target_pairs={{8,0},{16,8},{24,16},{9,1},{17,9},{25,17},{10,2},{18,10},{26,18},{... | collective-permute-start | bytes 506888 | tf_op jit(solution)/shard_map/ppermute | solution.py:27
  41.2 1.6 %copy.149 = f32[4,40,16,2]{3,2,1,0:T(8,128)} copy(f32[4,40,16,2]{1,2,3,0:T(8,128)S(1)} %collective-permute-done) | data formatting | bytes 40960 | tf_op jit(solution)/shard_map/ppermute | solution.py:24
  42.9 1.6 %copy.151 = f32[4,40,16,2]{3,2,1,0:T(8,128)} copy(f32[4,40,16,2]{1,2,3,0:T(8,128)S(1)} %collective-permute-done.1) | data formatting | bytes 40960 | tf_op jit(solution)/shard_map/ppermute | solution.py:27
  44.5 3.3 %maximum_maximum_fusion.1 = (f32[4,40,16,130]{3,2,1,0:T(8,128)S(1)}, f32[4,40,16,130]{3,2,1,0:T(8,128)S(1)}) fusion(f32[1,40,16,128]{3,2,1,0:T(8,128)} %copy-done.6, f32[1,40,16,128]{3,2,1,0:T(8,128)S(1)} %bitcast.226, f32[1,40,16,128]{3,2,1,0:T(8,128)S(1)} %bitcast.229, f32[1,40,16,128]{3,2,1,0:T(8,128)} %bitcast.232, f32[4,40,16,2]{3,2,1,0:T(8,128)} %copy.149, ...), kind=kLoop, calls=%fused_computation.2 | loop fusion | flops 2662400 | bytes 4014080 | tf_op jit(solution)/shard_map/concatenate | solution.py:28
  48.3 9.6 %collective-permute-done.4 = f32[4,40,2,132]{3,1,2,0:T(8,128)S(1)} collective-permute-done((f32[4,40,2,132]{3,1,2,0:T(8,128)}, f32[4,40,2,132]{3,1,2,0:T(8,128)S(1)}, u32[]{:S(2)}, u32[]{:S(2)}) %collective-permute-start.4) | collective-permute-done | bytes 168992 | tf_op jit(solution)/shard_map/ppermute | solution.py:14
  57.9 0.8 collective-permute-start.5
  58.7 3.1 %fusion.1 = (f32[3,40,16,129]{3,2,1,0:T(8,128)}, f32[3,40,16,129]{3,2,1,0:T(8,128)}) fusion(f32[4,40,16,130]{3,2,1,0:T(8,128)S(1)} %get-tuple-element.120, f32[4,40,16,130]{3,2,1,0:T(8,128)S(1)} %get-tuple-element.119, f32[40,16,129]{2,1,0:T(8,128)S(1)} %get-tuple-element.107, f32[40,16,129]{2,1,0:T(8,128)S(1)} %get-tuple-element.108), kind=kLoop, calls=%fused_computation.6 | loop fusion | flops 1733760 | bytes 6604800 | tf_op jit(solution)/shard_map/mul | solution.py:40
  61.8 13.2 %collective-permute-done.5 = f32[4,40,2,132]{3,1,2,0:T(8,128)} collective-permute-done((f32[4,40,2,132]{3,1,2,0:T(8,128)S(1)}, f32[4,40,2,132]{3,1,2,0:T(8,128)}, u32[]{:S(2)}, u32[]{:S(2)}) %collective-permute-start.5) | collective-permute-done | bytes 168992 | tf_op jit(solution)/shard_map/ppermute | solution.py:14
  74.9 1.8 %reverse = f32[4,40,2,256]{3,1,2,0:T(8,128)} reverse(f32[4,40,2,256]{3,1,2,0:T(8,128)} %bitcast.224), dimensions={3} | reverse | bytes 655360
  76.7 1.2 %multiply_select_fusion = f32[4,40,2,132]{3,1,2,0:T(8,128)S(1)} fusion(f32[4,40,2,132]{3,1,2,0:T(8,128)} %collective-permute-done.6, f32[4]{0:T(128)S(1)} %copy-done.80, pred[]{:T(512)S(6)} %eq.3, f32[4,40,2,256]{3,1,2,0:T(8,128)} %reverse), kind=kLoop, calls=%fused_computation.57 | loop fusion | flops 84480 | bytes 506897 | tf_op jit(solution)/shard_map/jit(_where)/select_n | solution.py:98
  78.0 1.1 %fusion.24 = f32[40,17,128]{2,0,1:T(8,128)S(1)} fusion(f32[4,40,2,132]{3,1,2,0:T(8,128)S(1)} %multiply_select_fusion, f32[4,40,16,2]{3,1,2,0:T(8,128)} %copy.154, f32[4,40,16,128]{3,1,2,0:T(8,128)S(1)} %copy.153, f32[4,40,16,2]{3,1,2,0:T(8,128)S(1)} %copy.152, f32[4,40,2,132]{3,1,2,0:T(8,128)} %collective-permute-done.2), kind=kLoop, calls=%fused_computation.42 | loop fusion | flops 609280 | bytes 2037760 | tf_op jit(solution)/shard_map/mul | solution.py:41
  79.3 1.2 %fusion.23 = f32[40,17,128]{2,0,1:T(8,128)S(1)} fusion(f32[4,40,2,132]{3,1,2,0:T(8,128)S(1)} %multiply_select_fusion, f32[4,40,16,2]{3,1,2,0:T(8,128)S(1)} %copy-done, f32[4,40,16,128]{3,1,2,0:T(8,128)S(1)} %copy.153, f32[4,40,16,2]{3,1,2,0:T(8,128)S(1)} %copy.152, f32[4,40,2,132]{3,1,2,0:T(8,128)} %collective-permute-done.2), kind=kLoop, calls=%fused_computation.40 | loop fusion | flops 1479680 | bytes 2037760 | tf_op jit(solution)/shard_map/mul | solution.py:40
  80.6 3.6 %pad_maximum_fusion = (f32[4,40,18,132]{3,1,2,0:T(8,128)S(1)}, f32[4,40,18,132]{3,1,2,0:T(8,128)S(1)}) fusion(f32[4,40,2,132]{3,1,2,0:T(8,128)S(1)} %multiply_select_fusion, f32[4,40,16,2]{3,1,2,0:T(8,128)S(1)} %copy-done, f32[4,40,16,128]{3,1,2,0:T(8,128)S(1)} %copy.153, f32[4,40,16,2]{3,1,2,0:T(8,128)S(1)} %copy.152, ...), kind=kLoop, calls=%fused_computation.1 | loop fusion | flops 2280960 | bytes 4730880 | tf_op jit(solution)/shard_map/concatenate | solution.py:99
  84.2 1.1 %fusion.130 = (f32[3,40,17,128]{3,1,2,0:T(8,128)S(1)}, f32[3,40,17,128]{3,1,2,0:T(8,128)S(1)}, f32[3,40,17,128]{3,1,2,0:T(8,128)S(1)}, f32[3,40,17,128]{3,1,2,0:T(8,128)S(1)}) fusion(f32[4,40,18,132]{3,1,2,0:T(8,128)S(1)} %get-tuple-element.110, f32[4,40,18,132]{3,1,2,0:T(8,128)S(1)} %get-tuple-element.109), kind=kLoop, calls=%fused_computation.385 | loop fusion | bytes 8355840 | tf_op jit(solution)/shard_map/slice | solution.py:39
  85.4 0.9 fusion.4
  88.1 1.6 %fusion.11 = f32[3,40,16,128]{3,2,1,0:T(8,128)S(1)} fusion(f32[3,40,17,128]{3,2,1,0:T(8,128)S(1)} %get-tuple-element.118, f32[3,40,17,128]{3,2,1,0:T(8,128)S(1)} %get-tuple-element.117, f32[3,40,16,129]{3,2,1,0:T(8,128)S(1)} %copy-done.2, f32[3,40,16,129]{3,2,1,0:T(8,128)S(1)} %copy-done.1, f32[1,40,16,128]{3,2,1,0:T(8,128)S(1)} %bitcast.227, ...), kind=kLoop, calls=%fused_computation.22 | loop fusion | flops 4423680 | bytes 10846220 | tf_op jit(solution)/shard_map/add | solution.py:60
  90.1 1.7 %constant_dynamic-update-slice_fusion.39 = (f32[3,40,16,128]{3,2,1,0:T(8,128)S(1)}, f32[3,1,16,128]{3,2,1,0:T(8,128)S(1)}, f32[3,1,16,128]{3,2,1,0:T(8,128)S(1)}...) fusion(f32[16,128]{1,0:T(8,128)} %get-tuple-element.126, ...), kind=kLoop, calls=%fused_computation.100 | loop fusion | flops 1210367 | bytes 2916352
  92.3 1.0 %slice_bitcast_fusion = (f32[40,16,128]{2,1,0:T(8,128)}, f32[40,16,128]{2,1,0:T(8,128)}, f32[40,16,128]{2,1,0:T(8,128)}) fusion(f32[3,40,16,128]{3,2,1,0:T(8,128)S(1)} %constant_dynamic-update-slice_fusion), kind=kLoop, calls=%fused_computation.46 | loop fusion | bytes 1966080 | tf_op jit(solution)/shard_map/squeeze | solution.py:112
  (223 shorter events, 5.7 us)
Async XLA Ops:
  5.9 7.3 %copy-start.75 = (f32[16,128]{1,0:T(8,128)S(1)}, f32[16,128]{1,0:T(8,128)}, u32[]{:S(2)}) copy-start(f32[16,128]{1,0:T(8,128)} %param.18) | copy-start | bytes 24580
  5.9 7.4 %copy-start.3 = (f32[40,16,128]{2,1,0:T(8,128)S(1)}, f32[40,16,128]{2,1,0:T(8,128)}, u32[]{:S(2)}) copy-start(f32[40,16,128]{2,1,0:T(8,128)} %param.13) | copy-start | bytes 983044
  5.9 7.4 %copy-start.4 = (f32[40,16,128]{2,1,0:T(8,128)S(1)}, f32[40,16,128]{2,1,0:T(8,128)}, u32[]{:S(2)}) copy-start(f32[40,16,128]{2,1,0:T(8,128)} %param.12) | copy-start | bytes 983044
  8.5 5.7 %copy-start.76 = (s32[16,128]{1,0:T(8,128)S(1)}, s32[16,128]{1,0:T(8,128)}, u32[]{:S(2)}) copy-start(s32[16,128]{1,0:T(8,128)} %param.20) | copy-start | bytes 24580
  8.5 19.7 %collective-permute-start = (f32[4,40,16,2]{1,2,3,0:T(8,128)}, f32[4,40,16,2]{1,2,3,0:T(8,128)S(1)}, u32[]{:S(2)}, u32[]{:S(2)}) collective-permute-start(f32[4,40,16,2]{1,2,3,0:T(8,128)} %copy.161), channel_id=1, source_target_pairs={{0,1},{1,2},{2,3},{3,4},{4,5},{5,6},{6,7},{7,0},{8,9},{9,10},{10,1... | collective-permute-start | bytes 61448 | tf_op jit(solution)/shard_map/ppermute | solution.py:24
  9.7 4.5 %copy-start.10 = (f32[40,16,128]{2,1,0:T(8,128)S(1)}, f32[40,16,128]{2,1,0:T(8,128)}, u32[]{:S(2)}) copy-start(f32[40,16,128]{2,1,0:T(8,128)} %param.14) | copy-start | bytes 983044
  9.7 4.5 %slice-start = ((f32[40,16,128]{2,1,0:T(8,128)}), f32[39,16,128]{2,1,0:T(8,128)S(1)}, s32[]{:S(2)}) async-start(f32[40,16,128]{2,1,0:T(8,128)} %param.14), calls=%async_computation | async-start | bytes 638976 | tf_op jit(solution)/shard_map/slice | solution.py:66
  9.7 19.0 %collective-permute-start.1 = (f32[4,40,16,2]{1,2,3,0:T(8,128)}, f32[4,40,16,2]{1,2,3,0:T(8,128)S(1)}, u32[]{:S(2)}, u32[]{:S(2)}) collective-permute-start(f32[4,40,16,2]{1,2,3,0:T(8,128)} %copy.162), channel_id=1, source_target_pairs={{1,0},{2,1},{3,2},{4,3},{5,4},{6,5},{7,6},{0,7},{9,8},{10,9},{11,1... | collective-permute-start | bytes 61448 | tf_op jit(solution)/shard_map/ppermute | solution.py:27
  14.2 12.5 %copy-start.77 = (f32[16,128]{1,0:T(8,128)S(1)}, f32[16,128]{1,0:T(8,128)}, u32[]{:S(2)}) copy-start(f32[16,128]{1,0:T(8,128)} %param.15) | copy-start | bytes 24580
  14.2 12.5 %copy-start.78 = (f32[16,128]{1,0:T(8,128)S(1)}, f32[16,128]{1,0:T(8,128)}, u32[]{:S(2)}) copy-start(f32[16,128]{1,0:T(8,128)} %param.17) | copy-start | bytes 24580
  14.2 12.5 %copy-start.79 = (f32[16,128]{1,0:T(8,128)S(1)}, f32[16,128]{1,0:T(8,128)}, u32[]{:S(2)}) copy-start(f32[16,128]{1,0:T(8,128)} %param.16) | copy-start | bytes 24580
  14.4 6.4 %copy-start.38 = (f32[1,16,128]{2,1,0:T(8,128)}, f32[1,16,128]{2,1,0:T(8,128)S(1)}, u32[]{:S(2)}) copy-start(f32[1,16,128]{2,1,0:T(8,128)S(1)} %get-tuple-element.46) | copy-start | bytes 24580
  15.0 5.8 %copy-start.40 = (f32[1,16,128]{2,1,0:T(8,128)}, f32[1,16,128]{2,1,0:T(8,128)S(1)}, u32[]{:S(2)}) copy-start(f32[1,16,128]{2,1,0:T(8,128)S(1)} %get-tuple-element.50) | copy-start | bytes 24580
  15.7 8.3 %copy-start.42 = (f32[1,16,128]{2,1,0:T(8,128)}, f32[1,16,128]{2,1,0:T(8,128)S(1)}, u32[]{:S(2)}) copy-start(f32[1,16,128]{2,1,0:T(8,128)S(1)} %get-tuple-element.53) | copy-start | bytes 24580
  16.3 3.8 %copy-start.44 = (f32[1,16,128]{2,1,0:T(8,128)}, f32[1,16,128]{2,1,0:T(8,128)S(1)}, u32[]{:S(2)}) copy-start(f32[1,16,128]{2,1,0:T(8,128)S(1)} %get-tuple-element.55) | copy-start | bytes 24580
  16.3 8.3 %copy-start.46 = (f32[1,16,128]{2,1,0:T(8,128)}, f32[1,16,128]{2,1,0:T(8,128)S(1)}, u32[]{:S(2)}) copy-start(f32[1,16,128]{2,1,0:T(8,128)S(1)} %get-tuple-element.56) | copy-start | bytes 24580
  17.0 3.2 %copy-start.11 = (f32[1,16,128]{2,1,0:T(8,128)}, f32[1,16,128]{2,1,0:T(8,128)S(1)}, u32[]{:S(2)}) copy-start(f32[1,16,128]{2,1,0:T(8,128)S(1)} %get-tuple-element.59) | copy-start | bytes 24580
  17.0 3.2 %copy-start.48 = (f32[1,16,128]{2,1,0:T(8,128)}, f32[1,16,128]{2,1,0:T(8,128)S(1)}, u32[]{:S(2)}) copy-start(f32[1,16,128]{2,1,0:T(8,128)S(1)} %get-tuple-element.58) | copy-start | bytes 24580
  17.6 3.9 %copy-start.50 = (f32[1,16,128]{2,1,0:T(8,128)}, f32[1,16,128]{2,1,0:T(8,128)S(1)}, u32[]{:S(2)}) copy-start(f32[1,16,128]{2,1,0:T(8,128)S(1)} %get-tuple-element.62) | copy-start | bytes 24580
  18.2 3.9 %copy-start.52 = (f32[1,16,128]{2,1,0:T(8,128)}, f32[1,16,128]{2,1,0:T(8,128)S(1)}, u32[]{:S(2)}) copy-start(f32[1,16,128]{2,1,0:T(8,128)S(1)} %get-tuple-element.65) | copy-start | bytes 24580
  18.8 3.9 %copy-start.54 = (f32[1,16,128]{2,1,0:T(8,128)}, f32[1,16,128]{2,1,0:T(8,128)S(1)}, u32[]{:S(2)}) copy-start(f32[1,16,128]{2,1,0:T(8,128)S(1)} %get-tuple-element.68) | copy-start | bytes 24580
  19.5 3.9 %copy-start.56 = (f32[1,16,128]{2,1,0:T(8,128)}, f32[1,16,128]{2,1,0:T(8,128)S(1)}, u32[]{:S(2)}) copy-start(f32[1,16,128]{2,1,0:T(8,128)S(1)} %get-tuple-element.70) | copy-start | bytes 24580
  19.5 4.5 %copy-start.58 = (f32[1,16,128]{2,1,0:T(8,128)}, f32[1,16,128]{2,1,0:T(8,128)S(1)}, u32[]{:S(2)}) copy-start(f32[1,16,128]{2,1,0:T(8,128)S(1)} %get-tuple-element.71) | copy-start | bytes 24580
  20.1 4.5 %copy-start.13 = (f32[1,16,128]{2,1,0:T(8,128)}, f32[1,16,128]{2,1,0:T(8,128)S(1)}, u32[]{:S(2)}) copy-start(f32[1,16,128]{2,1,0:T(8,128)S(1)} %get-tuple-element.73) | copy-start | bytes 24580
  20.8 4.5 %copy-start.17 = (f32[1,16,128]{2,1,0:T(8,128)}, f32[1,16,128]{2,1,0:T(8,128)S(1)}, u32[]{:S(2)}) copy-start(f32[1,16,128]{2,1,0:T(8,128)S(1)} %get-tuple-element.76) | copy-start | bytes 24580
  20.8 5.2 %copy-start.19 = (f32[1,16,128]{2,1,0:T(8,128)}, f32[1,16,128]{2,1,0:T(8,128)S(1)}, u32[]{:S(2)}) copy-start(f32[1,16,128]{2,1,0:T(8,128)S(1)} %get-tuple-element.77) | copy-start | bytes 24580
  21.5 2.5 %copy-start.60 = (f32[1,16,128]{2,1,0:T(8,128)}, f32[1,16,128]{2,1,0:T(8,128)S(1)}, u32[]{:S(2)}) copy-start(f32[1,16,128]{2,1,0:T(8,128)S(1)} %get-tuple-element.79) | copy-start | bytes 24580
  22.7 2.6 %copy-start.72 = (f32[1,16,128]{2,1,0:T(8,128)}, f32[1,16,128]{2,1,0:T(8,128)S(1)}, u32[]{:S(2)}) copy-start(f32[1,16,128]{2,1,0:T(8,128)S(1)} %get-tuple-element.85) | copy-start | bytes 24580
  23.4 3.3 %copy-start.73 = (f32[1,16,128]{2,1,0:T(8,128)}, f32[1,16,128]{2,1,0:T(8,128)S(1)}, u32[]{:S(2)}) copy-start(f32[1,16,128]{2,1,0:T(8,128)S(1)} %get-tuple-element.88) | copy-start | bytes 24580
  24.6 2.0 %copy-start.21 = (f32[1,16,128]{2,1,0:T(8,128)}, f32[1,16,128]{2,1,0:T(8,128)S(1)}, u32[]{:S(2)}) copy-start(f32[1,16,128]{2,1,0:T(8,128)S(1)} %get-tuple-element.94) | copy-start | bytes 24580
  34.2 43.8 %collective-permute-start.2 = (f32[4,40,2,132]{3,1,2,0:T(8,128)}, f32[4,40,2,132]{3,1,2,0:T(8,128)}, u32[]{:S(2)}, u32[]{:S(2)}) collective-permute-start(f32[4,40,2,132]{3,1,2,0:T(8,128)} %get-tuple-element.112), channel_id=1, source_target_pairs={{0,8},{8,16},{16,24},{1,9},{9,17},{17,25},{2,10},{10,18},{18,26},{... | collective-permute-start | bytes 506888 | tf_op jit(solution)/shard_map/ppermute | solution.py:24
  37.6 10.2 %collective-permute-start.3 = (f32[4,40,2,132]{3,1,2,0:T(8,128)}, f32[4,40,2,132]{3,1,2,0:T(8,128)}, u32[]{:S(2)}, u32[]{:S(2)}) collective-permute-start(f32[4,40,2,132]{3,1,2,0:T(8,128)} %rev.8), channel_id=1, source_target_pairs={{0,1},{1,0},{2,3},{3,2},{4,5},{5,4},{6,7},{7,6},{8,9},{9,8},{10,11... | collective-permute-start | bytes 506888 | tf_op jit(solution)/shard_map/ppermute | solution.py:14
  37.7 39.0 %collective-permute-start.6 = (f32[4,40,2,132]{3,1,2,0:T(8,128)}, f32[4,40,2,132]{3,1,2,0:T(8,128)}, u32[]{:S(2)}, u32[]{:S(2)}) collective-permute-start(f32[4,40,2,132]{3,1,2,0:T(8,128)} %get-tuple-element.111), channel_id=1, source_target_pairs={{8,0},{16,8},{24,16},{9,1},{17,9},{25,17},{10,2},{18,10},{26,18},{... | collective-permute-start | bytes 506888 | tf_op jit(solution)/shard_map/ppermute | solution.py:27
  47.8 10.1 %collective-permute-start.4 = (f32[4,40,2,132]{3,1,2,0:T(8,128)}, f32[4,40,2,132]{3,1,2,0:T(8,128)S(1)}, u32[]{:S(2)}, u32[]{:S(2)}) collective-permute-start(f32[4,40,2,132]{3,1,2,0:T(8,128)} %collective-permute-done.3), channel_id=1, source_target_pairs={{0,2},{2,0},{1,3},{3,1},{4,6},{6,4},{5,7},{7,5},{8,10},{10,8},{9,1... | collective-permute-start | bytes 506888 | tf_op jit(solution)/shard_map/ppermute | solution.py:14
  57.9 17.0 %collective-permute-start.5 = (f32[4,40,2,132]{3,1,2,0:T(8,128)S(1)}, f32[4,40,2,132]{3,1,2,0:T(8,128)}, u32[]{:S(2)}, u32[]{:S(2)}) collective-permute-start(f32[4,40,2,132]{3,1,2,0:T(8,128)S(1)} %collective-permute-done.4), channel_id=1, source_target_pairs={{0,4},{4,0},{1,5},{5,1},{2,6},{6,2},{3,7},{7,3},{8,12},{12,8},{9,1... | collective-permute-start | bytes 506888 | tf_op jit(solution)/shard_map/ppermute | solution.py:14
  58.7 18.0 %copy-start.80 = (f32[4]{0:T(128)S(1)}, f32[4]{0:T(128)}, u32[]{:S(2)}) copy-start(f32[4]{0:T(128)} %constant.5.clone) | copy-start | bytes 52
  85.4 2.1 %copy-start.2 = (f32[3,40,16,129]{3,2,1,0:T(8,128)S(1)}, f32[3,40,16,129]{3,2,1,0:T(8,128)}, u32[]{:S(2)}) copy-start(f32[3,40,16,129]{3,2,1,0:T(8,128)} %get-tuple-element.106) | copy-start | bytes 2972164
  85.4 2.1 %copy-start.5 = (f32[40,16,128]{2,1,0:T(8,128)S(1)}, f32[40,16,128]{2,1,0:T(8,128)}, u32[]{:S(2)}) copy-start(f32[40,16,128]{2,1,0:T(8,128)} %param.11) | copy-start | bytes 983044
  85.4 2.2 %copy-start.7 = (f32[40,16,128]{2,1,0:T(8,128)S(1)}, f32[40,16,128]{2,1,0:T(8,128)}, u32[]{:S(2)}) copy-start(f32[40,16,128]{2,1,0:T(8,128)} %get-tuple-element.188) | copy-start | bytes 983044
  85.4 2.3 %copy-start.8 = (f32[1,40,16,128]{3,2,1,0:T(8,128)S(1)}, f32[1,40,16,128]{3,2,1,0:T(8,128)}, u32[]{:S(2)}) copy-start(f32[1,40,16,128]{3,2,1,0:T(8,128)} %get-tuple-element.196) | copy-start | bytes 983044
  85.4 2.4 %copy-start.9 = (f32[1,40,16,128]{3,2,1,0:T(8,128)S(1)}, f32[1,40,16,128]{3,2,1,0:T(8,128)}, u32[]{:S(2)}) copy-start(f32[1,40,16,128]{3,2,1,0:T(8,128)} %get-tuple-element.197) | copy-start | bytes 983044
  87.8 2.0 %copy-start.20 = (f32[1,16,128]{2,1,0:T(8,128)S(1)}, f32[1,16,128]{2,1,0:T(8,128)}, u32[]{:S(2)}) copy-start(f32[1,16,128]{2,1,0:T(8,128)} %copy-done.19) | copy-start | bytes 24580
  87.8 2.0 %copy-start.22 = (f32[1,16,128]{2,1,0:T(8,128)S(1)}, f32[1,16,128]{2,1,0:T(8,128)}, u32[]{:S(2)}) copy-start(f32[1,16,128]{2,1,0:T(8,128)} %copy-done.21) | copy-start | bytes 24580
  87.9 2.0 %copy-start.24 = (f32[1,16,128]{2,1,0:T(8,128)S(1)}, f32[1,16,128]{2,1,0:T(8,128)}, u32[]{:S(2)}) copy-start(f32[1,16,128]{2,1,0:T(8,128)} %copy-done.23) | copy-start | bytes 24580
  87.9 2.0 %copy-start.26 = (f32[1,16,128]{2,1,0:T(8,128)S(1)}, f32[1,16,128]{2,1,0:T(8,128)}, u32[]{:S(2)}) copy-start(f32[1,16,128]{2,1,0:T(8,128)} %copy-done.25) | copy-start | bytes 24580
  87.9 2.0 %copy-start.27 = (f32[16,128]{1,0:T(8,128)S(1)}, f32[16,128]{1,0:T(8,128)}, u32[]{:S(2)}) copy-start(f32[16,128]{1,0:T(8,128)} %get-tuple-element.69) | copy-start | bytes 24580
  87.9 2.0 %copy-start.28 = (f32[16,128]{1,0:T(8,128)S(1)}, f32[16,128]{1,0:T(8,128)}, u32[]{:S(2)}) copy-start(f32[16,128]{1,0:T(8,128)} %get-tuple-element.90) | copy-start | bytes 24580
  87.9 2.0 %copy-start.29 = (f32[16,128]{1,0:T(8,128)S(1)}, f32[16,128]{1,0:T(8,128)}, u32[]{:S(2)}) copy-start(f32[16,128]{1,0:T(8,128)} %get-tuple-element.66) | copy-start | bytes 24580
  (41 other events, 68.0 us)
where the time goes:
time: 94.4 us; the launch traced here: 93.3 us
  other arithmetic  37.1 us (39%)
  waiting for transfers between devices  22.8 us (24%)
  local copies, waits for them, and re-layouts  20.1 us (21%)
  starting transfers between devices  11.4 us (12%)
  between operations  1.92 us (2%)
    ppermute x3, waiting for transfers between devices, partner(): return lax.ppermute(block, axis, route)  22.8 us
    mul x19, other arithmetic, column_solve(): below = values[level] + gains[level] * below  11.4 us
    unnamed x184, local copies, waits for them, and re-layouts  8.31 us
    ppermute x2, starting transfers between devices, padded(): lax.ppermute(lax.slice_in_dim(block, 0, width, axis=dim), axis, backward)  7.06 us
    mul x4, other arithmetic, flux_difference(): advect = face_mask * speed * value  5.56 us
    concatenate x2, other arithmetic, padded(): block = jnp.concatenate([low, block, high], axis=dim)  5.47 us
    concatenate x1, other arithmetic, fold_rows(): return jnp.concatenate([extended[:, :, :-2], north_rows], axis=2)  3.58 us
    ppermute x2, starting transfers between devices, padded(): lax.ppermute(lax.slice_in_dim(block, block.shape[dim] - width, None, axis...  3.39 us
  transfers between devices with their start and end apart: 7, of which 2 were waited for; matrix products, arithmetic and copies ran while one was open for 31% of the time, Pallas kernels for 0%

commit v1 on v0

v1 whole, which is shorter than its diff:
```python
import jax
import jax.numpy as jnp
from jax import lax
from jax.experimental import pallas as pl
from jax.experimental.pallas import tpu as pltpu
from jax.sharding import PartitionSpec as P

ROWS = 16
LANES = 128
VMEM = pl.BlockSpec(memory_space=pltpu.VMEM)
TAIL = 4


def lane_index(rows):
    return lax.broadcasted_iota(jnp.int32, (rows, LANES), 1)


def slab_place(depth, level, field):
    if level < 32:
        return field, 4 * level
    return TAIL, 32 * field + 4 * (level - 32)


def level_rows(row, depth):
    return pl.ds(row, depth, stride=ROWS)


def pack_kernel(temp, uvel, vvel, mask, first, second, edges):
    depth = temp.shape[0] // ROWS
    odd = lax.rem(lax.axis_index("lat"), 2)
    for out, near in ((first, (ROWS - 1) * (1 - odd)), (second, (ROWS - 1) * odd)):
        far = near + jnp.where(near == 0, 1, -1)
        for number, field in enumerate((temp, uvel, vvel)):
            base = 2 * depth * number
            out[base : base + depth, :] = field[level_rows(near, depth), :]
            out[base + depth : base + 2 * depth, :] = field[level_rows(far, depth), :]
        out[6 * depth : 7 * depth, :] = mask[level_rows(near, depth), :].astype(jnp.float32)
    lane = lane_index(ROWS)
    slabs = [jnp.zeros((ROWS, LANES), jnp.float32) for _ in range(TAIL + 1)]
    for level in range(depth):
        for number, field in enumerate((temp, uvel, vvel, mask)):
            block = field[level * ROWS : (level + 1) * ROWS, :].astype(jnp.float32)
            slab, start = slab_place(depth, level, number)
            moved = pltpu.roll(block, (start + 2) % LANES, 1)
            slabs[slab] = jnp.where(lane // 4 == start // 4, moved, slabs[slab])
    for number, slab in enumerate(slabs):
        edges[number * ROWS : (number + 1) * ROWS, :] = slab


def interior_kernel(
    temp, uvel, vvel, mask, mixing, inv_dx, inv_dy, spread, coriolis, levels, prov, solve
):
    depth = temp.shape[0] // ROWS
    lane = lane_index(ROWS)
    row = lax.broadcasted_iota(jnp.int32, (ROWS, LANES), 0)
    zonal = (inv_dx[...] * (-1.0 / 24.0), spread[...] * inv_dx[...] * inv_dx[...])
    merid = (inv_dy[...] * (-1.0 / 24.0), spread[...] * inv_dy[...] * inv_dy[...])
    turn = coriolis[...]
    active = levels[...]
    gain = jnp.zeros((ROWS, LANES), jnp.float32)
    lower = jnp.zeros((ROWS, LANES), jnp.float32)
    for level in range(depth):
        here = slice(level * ROWS, (level + 1) * ROWS)
        if level + 1 < depth:
            upper = jnp.where(
                level + 1 < active, mixing[(level + 1) * ROWS : (level + 2) * ROWS, :], 0.0
            )
        else:
            upper = jnp.zeros((ROWS, LANES), jnp.float32)
        inverse = 1.0 / (1.0 + lower + upper - lower * gain)
        gain = upper * inverse
        solve[0, here, :] = inverse
        solve[1, here, :] = lower * inverse
        solve[2, here, :] = gain
        lower = upper

        wet = mask[here, :].astype(jnp.float32)
        fields = [temp[here, :], uvel[here, :], vvel[here, :]]
        total = [None, None, None]
        for axis, size, index, scale, speed_of in (
            (1, LANES, lane, zonal, 1),
            (0, ROWS, row, merid, 2),
        ):
            face = jnp.where(index >= 1, pltpu.roll(wet, 1, axis), 0.0) * wet
            face_next = pltpu.roll(face, size - 1, axis)
            before = [pltpu.roll(q, 1, axis) for q in fields]
            speed = face * (before[speed_of] + fields[speed_of])
            for number, q in enumerate(fields):
                back = before[number]
                back2 = jnp.where(index >= 2, pltpu.roll(back, 1, axis), 0.0)
                ahead = pltpu.roll(q, size - 1, axis)
                ahead0 = jnp.where(index < size - 1, ahead, 0.0)
                advect = speed * (7.0 * (back + q) - (back2 + ahead0))
                advect_diff = pltpu.roll(advect, size - 1, axis) - advect
                spread_diff = face_next * (ahead - q) - face * (q - back)
                part = scale[0] * advect_diff + scale[1] * spread_diff
                total[number] = part if total[number] is None else total[number] + part
        total[1] = total[1] + turn * fields[2]
        total[2] = total[2] - turn * fields[1]
        for number, q in enumerate(fields):
            prov[number, here, :] = q + wet * total[number]


def finish_kernel(
    prov, solve, sent1, got1, sent2, got2, edges, east1, east2, mask, inv_dx, inv_dy, spread,
    temp_new, uvel_new, vvel_new, work, scratch
):
    depth = prov.shape[1] // ROWS
    odd = lax.rem(lax.axis_index("lat"), 2)
    fold = lax.axis_index("lat") == lax.axis_size("lat") - 1
    lon_odd = lax.rem(lax.axis_index("lon"), 2) == 1
    outs = (temp_new, uvel_new, vvel_new)

    lane = lane_index(ROWS)
    quad = lane % 4

    def wrap(x, shift):
        return pltpu.roll(x, shift % LANES, 1)

    four = jnp.where(quad < 2, LANES - 2 + quad, quad - 2)

    def replicate(x):
        return jnp.take_along_axis(x, four, axis=1, mode="promise_in_bounds")

    wide = replicate(inv_dx[...])
    wide2 = replicate(spread[...]) * wide * wide

    def slab_of(ref, number):
        return ref[number * ROWS : (number + 1) * ROWS, :]

    own = [slab_of(edges, s) for s in range(TAIL + 1)]
    first = [slab_of(east1, s) for s in range(TAIL + 1)]
    second = [slab_of(east2, s) for s in range(TAIL + 1)]
    west = [jnp.where(quad < 2, jnp.where(lon_odd, a, b), o) for a, b, o in zip(first, second, own)]
    east = [jnp.where(quad < 2, o, jnp.where(lon_odd, b, a)) for a, b, o in zip(first, second, own)]

    def split(slabs):
        tail = [slabs[TAIL] if f == 0 else wrap(slabs[TAIL], -32 * f) for f in range(4)]
        return [slabs[:TAIL], tail]

    corrections = []
    for west_part, east_part in zip(split(west), split(east)):
        wet = west_part[3]
        face = wrap(wet, 1) * wet
        face_next = wrap(face, -1)
        speed_sum = wrap(west_part[1], 1) + west_part[1]
        speed = face * speed_sum * (1.0 / 24.0)
        speed_next = wrap(speed, -1)
        wet_e = east_part[3]
        face_e = wrap(wet_e, -1) * wet_e
        speed_e = face_e * (wrap(east_part[1], -1) + east_part[1]) * (1.0 / 24.0)
        speed_e_before = wrap(speed_e, 1)
        part = []
        for number in range(3):
            q = west_part[number]
            back = wrap(q, 1)
            advect = speed * (7.0 * (back + q) - (wrap(q, 2) + wrap(q, -1)))
            reach = speed_next * back
            near = wide * (advect + reach) - wide2 * (face * (q - back))
            distant = wrap(reach, 1) * wide
            q = east_part[number]
            ahead = wrap(q, -1)
            advect = speed_e * (7.0 * (ahead + q) - (wrap(q, -2) + wrap(q, 1)))
            reach = speed_e_before * ahead
            near_e = wide2 * (face_e * (ahead - q)) - wide * (advect + reach)
            distant_e = wrap(reach, -1) * wide
            part.append(
                jnp.where(
                    quad < 2,
                    jnp.where(quad == 0, distant_e, near_e),
                    jnp.where(quad == 2, near, -distant),
                )
            )
        corrections.append(part)

    border = (lane < 2) | (lane >= LANES - 2)
    for level in range(depth):
        here = slice(level * ROWS, (level + 1) * ROWS)
        for number in range(3):
            if level < 32:
                source, start = corrections[0][number], 4 * level
            else:
                source, start = corrections[1][number], 4 * (level - 32)
            moved = jnp.where(border, wrap(source, -(start + 2)), 0.0)
            work[number, here, :] = prov[number, here, :] + moved

    flipped = lax.broadcasted_iota(jnp.int32, (7 * depth, LANES), 1)
    flipped = jnp.where(fold, LANES - 1 - flipped, flipped)
    scratch[...] = jnp.take_along_axis(got2[...], flipped, axis=1, mode="promise_in_bounds")
    minus = jnp.where(fold, -1.0, 1.0)
    for mine, ghost, near_row, turned in (
        (sent1, got1, (ROWS - 1) * (1 - odd), False),
        (sent2, scratch, (ROWS - 1) * odd, True),
    ):
        south = near_row == 0
        far_row = near_row + jnp.where(south, 1, -1)
        side = jnp.where(south, 1.0, -1.0)

        def piece(ref, number):
            return ref[number * depth : (number + 1) * depth, :]

        wet0 = piece(mine, 6)
        face = piece(ghost, 6) * wet0
        face_next = wet0 * mask[level_rows(far_row, depth), :].astype(jnp.float32)
        inv0 = inv_dy[pl.ds(near_row, 1), :]
        inv1 = inv_dy[pl.ds(far_row, 1), :] * side
        mix0 = spread[pl.ds(near_row, 1), :] * inv0 * inv0
        inv0 = inv0 * side
        flip = minus if turned else 1.0
        speed = face * (piece(ghost, 4) * flip + piece(mine, 4)) * (1.0 / 24.0)
        speed_next = face_next * (piece(mine, 4) + piece(mine, 5)) * (1.0 / 24.0)
        for number in range(3):
            sign = 1.0 if number == 0 else flip
            g0 = piece(ghost, 2 * number) * sign
            g1 = piece(ghost, 2 * number + 1) * sign
            o0 = piece(mine, 2 * number)
            o1 = piece(mine, 2 * number + 1)
            advect = speed * (7.0 * (g0 + o0) - (g1 + o1))
            reach = speed_next * g0
            near = inv0 * (advect + reach) + mix0 * (face * (g0 - o0))
            view = work.at[number]
            view[level_rows(near_row, depth), :] += near
            view[level_rows(far_row, depth), :] -= inv1 * reach

    values = [jnp.zeros((ROWS, LANES), jnp.float32)] * 3
    for level in range(depth):
        here = slice(level * ROWS, (level + 1) * ROWS)
        inverse = solve[0, here, :]
        carry = solve[1, here, :]
        for number in range(3):
            values[number] = inverse * work[number, here, :] + carry * values[number]
            work[number, here, :] = values[number]
    for number in range(3):
        outs[number][(depth - 1) * ROWS : depth * ROWS, :] = values[number]
    for level in range(depth - 2, -1, -1):
        here = slice(level * ROWS, (level + 1) * ROWS)
        gain = solve[2, here, :]
        for number in range(3):
            values[number] = work[number, here, :] + gain * values[number]
            outs[number][here, :] = values[number]


def swaps(pairs):
    return [route for a, b in pairs for route in ((a, b), (b, a))]


def exchange_routes(lats, lons):
    def at(lat, lon):
        return lat * lons + lon % lons

    every = range(lons)
    lon_first = [(at(l, c), at(l, c + 1)) for l in range(lats) for c in range(0, lons, 2)]
    lon_second = [(at(l, c), at(l, c + 1)) for l in range(lats) for c in range(1, lons, 2)]
    lat_first = [(at(l, c), at(l + 1, c)) for l in range(0, lats, 2) for c in every]
    lat_second = [(at(l, c), at(l + 1, c)) for l in range(1, lats - 1, 2) for c in every]
    lat_second += [(at(lats - 1, c), at(lats - 1, lons - 1 - c)) for c in range(lons // 2)]
    return [swaps(pairs) for pairs in (lon_first, lon_second, lat_first, lat_second)]


def per_device(
    temp, uvel, vvel, vert_mixing, inv_dx, inv_dy, horiz_mixing, coriolis, wet_mask, levels
):
    depth, rows, lanes = temp.shape
    assert (rows, lanes) == (ROWS, LANES) and depth == 40
    lats, lons = lax.axis_size("lat"), lax.axis_size("lon")
    assert lats % 2 == 0 and lons % 2 == 0
    flat = depth * rows

    def f32(*shape):
        return jax.ShapeDtypeStruct(shape, jnp.float32)

    temp, uvel, vvel, vert_mixing, wet_mask = (
        x.reshape(flat, lanes) for x in (temp, uvel, vvel, vert_mixing, wet_mask)
    )
    limit = pltpu.CompilerParams(vmem_limit_bytes=16 << 20)
    sent1, sent2, edges = pl.pallas_call(
        pack_kernel,
        name="pack",
        out_shape=(f32(7 * depth, lanes), f32(7 * depth, lanes), f32((TAIL + 1) * rows, lanes)),
        in_specs=[VMEM] * 4,
        out_specs=(VMEM,) * 3,
        compiler_params=limit,
    )(temp, uvel, vvel, wet_mask)
    lon_first, lon_second, lat_first, lat_second = exchange_routes(lats, lons)
    both = ("lat", "lon")
    got2 = lax.ppermute(sent2, both, lat_second)
    east2 = lax.ppermute(edges, both, lon_second)
    got1 = lax.ppermute(sent1, both, lat_first)
    east1 = lax.ppermute(edges, both, lon_first)
    prov, solve = pl.pallas_call(
        interior_kernel,
        name="interior",
        out_shape=(f32(3, flat, lanes), f32(3, flat, lanes)),
        in_specs=[VMEM] * 10,
        out_specs=(VMEM,) * 2,
        compiler_params=limit,
        cost_estimate=pl.CostEstimate(flops=20_000_000, bytes_accessed=6_000_000, transcendentals=0),
    )(temp, uvel, vvel, wet_mask, vert_mixing, inv_dx, inv_dy, horiz_mixing, coriolis, levels)
    outs = pl.pallas_call(
        finish_kernel,
        name="finish",
        out_shape=(f32(flat, lanes),) * 3,
        in_specs=[VMEM] * 13,
        out_specs=(VMEM,) * 3,
        scratch_shapes=[pltpu.VMEM((3, flat, lanes), jnp.float32), pltpu.VMEM((7 * depth, lanes), jnp.float32)],
        compiler_params=limit,
    )(prov, solve, sent1, got1, sent2, got2, edges, east1, east2, wet_mask, inv_dx, inv_dy, horiz_mixing)
    return tuple(x.reshape(depth, rows, lanes) for x in outs)


def solution(mesh):
    field, plane = P(None, "lat", "lon"), P("lat", "lon")
    return jax.shard_map(
        per_device,
        mesh=mesh,
        in_specs=(field,) * 4 + (plane,) * 4 + (field, plane),
        out_specs=(field,) * 3,
        check_vma=False,
    )
```

time: 94.4 us -> 28.1 us (0.30)
  the two profiles are of different devices: /device:TPU:4 before, /device:TPU:3 now
where the time goes in v1:
time: 28.1 us; the launch traced here: 27.8 us
  Pallas kernels  15 us (53%)
  starting transfers between devices  8.16 us (29%)
  local copies, waits for them, and re-layouts  3.91 us (14%)
  between operations  0.76 us (3%)
    pallas_call x1, Pallas kernels, per_device(): pl.pallas_call(interior_kernel, name='interior', out_shape=(f32(3, flat,...  12.4 us
    ppermute x1, starting transfers between devices, per_device(): got2 = lax.ppermute(sent2, both, lat_second)  4.31 us
    unnamed x22, local copies, waits for them, and re-layouts  3.91 us
    ppermute x1, starting transfers between devices, per_device(): east2 = lax.ppermute(edges, both, lon_second)  2.48 us
    pallas_call x1, Pallas kernels, per_device(): pl.pallas_call(finish_kernel, name='finish', out_shape=(f32(flat, lanes),...  2.12 us
    ppermute x1, starting transfers between devices, per_device(): east1 = lax.ppermute(edges, both, lon_first)  1.3 us
  transfers between devices with their start and end apart: 4, of which 0 were waited for; matrix products, arithmetic and copies ran while one was open for 0% of the time, Pallas kernels for 45%

profile of v1, /device:TPU:3, one launch (start us, length us, event | category | flops | bytes accessed | tf_op | source)
XLA Modules:
  0.0 27.8 jit_solution(10864569211546250661)
XLA Ops:
  0.6 0.0 copy-start
  0.6 1.0 %copy-done = s32[40,16,128]{2,1,0:T(8,128)S(1)} copy-done((s32[40,16,128]{2,1,0:T(8,128)S(1)}, s32[40,16,128]{2,1,0:T(8,128)}, u32[]{:S(2)}) %copy-start) | copy-done | bytes 327704
  1.6 0.0 copy-start.2
  1.6 1.0 %copy-done.2 = f32[40,16,128]{2,1,0:T(8,128)S(1)} copy-done((f32[40,16,128]{2,1,0:T(8,128)S(1)}, f32[40,16,128]{2,1,0:T(8,128)}, u32[]{:S(2)}) %copy-start.2) | copy-done | bytes 327704
  2.6 0.0 copy-start.3
  2.6 1.0 %copy-done.3 = f32[40,16,128]{2,1,0:T(8,128)S(1)} copy-done((f32[40,16,128]{2,1,0:T(8,128)S(1)}, f32[40,16,128]{2,1,0:T(8,128)}, u32[]{:S(2)}) %copy-start.3) | copy-done | bytes 327704
  3.6 0.0 copy-start.4
  3.6 1.0 %copy-done.4 = f32[40,16,128]{2,1,0:T(8,128)S(1)} copy-done((f32[40,16,128]{2,1,0:T(8,128)S(1)}, f32[40,16,128]{2,1,0:T(8,128)}, u32[]{:S(2)}) %copy-start.4) | copy-done | bytes 327704
  4.5 0.0 copy-start.5
  4.5 0.0 copy-start.6
  4.5 0.0 copy-start.7
  4.5 0.0 copy-start.8
  4.5 0.0 copy-start.9
  4.5 0.0 copy-start.10
  4.6 0.5 %pack.1 = (f32[280,128]{1,0:T(8,128)S(1)}, f32[280,128]{1,0:T(8,128)S(1)}, f32[80,128]{1,0:T(8,128)S(1)}) custom-call(f32[640,128]{1,0:T(8,128)S(1)} %bitcast.11, f32[640,128]{1,0:T(8,128)S(1)} %bitcast.13, f32[640,128]{1,0:T(8,128)S(1)} %bitcast.15, s32[640,128]{1,0:T(8,128)S(1)} %bitcast.8), custom_call_target="tpu_custom_call" | custom-call | tf_op jit(solution)/shard_map/pack/pallas_call | solution.py:276
  5.1 0.1 collective-permute-start
  5.1 4.3 %collective-permute-start.1 = (f32[280,128]{1,0:T(8,128)S(1)}, f32[280,128]{1,0:T(8,128)S(1)}, u32[]{:S(2)}, u32[]{:S(2)}) collective-permute-start(f32[280,128]{1,0:T(8,128)S(1)} %get-tuple-element.14.sent2), channel_id=1, source_target_pairs={{8,16},{16,8},{9,17},{17,9},{10,18},{18,10},{11,19},{19,11},{12,20... | collective-permute-start | bytes 430088 | tf_op jit(solution)/shard_map/ppermute | solution.py:286
  9.4 2.5 %collective-permute-start.3 = (f32[80,128]{1,0:T(8,128)S(1)}, f32[80,128]{1,0:T(8,128)S(1)}, u32[]{:S(2)}, u32[]{:S(2)}) collective-permute-start(f32[80,128]{1,0:T(8,128)S(1)} %get-tuple-element.15.edges), channel_id=1, source_target_pairs={{1,2},{2,1},{3,4},{4,3},{5,6},{6,5},{7,0},{0,7},{9,10},{10,9},{11,... | collective-permute-start | bytes 122888 | tf_op jit(solution)/shard_map/ppermute | solution.py:287
  11.9 1.3 %collective-permute-start.2 = (f32[80,128]{1,0:T(8,128)S(1)}, f32[80,128]{1,0:T(8,128)S(1)}, u32[]{:S(2)}, u32[]{:S(2)}) collective-permute-start(f32[80,128]{1,0:T(8,128)S(1)} %get-tuple-element.15.edges), channel_id=1, source_target_pairs={{0,1},{1,0},{2,3},{3,2},{4,5},{5,4},{6,7},{7,6},{8,9},{9,8},{10,11... | collective-permute-start | bytes 122888 | tf_op jit(solution)/shard_map/ppermute | solution.py:289
  13.2 0.0 copy-done.5
  13.2 0.0 copy-done.6
  13.2 0.0 copy-done.7
  13.2 0.0 copy-done.8
  13.2 0.0 copy-done.9
  13.2 0.0 copy-done.10
  13.3 0.0 copy-start.1
  13.3 12.4 %interior.1 = (f32[3,640,128]{2,1,0:T(8,128)S(1)}, f32[3,640,128]{2,1,0:T(8,128)S(1)}) custom-call(f32[640,128]{1,0:T(8,128)S(1)} %bitcast.12, f32[640,128]{1,0:T(8,128)S(1)} %bitcast.14, f32[640,128]{1,0:T(8,128)S(1)} %bitcast.16, s32[640,128]{1,0:T(8,128)S(1)} %bitcast.9, f32[640,128]{1,0:T(8,128)S(1)} %bitcast.17, f32[16,128]{1,0:T(8,128)S(1)} %copy-done.6, ...), custom_call_target="tpu_custom_call" | custom-call | flops 20000000 | bytes 6000000 | tf_op jit(solution)/shard_map/interior/pallas_call | solution.py:290
  25.7 0.0 collective-permute-done.3.east2
  25.7 0.0 collective-permute-done.2.east1
  25.7 0.0 collective-permute-done.got1
  25.7 0.0 collective-permute-done.1.got2
  25.7 0.0 copy-done.1
  25.7 2.1 %finish.1 = (f32[640,128]{1,0:T(8,128)}, f32[640,128]{1,0:T(8,128)}, f32[640,128]{1,0:T(8,128)}) custom-call(f32[3,640,128]{2,1,0:T(8,128)S(1)} %get-tuple-element.11.prov, f32[3,640,128]{2,1,0:T(8,128)S(1)} %get-tuple-element.12.solve, f32[280,128]{1,0:T(8,128)S(1)} %get-tuple-element.13.sent1, f32[280,128]{1,0:T(8,128)S(1)} %collective-permute-done.got1, ...), custom_call_target="tpu_custom_call" | custom-call | tf_op jit(solution)/shard_map/finish/pallas_call | solution.py:299
Async XLA Ops:
  0.6 1.0 %copy-start = (s32[40,16,128]{2,1,0:T(8,128)S(1)}, s32[40,16,128]{2,1,0:T(8,128)}, u32[]{:S(2)}) copy-start(s32[40,16,128]{2,1,0:T(8,128)} %param.18) | copy-start | bytes 983044
  1.6 1.0 %copy-start.2 = (f32[40,16,128]{2,1,0:T(8,128)S(1)}, f32[40,16,128]{2,1,0:T(8,128)}, u32[]{:S(2)}) copy-start(f32[40,16,128]{2,1,0:T(8,128)} %param.10) | copy-start | bytes 983044
  2.6 1.0 %copy-start.3 = (f32[40,16,128]{2,1,0:T(8,128)S(1)}, f32[40,16,128]{2,1,0:T(8,128)}, u32[]{:S(2)}) copy-start(f32[40,16,128]{2,1,0:T(8,128)} %param.11) | copy-start | bytes 983044
  3.6 1.0 %copy-start.4 = (f32[40,16,128]{2,1,0:T(8,128)S(1)}, f32[40,16,128]{2,1,0:T(8,128)}, u32[]{:S(2)}) copy-start(f32[40,16,128]{2,1,0:T(8,128)} %param.12) | copy-start | bytes 983044
  4.5 8.7 %copy-start.5 = (f32[40,16,128]{2,1,0:T(8,128)S(1)}, f32[40,16,128]{2,1,0:T(8,128)}, u32[]{:S(2)}) copy-start(f32[40,16,128]{2,1,0:T(8,128)} %param.13) | copy-start | bytes 983044
  4.5 8.7 %copy-start.6 = (f32[16,128]{1,0:T(8,128)S(1)}, f32[16,128]{1,0:T(8,128)}, u32[]{:S(2)}) copy-start(f32[16,128]{1,0:T(8,128)} %inv_dx.3) | copy-start | bytes 24580
  4.5 8.7 %copy-start.7 = (f32[16,128]{1,0:T(8,128)S(1)}, f32[16,128]{1,0:T(8,128)}, u32[]{:S(2)}) copy-start(f32[16,128]{1,0:T(8,128)} %inv_dy.3) | copy-start | bytes 24580
  4.5 8.7 %copy-start.8 = (f32[16,128]{1,0:T(8,128)S(1)}, f32[16,128]{1,0:T(8,128)}, u32[]{:S(2)}) copy-start(f32[16,128]{1,0:T(8,128)} %spread.3) | copy-start | bytes 24580
  4.5 8.7 %copy-start.9 = (f32[16,128]{1,0:T(8,128)S(1)}, f32[16,128]{1,0:T(8,128)}, u32[]{:S(2)}) copy-start(f32[16,128]{1,0:T(8,128)} %coriolis.1) | copy-start | bytes 24580
  4.5 8.7 %copy-start.10 = (s32[16,128]{1,0:T(8,128)S(1)}, s32[16,128]{1,0:T(8,128)}, u32[]{:S(2)}) copy-start(s32[16,128]{1,0:T(8,128)} %levels.1) | copy-start | bytes 24580
  5.1 20.6 %collective-permute-start = (f32[280,128]{1,0:T(8,128)S(1)}, f32[280,128]{1,0:T(8,128)S(1)}, u32[]{:S(2)}, u32[]{:S(2)}) collective-permute-start(f32[280,128]{1,0:T(8,128)S(1)} %get-tuple-element.13.sent1), channel_id=1, source_target_pairs={{0,8},{8,0},{1,9},{9,1},{2,10},{10,2},{3,11},{11,3},{4,12},{12,4},... | collective-permute-start | bytes 430088 | tf_op jit(solution)/shard_map/ppermute | solution.py:288
  5.1 20.6 %collective-permute-start.1 = (f32[280,128]{1,0:T(8,128)S(1)}, f32[280,128]{1,0:T(8,128)S(1)}, u32[]{:S(2)}, u32[]{:S(2)}) collective-permute-start(f32[280,128]{1,0:T(8,128)S(1)} %get-tuple-element.14.sent2), channel_id=1, source_target_pairs={{8,16},{16,8},{9,17},{17,9},{10,18},{18,10},{11,19},{19,11},{12,20... | collective-permute-start | bytes 430088 | tf_op jit(solution)/shard_map/ppermute | solution.py:286
  9.4 16.2 %collective-permute-start.3 = (f32[80,128]{1,0:T(8,128)S(1)}, f32[80,128]{1,0:T(8,128)S(1)}, u32[]{:S(2)}, u32[]{:S(2)}) collective-permute-start(f32[80,128]{1,0:T(8,128)S(1)} %get-tuple-element.15.edges), channel_id=1, source_target_pairs={{1,2},{2,1},{3,4},{4,3},{5,6},{6,5},{7,0},{0,7},{9,10},{10,9},{11,... | collective-permute-start | bytes 122888 | tf_op jit(solution)/shard_map/ppermute | solution.py:287
  11.9 13.7 %collective-permute-start.2 = (f32[80,128]{1,0:T(8,128)S(1)}, f32[80,128]{1,0:T(8,128)S(1)}, u32[]{:S(2)}, u32[]{:S(2)}) collective-permute-start(f32[80,128]{1,0:T(8,128)S(1)} %get-tuple-element.15.edges), channel_id=1, source_target_pairs={{0,1},{1,0},{2,3},{3,2},{4,5},{5,4},{6,7},{7,6},{8,9},{9,8},{10,11... | collective-permute-start | bytes 122888 | tf_op jit(solution)/shard_map/ppermute | solution.py:289
  13.3 12.4 %copy-start.1 = (s32[40,16,128]{2,1,0:T(8,128)S(1)}, s32[40,16,128]{2,1,0:T(8,128)}, u32[]{:S(2)}) copy-start(s32[40,16,128]{2,1,0:T(8,128)} %param.18) | copy-start | bytes 983044

commit v2 on v1

v2 whole, which is shorter than its diff:
```python
import jax
import jax.numpy as jnp
from jax import lax
from jax.experimental import pallas as pl
from jax.experimental.pallas import tpu as pltpu
from jax.sharding import PartitionSpec as P

ROWS = 16
LANES = 128
TILE = 8
TAIL = 4
VMEM = pl.BlockSpec(memory_space=pltpu.VMEM)
HBM = pl.BlockSpec(memory_space=pltpu.HBM)


def lane_index(rows):
    return lax.broadcasted_iota(jnp.int32, (rows, LANES), 1)


def turn_lanes(x, shift):
    return pltpu.roll(x, shift % LANES, 1)


def level_rows(row, depth):
    return pl.ds(row, depth, stride=ROWS)


def piece(ref, number, depth):
    return ref[number * depth : (number + 1) * depth, :]


def level(ref, number):
    return ref[number * ROWS : (number + 1) * ROWS, :]


def slab_place(number, field):
    if number < 32:
        return field, 4 * number
    return TAIL, 32 * field + 4 * (number - 32)


def fold_pack_kernel(temp, uvel, vvel, mask, out, half0, half1, half2, halfm, sems):
    depth = temp.shape[0]
    odd = lax.rem(lax.axis_index("lat"), 2)
    copies = []
    for number, (field, half) in enumerate(
        zip((temp, uvel, vvel, mask), (half0, half1, half2, halfm))
    ):
        copies.append(
            pltpu.make_async_copy(
                field.at[:, pl.ds(pl.multiple_of(odd * TILE, TILE), TILE), :],
                half.reshape(depth, TILE, LANES),
                sems.at[number],
            )
        )
    for copy in copies:
        copy.start()
    near = (TILE - 1) * odd
    far = near + 1 - 2 * odd
    keep = jnp.where(lax.axis_index("lat") == 0, 0.0, 1.0)
    for number, half in enumerate((half0, half1, half2)):
        copies[number].wait()
        base = 2 * depth * number
        out[base : base + depth, :] = half[pl.ds(near, depth, stride=TILE), :] * keep
        out[base + depth : base + 2 * depth, :] = half[pl.ds(far, depth, stride=TILE), :] * keep
    copies[3].wait()
    out[6 * depth : 7 * depth, :] = halfm[pl.ds(near, depth, stride=TILE), :].astype(jnp.float32) * keep


def pack_kernel(temp, uvel, vvel, mask, first, edges):
    depth = temp.shape[0] // ROWS
    odd = lax.rem(lax.axis_index("lat"), 2)
    near = (ROWS - 1) * (1 - odd)
    far = near + 2 * odd - 1
    for number, field in enumerate((temp, uvel, vvel)):
        base = 2 * depth * number
        first[base : base + depth, :] = field[level_rows(near, depth), :]
        first[base + depth : base + 2 * depth, :] = field[level_rows(far, depth), :]
    first[6 * depth : 7 * depth, :] = mask[level_rows(near, depth), :].astype(jnp.float32)
    group = lane_index(ROWS) // 4
    slabs = [jnp.zeros((ROWS, LANES), jnp.float32) for _ in range(TAIL + 1)]
    for number in range(depth):
        for index, field in enumerate((temp, uvel, vvel, mask)):
            block = level(field, number).astype(jnp.float32)
            slab, start = slab_place(number, index)
            slabs[slab] = jnp.where(group == start // 4, turn_lanes(block, start + 2), slabs[slab])
    for number, slab in enumerate(slabs):
        edges[number * ROWS : (number + 1) * ROWS, :] = slab


def interior_kernel(
    temp, uvel, vvel, mask, mixing, inv_dx, inv_dy, spread, coriolis, levels, prov, solve, middle
):
    depth = temp.shape[0] // ROWS
    half = depth // 2
    lane = lane_index(depth)
    active = levels[...]
    zero = jnp.zeros((ROWS, LANES), jnp.float32)

    def coupling(number):
        if 0 <= number < depth - 1:
            return jnp.where(number + 1 < active, level(mixing, number + 1), 0.0)
        return zero

    chains = [zero, zero]

    def factor(step):
        for side, number in enumerate((step, depth - 1 - step)):
            above, below = coupling(number - 1), coupling(number)
            done, left = (above, below) if side == 0 else (below, above)
            inverse = 1.0 / (1.0 + left + done * (1.0 - chains[side]))
            chains[side] = left * inverse
            here = slice(number * ROWS, (number + 1) * ROWS)
            solve[0, here, :] = inverse
            solve[1, here, :] = done * inverse
            solve[2, here, :] = chains[side]

    def rows_of(ref, row):
        return ref[level_rows(row, depth), :]

    def wet_of(row):
        return rows_of(mask, row).astype(jnp.float32)

    fields = (temp, uvel, vvel)
    steps = 0
    advect_south = [0.0] * 3
    spread_south = [0.0] * 3
    for row in range(ROWS):
        while steps < half and steps * ROWS <= row * half + half - 1:
            factor(steps)
            steps += 1
        one = slice(row, row + 1)
        scale = inv_dx[one, :]
        spread_x = spread[one, :] * scale * scale
        scale = scale * (-1.0 / 24.0)
        wet = wet_of(row)
        face_w = wet * jnp.where(lane >= 1, turn_lanes(wet, 1), 0.0)
        face_e = wet * jnp.where(lane < LANES - 1, turn_lanes(wet, -1), 0.0)
        u = rows_of(uvel, row)
        speed_w = scale * face_w * (turn_lanes(u, 1) + u)
        speed_e = scale * face_e * (turn_lanes(u, -1) + u)
        face_w = spread_x * face_w
        face_e = spread_x * face_e
        scale_y = inv_dy[one, :]
        spread_y = spread[one, :] * scale_y * scale_y
        scale_y = scale_y * (-1.0 / 24.0)
        if row + 1 < ROWS:
            face_n = wet * wet_of(row + 1)
            speed_n = face_n * (rows_of(vvel, row) + rows_of(vvel, row + 1))
        turn = wet * coriolis[one, :]
        for number, field in enumerate(fields):
            q = rows_of(field, row)
            west, east = turn_lanes(q, 1), turn_lanes(q, -1)
            value_w = 7.0 * (west + q) - (turn_lanes(q, 2) + east)
            value_e = 7.0 * (east + q) - (west + turn_lanes(q, -2))
            total = speed_e * value_e - speed_w * value_w + face_e * (east - q) - face_w * (q - west)
            if row + 1 < ROWS:
                north = rows_of(field, row + 1)
                outer = None
                if row >= 1:
                    outer = rows_of(field, row - 1)
                if row + 2 < ROWS:
                    beyond = rows_of(field, row + 2)
                    outer = beyond if outer is None else outer + beyond
                advect_north = speed_n * (7.0 * (q + north) - outer)
                spread_north = face_n * (north - q)
            else:
                advect_north, spread_north = 0.0, 0.0
            total = total + scale_y * (advect_north - advect_south[number])
            total = total + spread_y * (spread_north - spread_south[number])
            advect_south[number], spread_south[number] = advect_north, spread_north
            if number == 1:
                total = total + turn * rows_of(vvel, row)
            if number == 2:
                total = total - turn * u
            target = prov.at[number]
            target[level_rows(row, depth), :] = q + total
    while steps < half:
        factor(steps)
        steps += 1
    middle[...] = 1.0 / (1.0 - chains[0] * chains[1])


def add_row_ghosts(prov, mine, ghost, near, odd_sign, mask, inv_dy, spread, flip):
    depth = prov.shape[1] // ROWS
    far = near + odd_sign
    side = odd_sign.astype(jnp.float32)
    wet = piece(mine, 6, depth)
    face = piece(ghost, 6, depth) * wet
    face_next = wet * mask[level_rows(far, depth), :].astype(jnp.float32)
    inv0 = inv_dy[pl.ds(near, 1), :]
    inv1 = inv_dy[pl.ds(far, 1), :] * side
    mix0 = spread[pl.ds(near, 1), :] * inv0 * inv0
    inv0 = inv0 * side
    speed = face * (piece(ghost, 4, depth) * flip + piece(mine, 4, depth)) * (1.0 / 24.0)
    speed_next = face_next * (piece(mine, 4, depth) + piece(mine, 5, depth)) * (1.0 / 24.0)
    for number in range(3):
        sign = 1.0 if number == 0 else flip
        g0 = piece(ghost, 2 * number, depth) * sign
        g1 = piece(ghost, 2 * number + 1, depth) * sign
        o0 = piece(mine, 2 * number, depth)
        o1 = piece(mine, 2 * number + 1, depth)
        advect = speed * (7.0 * (g0 + o0) - (g1 + o1))
        reach = speed_next * g0
        view = prov.at[number]
        view[level_rows(near, depth), :] += inv0 * (advect + reach) + mix0 * (face * (g0 - o0))
        view[level_rows(far, depth), :] -= inv1 * reach


def ghosts_kernel(
    prov_in, sent1, got1, edges, east1, east2, mask, inv_dx, inv_dy, spread, prov
):
    depth = prov.shape[1] // ROWS
    odd = lax.rem(lax.axis_index("lat"), 2)
    lon_odd = lax.rem(lax.axis_index("lon"), 2) == 1
    lane = lane_index(ROWS)
    quad = lane % 4
    four = jnp.where(quad < 2, LANES - 2 + quad, quad - 2)

    def replicate(x):
        return jnp.take_along_axis(x, four, axis=1, mode="promise_in_bounds")

    wide = replicate(inv_dx[...])
    wide2 = replicate(spread[...]) * wide * wide
    own = [level(edges, s) for s in range(TAIL + 1)]
    first = [level(east1, s) for s in range(TAIL + 1)]
    second = [level(east2, s) for s in range(TAIL + 1)]
    west = [jnp.where(quad < 2, jnp.where(lon_odd, a, b), o) for a, b, o in zip(first, second, own)]
    east = [jnp.where(quad < 2, o, jnp.where(lon_odd, b, a)) for a, b, o in zip(first, second, own)]

    def split(slabs):
        tail = [slabs[TAIL] if f == 0 else turn_lanes(slabs[TAIL], -32 * f) for f in range(4)]
        return [slabs[:TAIL], tail]

    corrections = []
    for west_part, east_part, own_part in zip(split(west), split(east), split(own)):
        wet = west_part[3]
        face = turn_lanes(wet, 1) * wet
        speed = face * (turn_lanes(west_part[1], 1) + west_part[1]) * (1.0 / 24.0)
        speed_next = turn_lanes(speed, -1)
        wet_e = east_part[3]
        face_e = turn_lanes(wet_e, -1) * wet_e
        speed_e = face_e * (turn_lanes(east_part[1], -1) + east_part[1]) * (1.0 / 24.0)
        speed_e_before = turn_lanes(speed_e, 1)
        part = []
        for number in range(3):
            mine = own_part[number]
            q = west_part[number]
            back = turn_lanes(q, 1)
            advect = speed * (7.0 * (back + q) - (turn_lanes(q, 2) + turn_lanes(q, -1)))
            reach = speed_next * turn_lanes(q - mine, 1)
            near = wide * (advect + reach) - wide2 * (face * (q - back))
            distant = turn_lanes(reach, 1) * wide
            q = east_part[number]
            ahead = turn_lanes(q, -1)
            advect = speed_e * (7.0 * (ahead + q) - (turn_lanes(q, -2) + turn_lanes(q, 1)))
            reach = speed_e_before * turn_lanes(q - mine, -1)
            near_e = wide2 * (face_e * (ahead - q)) - wide * (advect + reach)
            distant_e = turn_lanes(reach, -1) * wide
            part.append(
                jnp.where(
                    quad < 2,
                    jnp.where(quad == 0, distant_e, near_e),
                    jnp.where(quad == 2, near, -distant),
                )
            )
        corrections.append(part)

    border = (lane < 2) | (lane >= LANES - 2)
    for number in range(depth):
        here = slice(number * ROWS, (number + 1) * ROWS)
        for field in range(3):
            if number < 32:
                source, start = corrections[0][field], 4 * number
            else:
                source, start = corrections[1][field], 4 * (number - 32)
            moved = jnp.where(border, turn_lanes(source, -(start + 2)), 0.0)
            prov[field, here, :] = prov_in[field, here, :] + moved
    add_row_ghosts(prov, sent1, got1, (ROWS - 1) * (1 - odd), 2 * odd - 1, mask, inv_dy, spread, 1.0)


def finish_kernel(
    prov_in, solve, middle, mine, ghost, mask, inv_dy, spread,
    temp_new, uvel_new, vvel_new, prov, work, turned, sems
):
    depth = prov.shape[1] // ROWS
    half = depth // 2
    odd = lax.rem(lax.axis_index("lat"), 2)
    fold = lax.axis_index("lat") == lax.axis_size("lat") - 1
    lane = lane_index(7 * depth)
    lane = jnp.where(fold, LANES - 1 - lane, lane)
    turned[...] = jnp.take_along_axis(ghost[...], lane, axis=1, mode="promise_in_bounds")
    flip = jnp.where(fold, -1.0, 1.0)
    add_row_ghosts(prov, mine, turned, (ROWS - 1) * odd, 1 - 2 * odd, mask, inv_dy, spread, flip)

    outs = (temp_new, uvel_new, vvel_new)
    zero = jnp.zeros((ROWS, LANES), jnp.float32)
    values = [[zero] * 3, [zero] * 3]
    for step in range(half):
        for side, number in enumerate((step, depth - 1 - step)):
            here = slice(number * ROWS, (number + 1) * ROWS)
            inverse, carry = solve[0, here, :], solve[1, here, :]
            for field in range(3):
                value = inverse * prov[field, here, :] + carry * values[side][field]
                values[side][field] = value
                work[field, here, :] = value
    above, below = half - 1, half
    gain = solve[2, above * ROWS : (above + 1) * ROWS, :]
    scale = middle[...]
    for field in range(3):
        top = scale * (values[0][field] + gain * values[1][field])
        values[1][field] = top
        values[0][field] = None
    tops = values[1]
    for field in range(3):
        work[field, above * ROWS : (above + 1) * ROWS, :] = tops[field]
    chains = [list(tops), list(tops)]
    copies = []
    for step in range(half):
        for side, number in enumerate((above - 1 - step, below + step)):
            if number < 0:
                continue
            here = slice(number * ROWS, (number + 1) * ROWS)
            gain = solve[2, here, :]
            for field in range(3):
                value = work[field, here, :] + gain * chains[side][field]
                chains[side][field] = value
                work[field, here, :] = value
        if step == half // 2 - 1:
            low, high = above - 1 - step, below + step + 1
            for field in range(3):
                rows = pl.ds(low * ROWS, (high - low) * ROWS)
                copies.append(
                    pltpu.make_async_copy(
                        work.at[field, rows, :], outs[field].at[rows, :], sems.at[field]
                    )
                )
                copies[-1].start()
    for field in range(3):
        for part, (start, stop) in enumerate(((0, low), (high, depth))):
            rows = pl.ds(start * ROWS, (stop - start) * ROWS)
            copies.append(
                pltpu.make_async_copy(
                    work.at[field, rows, :], outs[field].at[rows, :], sems.at[3 + 2 * field + part]
                )
            )
            copies[-1].start()
    for copy in copies:
        copy.wait()


def swaps(pairs):
    return [route for a, b in pairs for route in ((a, b), (b, a))]


def exchange_routes(lats, lons):
    def at(lat, lon):
        return lat * lons + lon % lons

    every = range(lons)
    lon_first = [(at(l, c), at(l, c + 1)) for l in range(lats) for c in range(0, lons, 2)]
    lon_second = [(at(l, c), at(l, c + 1)) for l in range(lats) for c in range(1, lons, 2)]
    lat_first = [(at(l, c), at(l + 1, c)) for l in range(0, lats, 2) for c in every]
    lat_second = [(at(l, c), at(l + 1, c)) for l in range(1, lats - 1, 2) for c in every]
    lat_second += [(at(lats - 1, c), at(lats - 1, lons - 1 - c)) for c in range(lons // 2)]
    lat_second += [(at(0, c), at(0, c + 1)) for c in range(0, lons, 2)]
    return [swaps(pairs) for pairs in (lon_first, lon_second, lat_first, lat_second)]


def per_device(
    temp, uvel, vvel, vert_mixing, inv_dx, inv_dy, horiz_mixing, coriolis, wet_mask, levels
):
    depth, rows, lanes = temp.shape
    assert (rows, lanes) == (ROWS, LANES) and depth == 40
    lats, lons = lax.axis_size("lat"), lax.axis_size("lon")
    assert lats % 2 == 0 and lons % 2 == 0
    flat = depth * rows

    def f32(*shape):
        return jax.ShapeDtypeStruct(shape, jnp.float32)

    def vmem(*shape, dtype=jnp.float32):
        return pltpu.VMEM(shape, dtype)

    limit = pltpu.CompilerParams(vmem_limit_bytes=16 << 20)
    both = ("lat", "lon")
    lon_first, lon_second, lat_first, lat_second = exchange_routes(lats, lons)
    sent2 = pl.pallas_call(
        fold_pack_kernel,
        name="fold_pack",
        out_shape=f32(7 * depth, lanes),
        in_specs=[HBM] * 4,
        out_specs=VMEM,
        scratch_shapes=[vmem(depth * TILE, lanes)] * 3
        + [vmem(depth * TILE, lanes, dtype=jnp.int32), pltpu.SemaphoreType.DMA((4,))],
        compiler_params=limit,
    )(temp, uvel, vvel, wet_mask)
    got2 = lax.ppermute(sent2, both, lat_second)
    temp, uvel, vvel, vert_mixing, wet_mask = (
        x.reshape(flat, lanes) for x in (temp, uvel, vvel, vert_mixing, wet_mask)
    )
    sent1, edges = pl.pallas_call(
        pack_kernel,
        name="pack",
        out_shape=(f32(7 * depth, lanes), f32((TAIL + 1) * rows, lanes)),
        in_specs=[VMEM] * 4,
        out_specs=(VMEM,) * 2,
        compiler_params=limit,
    )(temp, uvel, vvel, wet_mask)
    got1 = lax.ppermute(sent1, both, lat_first)
    east2 = lax.ppermute(edges, both, lon_second)
    east1 = lax.ppermute(edges, both, lon_first)
    prov, solve, middle = pl.pallas_call(
        interior_kernel,
        name="interior",
        out_shape=(f32(3, flat, lanes), f32(3, flat, lanes), f32(rows, lanes)),
        in_specs=[VMEM] * 10,
        out_specs=(VMEM,) * 3,
        compiler_params=limit,
        cost_estimate=pl.CostEstimate(flops=20_000_000, bytes_accessed=6_000_000, transcendentals=0),
    )(temp, uvel, vvel, wet_mask, vert_mixing, inv_dx, inv_dy, horiz_mixing, coriolis, levels)
    prov = pl.pallas_call(
        ghosts_kernel,
        name="ghosts",
        out_shape=f32(3, flat, lanes),
        in_specs=[VMEM] * 10,
        out_specs=VMEM,
        input_output_aliases={0: 0},
        compiler_params=limit,
    )(prov, sent1, got1, edges, east1, east2, wet_mask, inv_dx, inv_dy, horiz_mixing)
    outs = pl.pallas_call(
        finish_kernel,
        name="finish",
        out_shape=(f32(flat, lanes),) * 3 + (f32(3, flat, lanes),),
        in_specs=[VMEM] * 8,
        out_specs=(HBM,) * 3 + (VMEM,),
        input_output_aliases={0: 3},
        scratch_shapes=[
            vmem(3, flat, lanes),
            vmem(7 * depth, lanes),
            pltpu.SemaphoreType.DMA((9,)),
        ],
        compiler_params=limit,
    )(prov, solve, middle, sent2, got2, wet_mask, inv_dy, horiz_mixing)
    return tuple(x.reshape(depth, rows, lanes) for x in outs[:3])


def solution(mesh):
    field, plane = P(None, "lat", "lon"), P("lat", "lon")
    return jax.shard_map(
        per_device,
        mesh=mesh,
        in_specs=(field,) * 4 + (plane,) * 4 + (field, plane),
        out_specs=(field,) * 3,
        check_vma=False,
    )
```

time: 28.1 us -> 18.4 us (0.65)
  the two profiles are of different devices: /device:TPU:3 before, /device:TPU:15 now
where the time goes in v2:
time: 18.4 us; the launch traced here: 18.1 us
  Pallas kernels  5.23 us (28%)
  starting transfers between devices  5.11 us (28%)
  local copies, waits for them, and re-layouts  3.92 us (21%)
  waiting for transfers between devices  3.12 us (17%)
  between operations  0.73 us (4%)
    unnamed x22, local copies, waits for them, and re-layouts  3.92 us
    ppermute x1, waiting for transfers between devices, per_device(): east2 = lax.ppermute(edges, both, lon_second)  3.11 us
    ppermute x1, starting transfers between devices, per_device(): east1 = lax.ppermute(edges, both, lon_first)  2.51 us
    pallas_call x1, Pallas kernels, per_device(): pl.pallas_call(interior_kernel, name='interior', out_shape=(f32(3, flat,...  2.38 us
    ppermute x1, starting transfers between devices, per_device(): got2 = lax.ppermute(sent2, both, lat_second)  2.2 us
    pallas_call x1, Pallas kernels, per_device(): pl.pallas_call(finish_kernel, name='finish', out_shape=(f32(flat, lanes),...  1.37 us
    pallas_call x1, Pallas kernels, per_device(): pl.pallas_call(ghosts_kernel, name='ghosts', out_shape=f32(3, flat, lanes...  0.89 us
    pallas_call x1, Pallas kernels, per_device(): pl.pallas_call(pack_kernel, name='pack', out_shape=(f32(7 * depth, lanes)...  0.43 us
  transfers between devices with their start and end apart: 4, of which 1 were waited for; matrix products, arithmetic and copies ran while one was open for 0% of the time, Pallas kernels for 19%

profile of v2, /device:TPU:15, one launch (start us, length us, event | category | flops | bytes accessed | tf_op | source)
XLA Modules:
  0.0 18.1 jit_solution(12391572837448378474)
XLA Ops:
  0.6 0.0 copy-start
  0.6 1.0 %copy-done = s32[40,16,128]{2,1,0:T(8,128)S(1)} copy-done((s32[40,16,128]{2,1,0:T(8,128)S(1)}, s32[40,16,128]{2,1,0:T(8,128)}, u32[]{:S(2)}) %copy-start) | copy-done | bytes 327704
  1.6 0.0 copy-start.2
  1.6 1.0 %copy-done.2 = f32[40,16,128]{2,1,0:T(8,128)S(1)} copy-done((f32[40,16,128]{2,1,0:T(8,128)S(1)}, f32[40,16,128]{2,1,0:T(8,128)}, u32[]{:S(2)}) %copy-start.2) | copy-done | bytes 327704
  2.6 0.0 copy-start.3
  2.6 1.0 %copy-done.3 = f32[40,16,128]{2,1,0:T(8,128)S(1)} copy-done((f32[40,16,128]{2,1,0:T(8,128)S(1)}, f32[40,16,128]{2,1,0:T(8,128)}, u32[]{:S(2)}) %copy-start.3) | copy-done | bytes 327704
  3.6 0.0 copy-start.4
  3.6 1.0 %copy-done.4 = f32[40,16,128]{2,1,0:T(8,128)S(1)} copy-done((f32[40,16,128]{2,1,0:T(8,128)S(1)}, f32[40,16,128]{2,1,0:T(8,128)}, u32[]{:S(2)}) %copy-start.4) | copy-done | bytes 327704
  4.5 0.4 %pack.1 = (f32[280,128]{1,0:T(8,128)S(1)}, f32[80,128]{1,0:T(8,128)S(1)}) custom-call(f32[640,128]{1,0:T(8,128)S(1)} %bitcast.12, f32[640,128]{1,0:T(8,128)S(1)} %bitcast.14, f32[640,128]{1,0:T(8,128)S(1)} %bitcast.16, s32[640,128]{1,0:T(8,128)S(1)} %bitcast.8), custom_call_target="tpu_custom_call" | custom-call | tf_op jit(solution)/shard_map/pack/pallas_call | solution.py:402
  5.0 0.0 copy-start.5
  5.0 0.3 %collective-permute-start = (f32[280,128]{1,0:T(8,128)S(1)}, f32[280,128]{1,0:T(8,128)S(1)}, u32[]{:S(2)}, u32[]{:S(2)}) collective-permute-start(f32[280,128]{1,0:T(8,128)S(1)} %get-tuple-element.12.sent1), channel_id=1, source_target_pairs={{0,8},{8,0},{1,9},{9,1},{2,10},{10,2},{3,11},{11,3},{4,12},{12,4},... | collective-permute-start | bytes 430088 | tf_op jit(solution)/shard_map/ppermute | solution.py:410
  5.3 0.0 copy-start.6
  5.3 0.0 copy-start.7
  5.3 0.0 copy-start.8
  5.3 0.0 copy-start.9
  5.3 0.0 copy-start.10
  5.3 0.2 fold_pack.1.mine
  5.5 2.2 %collective-permute-start.3 = (f32[280,128]{1,0:T(8,128)S(1)}, f32[280,128]{1,0:T(8,128)S(1)}, u32[]{:S(2)}, u32[]{:S(2)}) collective-permute-start(f32[280,128]{1,0:T(8,128)S(1)} %fold_pack.1.mine), channel_id=1, source_target_pairs={{8,16},{16,8},{9,17},{17,9},{10,18},{18,10},{11,19},{19,11},{12,20... | collective-permute-start | bytes 430088 | tf_op jit(solution)/shard_map/ppermute | solution.py:398
  7.7 0.1 collective-permute-start.2
  7.8 2.5 %collective-permute-start.1 = (f32[80,128]{1,0:T(8,128)S(1)}, f32[80,128]{1,0:T(8,128)S(1)}, u32[]{:S(2)}, u32[]{:S(2)}) collective-permute-start(f32[80,128]{1,0:T(8,128)S(1)} %get-tuple-element.13.edges), channel_id=1, source_target_pairs={{0,1},{1,0},{2,3},{3,2},{4,5},{5,4},{6,7},{7,6},{8,9},{9,8},{10,11... | collective-permute-start | bytes 122888 | tf_op jit(solution)/shard_map/ppermute | solution.py:412
  10.3 0.0 copy-done.5
  10.3 0.0 copy-done.6
  10.3 0.0 copy-done.7
  10.3 0.0 copy-done.8
  10.3 0.0 copy-done.9
  10.3 0.0 copy-done.10
  10.3 0.0 copy-start.1
  10.3 2.4 %interior.1 = (f32[3,640,128]{2,1,0:T(8,128)S(1)}, f32[3,640,128]{2,1,0:T(8,128)S(1)}, f32[16,128]{1,0:T(8,128)S(1)}) custom-call(f32[640,128]{1,0:T(8,128)S(1)} %bitcast.13, f32[640,128]{1,0:T(8,128)S(1)} %bitcast.15, f32[640,128]{1,0:T(8,128)S(1)} %bitcast.17, s32[640,128]{1,0:T(8,128)S(1)} %bitcast.9, f32[640,128]{1,0:T(8,128)S(1)} %bitcast.18, ...), custom_call_target="tpu_custom_call" | custom-call | flops 20000000 | bytes 6000000 | tf_op jit(solution)/shard_map/interior/pallas_call | solution.py:413
  12.7 3.1 %collective-permute-done.2.east2 = f32[80,128]{1,0:T(8,128)S(1)} collective-permute-done((f32[80,128]{1,0:T(8,128)S(1)}, f32[80,128]{1,0:T(8,128)S(1)}, u32[]{:S(2)}, u32[]{:S(2)}) %collective-permute-start.2) | collective-permute-done | bytes 40992 | tf_op jit(solution)/shard_map/ppermute | solution.py:411
  15.8 0.0 collective-permute-done.1.east1
  15.8 0.0 collective-permute-done.got1
  15.8 0.0 copy-done.1
  15.8 0.9 %ghosts.1.prov_in = f32[3,640,128]{2,1,0:T(8,128)S(1)} custom-call(f32[3,640,128]{2,1,0:T(8,128)S(1)} %get-tuple-element.11.prov_in, f32[280,128]{1,0:T(8,128)S(1)} %get-tuple-element.12.sent1, f32[280,128]{1,0:T(8,128)S(1)} %collective-permute-done.got1, f32[80,128]{1,0:T(8,128)S(1)} %get-tuple-element.13.edges, ...), custom_call_target="tpu_custom_call", output_to_operand_aliasing={{}: (0, {})} | custom-call | tf_op jit(solution)/shard_map/ghosts/pallas_call | solution.py:422
  16.7 0.0 collective-permute-done.3.ghost
  16.7 1.4 %finish.1 = (f32[640,128]{1,0:T(8,128)}, f32[640,128]{1,0:T(8,128)}, f32[640,128]{1,0:T(8,128)}, f32[3,640,128]{2,1,0:T(8,128)S(1)}) custom-call(f32[3,640,128]{2,1,0:T(8,128)S(1)} %ghosts.1.prov_in, f32[3,640,128]{2,1,0:T(8,128)S(1)} %get-tuple-element.14.solve, f32[16,128]{1,0:T(8,128)S(1)} %get-tuple-element.15.middle, ...), custom_call_target="tpu_custom_call", output_to_operand_aliasing={{3}: (0, {})} | custom-call | tf_op jit(solution)/shard_map/finish/pallas_call | solution.py:431
Async XLA Ops:
  0.6 1.0 %copy-start = (s32[40,16,128]{2,1,0:T(8,128)S(1)}, s32[40,16,128]{2,1,0:T(8,128)}, u32[]{:S(2)}) copy-start(s32[40,16,128]{2,1,0:T(8,128)} %mask.1) | copy-start | bytes 983044
  1.6 1.0 %copy-start.2 = (f32[40,16,128]{2,1,0:T(8,128)S(1)}, f32[40,16,128]{2,1,0:T(8,128)}, u32[]{:S(2)}) copy-start(f32[40,16,128]{2,1,0:T(8,128)} %temp.1) | copy-start | bytes 983044
  2.6 1.0 %copy-start.3 = (f32[40,16,128]{2,1,0:T(8,128)S(1)}, f32[40,16,128]{2,1,0:T(8,128)}, u32[]{:S(2)}) copy-start(f32[40,16,128]{2,1,0:T(8,128)} %uvel.1) | copy-start | bytes 983044
  3.6 1.0 %copy-start.4 = (f32[40,16,128]{2,1,0:T(8,128)S(1)}, f32[40,16,128]{2,1,0:T(8,128)}, u32[]{:S(2)}) copy-start(f32[40,16,128]{2,1,0:T(8,128)} %vvel.1) | copy-start | bytes 983044
  5.0 5.3 %copy-start.5 = (f32[40,16,128]{2,1,0:T(8,128)S(1)}, f32[40,16,128]{2,1,0:T(8,128)}, u32[]{:S(2)}) copy-start(f32[40,16,128]{2,1,0:T(8,128)} %param.13) | copy-start | bytes 983044
  5.0 10.9 %collective-permute-start = (f32[280,128]{1,0:T(8,128)S(1)}, f32[280,128]{1,0:T(8,128)S(1)}, u32[]{:S(2)}, u32[]{:S(2)}) collective-permute-start(f32[280,128]{1,0:T(8,128)S(1)} %get-tuple-element.12.sent1), channel_id=1, source_target_pairs={{0,8},{8,0},{1,9},{9,1},{2,10},{10,2},{3,11},{11,3},{4,12},{12,4},... | collective-permute-start | bytes 430088 | tf_op jit(solution)/shard_map/ppermute | solution.py:410
  5.3 5.0 %copy-start.6 = (f32[16,128]{1,0:T(8,128)S(1)}, f32[16,128]{1,0:T(8,128)}, u32[]{:S(2)}) copy-start(f32[16,128]{1,0:T(8,128)} %inv_dy.5) | copy-start | bytes 24580
  5.3 5.0 %copy-start.7 = (f32[16,128]{1,0:T(8,128)S(1)}, f32[16,128]{1,0:T(8,128)}, u32[]{:S(2)}) copy-start(f32[16,128]{1,0:T(8,128)} %spread.5) | copy-start | bytes 24580
  5.3 5.0 %copy-start.8 = (f32[16,128]{1,0:T(8,128)S(1)}, f32[16,128]{1,0:T(8,128)}, u32[]{:S(2)}) copy-start(f32[16,128]{1,0:T(8,128)} %inv_dx.3) | copy-start | bytes 24580
  5.3 5.0 %copy-start.9 = (f32[16,128]{1,0:T(8,128)S(1)}, f32[16,128]{1,0:T(8,128)}, u32[]{:S(2)}) copy-start(f32[16,128]{1,0:T(8,128)} %coriolis.1) | copy-start | bytes 24580
  5.3 5.0 %copy-start.10 = (s32[16,128]{1,0:T(8,128)S(1)}, s32[16,128]{1,0:T(8,128)}, u32[]{:S(2)}) copy-start(s32[16,128]{1,0:T(8,128)} %levels.1) | copy-start | bytes 24580
  5.5 11.3 %collective-permute-start.3 = (f32[280,128]{1,0:T(8,128)S(1)}, f32[280,128]{1,0:T(8,128)S(1)}, u32[]{:S(2)}, u32[]{:S(2)}) collective-permute-start(f32[280,128]{1,0:T(8,128)S(1)} %fold_pack.1.mine), channel_id=1, source_target_pairs={{8,16},{16,8},{9,17},{17,9},{10,18},{18,10},{11,19},{19,11},{12,20... | collective-permute-start | bytes 430088 | tf_op jit(solution)/shard_map/ppermute | solution.py:398
  7.7 8.1 %collective-permute-start.2 = (f32[80,128]{1,0:T(8,128)S(1)}, f32[80,128]{1,0:T(8,128)S(1)}, u32[]{:S(2)}, u32[]{:S(2)}) collective-permute-start(f32[80,128]{1,0:T(8,128)S(1)} %get-tuple-element.13.edges), channel_id=1, source_target_pairs={{1,2},{2,1},{3,4},{4,3},{5,6},{6,5},{7,0},{0,7},{9,10},{10,9},{11,... | collective-permute-start | bytes 122888 | tf_op jit(solution)/shard_map/ppermute | solution.py:411
  7.8 8.1 %collective-permute-start.1 = (f32[80,128]{1,0:T(8,128)S(1)}, f32[80,128]{1,0:T(8,128)S(1)}, u32[]{:S(2)}, u32[]{:S(2)}) collective-permute-start(f32[80,128]{1,0:T(8,128)S(1)} %get-tuple-element.13.edges), channel_id=1, source_target_pairs={{0,1},{1,0},{2,3},{3,2},{4,5},{5,4},{6,7},{7,6},{8,9},{9,8},{10,11... | collective-permute-start | bytes 122888 | tf_op jit(solution)/shard_map/ppermute | solution.py:412
  10.3 5.5 %copy-start.1 = (s32[40,16,128]{2,1,0:T(8,128)S(1)}, s32[40,16,128]{2,1,0:T(8,128)}, u32[]{:S(2)}) copy-start(s32[40,16,128]{2,1,0:T(8,128)} %mask.1) | copy-start | bytes 983044

commit v3 on v2

--- a/solution.py
+++ b/solution.py
@@ -39,51 +39,36 @@
     return TAIL, 32 * field + 4 * (number - 32)
 
 
-def fold_pack_kernel(temp, uvel, vvel, mask, out, half0, half1, half2, halfm, sems):
-    depth = temp.shape[0]
+def edges_kernel(
+    temp_hbm, uvel_hbm, vvel_hbm, mask_hbm, temp, uvel, vvel, mask, first, second, edges, raw, sems
+):
+    depth = temp.shape[0] // ROWS
     odd = lax.rem(lax.axis_index("lat"), 2)
-    copies = []
-    for number, (field, half) in enumerate(
-        zip((temp, uvel, vvel, mask), (half0, half1, half2, halfm))
-    ):
-        copies.append(
-            pltpu.make_async_copy(
-                field.at[:, pl.ds(pl.multiple_of(odd * TILE, TILE), TILE), :],
-                half.reshape(depth, TILE, LANES),
-                sems.at[number],
-            )
-        )
+    sources = (temp_hbm, uvel_hbm, vvel_hbm, mask_hbm)
+    copies = [
+        pltpu.make_async_copy(source, target.reshape(depth, ROWS, LANES), sems.at[number])
+        for number, (source, target) in enumerate(zip(sources, (temp, uvel, vvel, raw)))
+    ]
     for copy in copies:
         copy.start()
-    near = (TILE - 1) * odd
-    far = near + 1 - 2 * odd
     keep = jnp.where(lax.axis_index("lat") == 0, 0.0, 1.0)
-    for number, half in enumerate((half0, half1, half2)):
-        copies[number].wait()
-        base = 2 * depth * number
-        out[base : base + depth, :] = half[pl.ds(near, depth, stride=TILE), :] * keep
-        out[base + depth : base + 2 * depth, :] = half[pl.ds(far, depth, stride=TILE), :] * keep
-    copies[3].wait()
-    out[6 * depth : 7 * depth, :] = halfm[pl.ds(near, depth, stride=TILE), :].astype(jnp.float32) * keep
-
-
-def pack_kernel(temp, uvel, vvel, mask, first, edges):
-    depth = temp.shape[0] // ROWS
-    odd = lax.rem(lax.axis_index("lat"), 2)
-    near = (ROWS - 1) * (1 - odd)
-    far = near + 2 * odd - 1
-    for number, field in enumerate((temp, uvel, vvel)):
-        base = 2 * depth * number
-        first[base : base + depth, :] = field[level_rows(near, depth), :]
-        first[base + depth : base + 2 * depth, :] = field[level_rows(far, depth), :]
-    first[6 * depth : 7 * depth, :] = mask[level_rows(near, depth), :].astype(jnp.float32)
     group = lane_index(ROWS) // 4
     slabs = [jnp.zeros((ROWS, LANES), jnp.float32) for _ in range(TAIL + 1)]
-    for number in range(depth):
-        for index, field in enumerate((temp, uvel, vvel, mask)):
-            block = level(field, number).astype(jnp.float32)
+    for index, field in enumerate((temp, uvel, vvel, mask)):
+        copies[index].wait()
+        if index == 3:
+            mask[...] = raw[...].astype(jnp.float32)
+        for out, near in ((second, (ROWS - 1) * odd), (first, (ROWS - 1) * (1 - odd))):
+            far = near + jnp.where(near == 0, 1, -1)
+            factor = keep if out is second else 1.0
+            base = 2 * depth * index
+            out[base : base + depth, :] = field[level_rows(near, depth), :] * factor
+            if index < 3:
+                out[base + depth : base + 2 * depth, :] = field[level_rows(far, depth), :] * factor
+        for number in range(depth):
             slab, start = slab_place(number, index)
-            slabs[slab] = jnp.where(group == start // 4, turn_lanes(block, start + 2), slabs[slab])
+            moved = turn_lanes(level(field, number), start + 2)
+            slabs[slab] = jnp.where(group == start // 4, moved, slabs[slab])
     for number, slab in enumerate(slabs):
         edges[number * ROWS : (number + 1) * ROWS, :] = slab
 
@@ -117,9 +102,6 @@
 
     def rows_of(ref, row):
         return ref[level_rows(row, depth), :]
-
-    def wet_of(row):
-        return rows_of(mask, row).astype(jnp.float32)
 
     fields = (temp, uvel, vvel)
     steps = 0
@@ -133,7 +115,7 @@
         scale = inv_dx[one, :]
         spread_x = spread[one, :] * scale * scale
         scale = scale * (-1.0 / 24.0)
-        wet = wet_of(row)
+        wet = rows_of(mask, row)
         face_w = wet * jnp.where(lane >= 1, turn_lanes(wet, 1), 0.0)
         face_e = wet * jnp.where(lane < LANES - 1, turn_lanes(wet, -1), 0.0)
         u = rows_of(uvel, row)
@@ -145,7 +127,7 @@
         spread_y = spread[one, :] * scale_y * scale_y
         scale_y = scale_y * (-1.0 / 24.0)
         if row + 1 < ROWS:
-            face_n = wet * wet_of(row + 1)
+            face_n = wet * rows_of(mask, row + 1)
             speed_n = face_n * (rows_of(vvel, row) + rows_of(vvel, row + 1))
         turn = wet * coriolis[one, :]
         for number, field in enumerate(fields):
@@ -187,7 +169,7 @@
     side = odd_sign.astype(jnp.float32)
     wet = piece(mine, 6, depth)
     face = piece(ghost, 6, depth) * wet
-    face_next = wet * mask[level_rows(far, depth), :].astype(jnp.float32)
+    face_next = wet * mask[level_rows(far, depth), :]
     inv0 = inv_dy[pl.ds(near, 1), :]
     inv1 = inv_dy[pl.ds(far, 1), :] * side
     mix0 = spread[pl.ds(near, 1), :] * inv0 * inv0
@@ -385,28 +367,20 @@
     limit = pltpu.CompilerParams(vmem_limit_bytes=16 << 20)
     both = ("lat", "lon")
     lon_first, lon_second, lat_first, lat_second = exchange_routes(lats, lons)
-    sent2 = pl.pallas_call(
-        fold_pack_kernel,
-        name="fold_pack",
-        out_shape=f32(7 * depth, lanes),
+    inputs = [pltpu.with_memory_space_constraint(x, pltpu.HBM) for x in (temp, uvel, vvel, wet_mask)]
+    temp, uvel, vvel, wet, sent1, sent2, edges = pl.pallas_call(
+        edges_kernel,
+        name="edges",
+        out_shape=(f32(flat, lanes),) * 4
+        + (f32(7 * depth, lanes),) * 2
+        + (f32((TAIL + 1) * rows, lanes),),
         in_specs=[HBM] * 4,
-        out_specs=VMEM,
-        scratch_shapes=[vmem(depth * TILE, lanes)] * 3
-        + [vmem(depth * TILE, lanes, dtype=jnp.int32), pltpu.SemaphoreType.DMA((4,))],
+        out_specs=(VMEM,) * 7,
+        scratch_shapes=[vmem(flat, lanes, dtype=jnp.int32), pltpu.SemaphoreType.DMA((4,))],
         compiler_params=limit,
-    )(temp, uvel, vvel, wet_mask)
+    )(*inputs)
+    vert_mixing = vert_mixing.reshape(flat, lanes)
     got2 = lax.ppermute(sent2, both, lat_second)
-    temp, uvel, vvel, vert_mixing, wet_mask = (
-        x.reshape(flat, lanes) for x in (temp, uvel, vvel, vert_mixing, wet_mask)
-    )
-    sent1, edges = pl.pallas_call(
-        pack_kernel,
-        name="pack",
-        out_shape=(f32(7 * depth, lanes), f32((TAIL + 1) * rows, lanes)),
-        in_specs=[VMEM] * 4,
-        out_specs=(VMEM,) * 2,
-        compiler_params=limit,
-    )(temp, uvel, vvel, wet_mask)
     got1 = lax.ppermute(sent1, both, lat_first)
     east2 = lax.ppermute(edges, both, lon_second)
     east1 = lax.ppermute(edges, both, lon_first)
@@ -418,7 +392,7 @@
         out_specs=(VMEM,) * 3,
         compiler_params=limit,
         cost_estimate=pl.CostEstimate(flops=20_000_000, bytes_accessed=6_000_000, transcendentals=0),
-    )(temp, uvel, vvel, wet_mask, vert_mixing, inv_dx, inv_dy, horiz_mixing, coriolis, levels)
+    )(temp, uvel, vvel, wet, vert_mixing, inv_dx, inv_dy, horiz_mixing, coriolis, levels)
     prov = pl.pallas_call(
         ghosts_kernel,
         name="ghosts",
@@ -427,7 +401,7 @@
         out_specs=VMEM,
         input_output_aliases={0: 0},
         compiler_params=limit,
-    )(prov, sent1, got1, edges, east1, east2, wet_mask, inv_dx, inv_dy, horiz_mixing)
+    )(prov, sent1, got1, edges, east1, east2, wet, inv_dx, inv_dy, horiz_mixing)
     outs = pl.pallas_call(
         finish_kernel,
         name="finish",
@@ -441,7 +415,7 @@
             pltpu.SemaphoreType.DMA((9,)),
         ],
         compiler_params=limit,
-    )(prov, solve, middle, sent2, got2, wet_mask, inv_dy, horiz_mixing)
+    )(prov, solve, middle, sent2, got2, wet, inv_dy, horiz_mixing)
     return tuple(x.reshape(depth, rows, lanes) for x in outs[:3])
 
 

time: 18.4 us -> 15.6 us (0.85)
  local copies, waits for them, and re-layouts: 3.92 us -> 0.03 us
  Pallas kernels: 5.23 us -> 6.48 us
    unnamed x22 -> x12, local copies, waits for them, and re-layouts: 3.92 us -> 0.03 us
    pallas_call x2 -> x1, Pallas kernels: 0.59 us -> 1.83 us  [per_device(): pl.pallas_call(edges_kernel, name='edges', out_shape=(f32(flat, lanes),)...]
  transfers between devices with their start and end apart: 4 -> 4, of which waited for: 1 -> 1; matrix products, arithmetic and copies ran while one was open for 0% -> 0% of each run, Pallas kernels for 19% -> 21%
where the time goes in v3:
time: 15.6 us; the launch traced here: 15.5 us
  Pallas kernels  6.48 us (42%)
  starting transfers between devices  5.08 us (33%)
  waiting for transfers between devices  3.14 us (20%)
  between operations  0.74 us (5%)
    ppermute x1, waiting for transfers between devices, per_device(): east2 = lax.ppermute(edges, both, lon_second)  3.13 us
    ppermute x1, starting transfers between devices, per_device(): east1 = lax.ppermute(edges, both, lon_first)  2.56 us
    pallas_call x1, Pallas kernels, per_device(): pl.pallas_call(interior_kernel, name='interior', out_shape=(f32(3, flat,...  2.38 us
    ppermute x1, starting transfers between devices, per_device(): got2 = lax.ppermute(sent2, both, lat_second)  2.14 us
    pallas_call x1, Pallas kernels, per_device(): pl.pallas_call(edges_kernel, name='edges', out_shape=(f32(flat, lanes),)...  1.83 us
    pallas_call x1, Pallas kernels, per_device(): pl.pallas_call(finish_kernel, name='finish', out_shape=(f32(flat, lanes),...  1.37 us
    pallas_call x1, Pallas kernels, per_device(): pl.pallas_call(ghosts_kernel, name='ghosts', out_shape=f32(3, flat, lanes...  0.89 us
    ppermute x1, starting transfers between devices, per_device(): got1 = lax.ppermute(sent1, both, lat_first)  0.36 us
  transfers between devices with their start and end apart: 4, of which 1 were waited for; matrix products, arithmetic and copies ran while one was open for 0% of the time, Pallas kernels for 21%

profile of v3, /device:TPU:15, one launch (start us, length us, event | category | flops | bytes accessed | tf_op | source)
XLA Modules:
  0.0 15.5 jit_solution(11878681791968363446)
XLA Ops:
  0.6 0.0 copy-start
  0.6 0.0 copy-start.2
  0.7 0.0 copy-start.3
  0.7 0.0 copy-start.4
  0.7 0.0 copy-start.5
  0.7 1.8 %edges.1 = (f32[640,128]{1,0:T(8,128)S(1)}, f32[640,128]{1,0:T(8,128)S(1)}, f32[640,128]{1,0:T(8,128)S(1)}, f32[640,128]{1,0:T(8,128)S(1)}, f32[280,128]{1,0:T(8...) custom-call(f32[40,16,128]{2,1,0:T(8,128)} %temp_hbm.1, f32[40,16,128]{2,1,0:T(8,128)} %uvel_hbm.1, ...), custom_call_target="tpu_custom_call" | custom-call | tf_op jit(solution)/shard_map/edges/pallas_call | solution.py:371
  2.5 0.0 copy-start.1
  2.5 0.4 %collective-permute-start = (f32[280,128]{1,0:T(8,128)S(1)}, f32[280,128]{1,0:T(8,128)S(1)}, u32[]{:S(2)}, u32[]{:S(2)}) collective-permute-start(f32[280,128]{1,0:T(8,128)S(1)} %get-tuple-element.21.sent1), channel_id=1, source_target_pairs={{0,8},{8,0},{1,9},{9,1},{2,10},{10,2},{3,11},{11,3},{4,12},{12,4},... | collective-permute-start | bytes 430088 | tf_op jit(solution)/shard_map/ppermute | solution.py:384
  2.9 2.1 %collective-permute-start.3 = (f32[280,128]{1,0:T(8,128)S(1)}, f32[280,128]{1,0:T(8,128)S(1)}, u32[]{:S(2)}, u32[]{:S(2)}) collective-permute-start(f32[280,128]{1,0:T(8,128)S(1)} %get-tuple-element.25.mine), channel_id=1, source_target_pairs={{8,16},{16,8},{9,17},{17,9},{10,18},{18,10},{11,19},{19,11},{12,20... | collective-permute-start | bytes 430088 | tf_op jit(solution)/shard_map/ppermute | solution.py:383
  5.0 0.0 collective-permute-start.2
  5.1 2.6 %collective-permute-start.1 = (f32[80,128]{1,0:T(8,128)S(1)}, f32[80,128]{1,0:T(8,128)S(1)}, u32[]{:S(2)}, u32[]{:S(2)}) collective-permute-start(f32[80,128]{1,0:T(8,128)S(1)} %get-tuple-element.22.edges), channel_id=1, source_target_pairs={{0,1},{1,0},{2,3},{3,2},{4,5},{5,4},{6,7},{7,6},{8,9},{9,8},{10,11... | collective-permute-start | bytes 122888 | tf_op jit(solution)/shard_map/ppermute | solution.py:386
  7.6 0.0 copy-done
  7.6 0.0 copy-done.2
  7.6 0.0 copy-done.3
  7.6 0.0 copy-done.4
  7.6 0.0 copy-done.5
  7.6 0.0 copy-done.1
  7.7 2.4 %interior.1 = (f32[3,640,128]{2,1,0:T(8,128)S(1)}, f32[3,640,128]{2,1,0:T(8,128)S(1)}, f32[16,128]{1,0:T(8,128)S(1)}) custom-call(f32[640,128]{1,0:T(8,128)S(1)} %get-tuple-element.16.temp, f32[640,128]{1,0:T(8,128)S(1)} %get-tuple-element.17.uvel, f32[640,128]{1,0:T(8,128)S(1)} %get-tuple-element.18.vvel, f32[640,128]{1,0:T(8,128)S(1)} %get-tuple-element.19.mask, ...), custom_call_target="tpu_custom_call" | custom-call | flops 20000000 | bytes 6000000 | tf_op jit(solution)/shard_map/interior/pallas_call | solution.py:387
  10.0 3.1 %collective-permute-done.2.east2 = f32[80,128]{1,0:T(8,128)S(1)} collective-permute-done((f32[80,128]{1,0:T(8,128)S(1)}, f32[80,128]{1,0:T(8,128)S(1)}, u32[]{:S(2)}, u32[]{:S(2)}) %collective-permute-start.2) | collective-permute-done | bytes 40992 | tf_op jit(solution)/shard_map/ppermute | solution.py:385
  13.2 0.0 collective-permute-done.1.east1
  13.2 0.0 collective-permute-done.got1
  13.2 0.9 %ghosts.1.prov_in = f32[3,640,128]{2,1,0:T(8,128)S(1)} custom-call(f32[3,640,128]{2,1,0:T(8,128)S(1)} %get-tuple-element.20.prov_in, f32[280,128]{1,0:T(8,128)S(1)} %get-tuple-element.21.sent1, f32[280,128]{1,0:T(8,128)S(1)} %collective-permute-done.got1, f32[80,128]{1,0:T(8,128)S(1)} %get-tuple-element.22.edges, ...), custom_call_target="tpu_custom_call", output_to_operand_aliasing={{}: (0, {})} | custom-call | tf_op jit(solution)/shard_map/ghosts/pallas_call | solution.py:396
  14.1 0.0 collective-permute-done.3.ghost
  14.1 1.4 %finish.1 = (f32[640,128]{1,0:T(8,128)}, f32[640,128]{1,0:T(8,128)}, f32[640,128]{1,0:T(8,128)}, f32[3,640,128]{2,1,0:T(8,128)S(1)}) custom-call(f32[3,640,128]{2,1,0:T(8,128)S(1)} %ghosts.1.prov_in, f32[3,640,128]{2,1,0:T(8,128)S(1)} %get-tuple-element.23.solve, f32[16,128]{1,0:T(8,128)S(1)} %get-tuple-element.24.middle, ...), custom_call_target="tpu_custom_call", output_to_operand_aliasing={{3}: (0, {})} | custom-call | tf_op jit(solution)/shard_map/finish/pallas_call | solution.py:405
Async XLA Ops:
  0.6 7.0 %copy-start = (f32[40,16,128]{2,1,0:T(8,128)S(1)}, f32[40,16,128]{2,1,0:T(8,128)}, u32[]{:S(2)}) copy-start(f32[40,16,128]{2,1,0:T(8,128)} %param.13) | copy-start | bytes 983044
  0.6 7.0 %copy-start.2 = (f32[16,128]{1,0:T(8,128)S(1)}, f32[16,128]{1,0:T(8,128)}, u32[]{:S(2)}) copy-start(f32[16,128]{1,0:T(8,128)} %spread.5) | copy-start | bytes 24580
  0.7 7.0 %copy-start.3 = (f32[16,128]{1,0:T(8,128)S(1)}, f32[16,128]{1,0:T(8,128)}, u32[]{:S(2)}) copy-start(f32[16,128]{1,0:T(8,128)} %inv_dx.3) | copy-start | bytes 24580
  0.7 7.0 %copy-start.4 = (f32[16,128]{1,0:T(8,128)S(1)}, f32[16,128]{1,0:T(8,128)}, u32[]{:S(2)}) copy-start(f32[16,128]{1,0:T(8,128)} %coriolis.1) | copy-start | bytes 24580
  0.7 7.0 %copy-start.5 = (s32[16,128]{1,0:T(8,128)S(1)}, s32[16,128]{1,0:T(8,128)}, u32[]{:S(2)}) copy-start(s32[16,128]{1,0:T(8,128)} %levels.1) | copy-start | bytes 24580
  2.5 5.1 %copy-start.1 = (f32[16,128]{1,0:T(8,128)S(1)}, f32[16,128]{1,0:T(8,128)}, u32[]{:S(2)}) copy-start(f32[16,128]{1,0:T(8,128)} %inv_dy.5) | copy-start | bytes 24580
  2.5 10.6 %collective-permute-start = (f32[280,128]{1,0:T(8,128)S(1)}, f32[280,128]{1,0:T(8,128)S(1)}, u32[]{:S(2)}, u32[]{:S(2)}) collective-permute-start(f32[280,128]{1,0:T(8,128)S(1)} %get-tuple-element.21.sent1), channel_id=1, source_target_pairs={{0,8},{8,0},{1,9},{9,1},{2,10},{10,2},{3,11},{11,3},{4,12},{12,4},... | collective-permute-start | bytes 430088 | tf_op jit(solution)/shard_map/ppermute | solution.py:384
  2.9 11.2 %collective-permute-start.3 = (f32[280,128]{1,0:T(8,128)S(1)}, f32[280,128]{1,0:T(8,128)S(1)}, u32[]{:S(2)}, u32[]{:S(2)}) collective-permute-start(f32[280,128]{1,0:T(8,128)S(1)} %get-tuple-element.25.mine), channel_id=1, source_target_pairs={{8,16},{16,8},{9,17},{17,9},{10,18},{18,10},{11,19},{19,11},{12,20... | collective-permute-start | bytes 430088 | tf_op jit(solution)/shard_map/ppermute | solution.py:383
  5.0 8.1 %collective-permute-start.2 = (f32[80,128]{1,0:T(8,128)S(1)}, f32[80,128]{1,0:T(8,128)S(1)}, u32[]{:S(2)}, u32[]{:S(2)}) collective-permute-start(f32[80,128]{1,0:T(8,128)S(1)} %get-tuple-element.22.edges), channel_id=1, source_target_pairs={{1,2},{2,1},{3,4},{4,3},{5,6},{6,5},{7,0},{0,7},{9,10},{10,9},{11,... | collective-permute-start | bytes 122888 | tf_op jit(solution)/shard_map/ppermute | solution.py:385
  5.1 8.1 %collective-permute-start.1 = (f32[80,128]{1,0:T(8,128)S(1)}, f32[80,128]{1,0:T(8,128)S(1)}, u32[]{:S(2)}, u32[]{:S(2)}) collective-permute-start(f32[80,128]{1,0:T(8,128)S(1)} %get-tuple-element.22.edges), channel_id=1, source_target_pairs={{0,1},{1,0},{2,3},{3,2},{4,5},{5,4},{6,7},{7,6},{8,9},{9,8},{10,11... | collective-permute-start | bytes 122888 | tf_op jit(solution)/shard_map/ppermute | solution.py:386

commit v4 on v2

--- a/solution.py
+++ b/solution.py
@@ -65,9 +65,10 @@
         out[base + depth : base + 2 * depth, :] = half[pl.ds(far, depth, stride=TILE), :] * keep
     copies[3].wait()
     out[6 * depth : 7 * depth, :] = halfm[pl.ds(near, depth, stride=TILE), :].astype(jnp.float32) * keep
-
-
-def pack_kernel(temp, uvel, vvel, mask, first, edges):
+    out[7 * depth :, :] = jnp.zeros((TILE, LANES), jnp.float32)
+
+
+def rows_pack_kernel(temp, uvel, vvel, mask, after, first):
     depth = temp.shape[0] // ROWS
     odd = lax.rem(lax.axis_index("lat"), 2)
     near = (ROWS - 1) * (1 - odd)
@@ -77,23 +78,11 @@
         first[base : base + depth, :] = field[level_rows(near, depth), :]
         first[base + depth : base + 2 * depth, :] = field[level_rows(far, depth), :]
     first[6 * depth : 7 * depth, :] = mask[level_rows(near, depth), :].astype(jnp.float32)
-    group = lane_index(ROWS) // 4
-    slabs = [jnp.zeros((ROWS, LANES), jnp.float32) for _ in range(TAIL + 1)]
-    for number in range(depth):
-        for index, field in enumerate((temp, uvel, vvel, mask)):
-            block = level(field, number).astype(jnp.float32)
-            slab, start = slab_place(number, index)
-            slabs[slab] = jnp.where(group == start // 4, turn_lanes(block, start + 2), slabs[slab])
-    for number, slab in enumerate(slabs):
-        edges[number * ROWS : (number + 1) * ROWS, :] = slab
-
-
-def interior_kernel(
-    temp, uvel, vvel, mask, mixing, inv_dx, inv_dy, spread, coriolis, levels, prov, solve, middle
-):
+
+
+def columns_kernel(temp, uvel, vvel, mask, mixing, levels, edges, longer, solve, middle):
     depth = temp.shape[0] // ROWS
     half = depth // 2
-    lane = lane_index(depth)
     active = levels[...]
     zero = jnp.zeros((ROWS, LANES), jnp.float32)
 
@@ -102,9 +91,10 @@
             return jnp.where(number + 1 < active, level(mixing, number + 1), 0.0)
         return zero
 
+    group = lane_index(ROWS) // 4
+    slabs = [zero] * (TAIL + 1)
     chains = [zero, zero]
-
-    def factor(step):
+    for step in range(half):
         for side, number in enumerate((step, depth - 1 - step)):
             above, below = coupling(number - 1), coupling(number)
             done, left = (above, below) if side == 0 else (below, above)
@@ -114,6 +104,23 @@
             solve[0, here, :] = inverse
             solve[1, here, :] = done * inverse
             solve[2, here, :] = chains[side]
+            for index, field in enumerate((temp, uvel, vvel, mask)):
+                block = level(field, number).astype(jnp.float32)
+                slab, start = slab_place(number, index)
+                moved = turn_lanes(block, start + 2)
+                slabs[slab] = jnp.where(group == start // 4, moved, slabs[slab])
+    middle[...] = 1.0 / (1.0 - chains[0] * chains[1])
+    for number, slab in enumerate(slabs):
+        edges[number * ROWS : (number + 1) * ROWS, :] = slab
+        longer[number * ROWS : (number + 1) * ROWS, :] = slab
+    longer[(TAIL + 1) * ROWS :, :] = jnp.zeros((TILE, LANES), jnp.float32)
+
+
+def interior_kernel(
+    temp, uvel, vvel, mask, inv_dx, inv_dy, spread, coriolis, prov
+):
+    depth = temp.shape[0] // ROWS
+    lane = lane_index(depth)
 
     def rows_of(ref, row):
         return ref[level_rows(row, depth), :]
@@ -122,13 +129,9 @@
         return rows_of(mask, row).astype(jnp.float32)
 
     fields = (temp, uvel, vvel)
-    steps = 0
     advect_south = [0.0] * 3
     spread_south = [0.0] * 3
     for row in range(ROWS):
-        while steps < half and steps * ROWS <= row * half + half - 1:
-            factor(steps)
-            steps += 1
         one = slice(row, row + 1)
         scale = inv_dx[one, :]
         spread_x = spread[one, :] * scale * scale
@@ -175,10 +178,6 @@
                 total = total - turn * u
             target = prov.at[number]
             target[level_rows(row, depth), :] = q + total
-    while steps < half:
-        factor(steps)
-        steps += 1
-    middle[...] = 1.0 / (1.0 - chains[0] * chains[1])
 
 
 def add_row_ghosts(prov, mine, ghost, near, odd_sign, mask, inv_dy, spread, flip):
@@ -207,80 +206,75 @@
         view[level_rows(far, depth), :] -= inv1 * reach
 
 
-def ghosts_kernel(
-    prov_in, sent1, got1, edges, east1, east2, mask, inv_dx, inv_dy, spread, prov
-):
-    depth = prov.shape[1] // ROWS
-    odd = lax.rem(lax.axis_index("lat"), 2)
-    lon_odd = lax.rem(lax.axis_index("lon"), 2) == 1
-    lane = lane_index(ROWS)
-    quad = lane % 4
+def column_ghosts(edges, other, west, inv_dx, spread):
+    quad = lane_index(ROWS) % 4
     four = jnp.where(quad < 2, LANES - 2 + quad, quad - 2)
+    side = jnp.where(west, 1, -1)
+
+    def toward(x, count):
+        return pltpu.roll(x, lax.rem(side * count + LANES, LANES), 1)
 
     def replicate(x):
         return jnp.take_along_axis(x, four, axis=1, mode="promise_in_bounds")
 
     wide = replicate(inv_dx[...])
     wide2 = replicate(spread[...]) * wide * wide
+    wide = wide * side.astype(jnp.float32)
     own = [level(edges, s) for s in range(TAIL + 1)]
-    first = [level(east1, s) for s in range(TAIL + 1)]
-    second = [level(east2, s) for s in range(TAIL + 1)]
-    west = [jnp.where(quad < 2, jnp.where(lon_odd, a, b), o) for a, b, o in zip(first, second, own)]
-    east = [jnp.where(quad < 2, o, jnp.where(lon_odd, b, a)) for a, b, o in zip(first, second, own)]
+    ghost = quad * side < jnp.where(west, 2, -1)
+    both = [jnp.where(ghost, level(other, s), own[s]) for s in range(TAIL + 1)]
+    near_lane = quad == jnp.where(west, 2, 1)
 
     def split(slabs):
         tail = [slabs[TAIL] if f == 0 else turn_lanes(slabs[TAIL], -32 * f) for f in range(4)]
         return [slabs[:TAIL], tail]
 
     corrections = []
-    for west_part, east_part, own_part in zip(split(west), split(east), split(own)):
-        wet = west_part[3]
-        face = turn_lanes(wet, 1) * wet
-        speed = face * (turn_lanes(west_part[1], 1) + west_part[1]) * (1.0 / 24.0)
-        speed_next = turn_lanes(speed, -1)
-        wet_e = east_part[3]
-        face_e = turn_lanes(wet_e, -1) * wet_e
-        speed_e = face_e * (turn_lanes(east_part[1], -1) + east_part[1]) * (1.0 / 24.0)
-        speed_e_before = turn_lanes(speed_e, 1)
-        part = []
+    for part, mine in zip(split(both), split(own)):
+        face = toward(part[3], 1) * part[3]
+        speed = face * (toward(part[1], 1) + part[1]) * (1.0 / 24.0)
+        speed_next = toward(speed, -1)
+        result = []
         for number in range(3):
-            mine = own_part[number]
-            q = west_part[number]
-            back = turn_lanes(q, 1)
-            advect = speed * (7.0 * (back + q) - (turn_lanes(q, 2) + turn_lanes(q, -1)))
-            reach = speed_next * turn_lanes(q - mine, 1)
-            near = wide * (advect + reach) - wide2 * (face * (q - back))
-            distant = turn_lanes(reach, 1) * wide
-            q = east_part[number]
-            ahead = turn_lanes(q, -1)
-            advect = speed_e * (7.0 * (ahead + q) - (turn_lanes(q, -2) + turn_lanes(q, 1)))
-            reach = speed_e_before * turn_lanes(q - mine, -1)
-            near_e = wide2 * (face_e * (ahead - q)) - wide * (advect + reach)
-            distant_e = turn_lanes(reach, -1) * wide
-            part.append(
-                jnp.where(
-                    quad < 2,
-                    jnp.where(quad == 0, distant_e, near_e),
-                    jnp.where(quad == 2, near, -distant),
-                )
-            )
-        corrections.append(part)
-
-    border = (lane < 2) | (lane >= LANES - 2)
+            q = part[number]
+            ahead = toward(q, 1)
+            advect = speed * (7.0 * (ahead + q) - (toward(q, 2) + toward(q, -1)))
+            reach = speed_next * toward(q - mine[number], 1)
+            near = wide * (advect + reach) + wide2 * (face * (ahead - q))
+            result.append(jnp.where(near_lane, near, -wide * toward(reach, 1)))
+        corrections.append(result)
+    return corrections
+
+
+def border_of(west):
+    lane = lane_index(ROWS)
+    return jnp.where(west, lane, LANES - 1 - lane) < 2
+
+
+def border_part(corrections, border, number, field):
+    if number < 32:
+        source, start = corrections[0][field], 4 * number
+    else:
+        source, start = corrections[1][field], 4 * (number - 32)
+    return jnp.where(border, turn_lanes(source, -(start + 2)), 0.0)
+
+
+def ghosts_kernel(prov_in, sent1, got1, edges, other, mask, inv_dx, inv_dy, spread, prov):
+    depth = prov.shape[1] // ROWS
+    odd = lax.rem(lax.axis_index("lat"), 2)
+    west = lax.rem(lax.axis_index("lon"), 2) == 1
+    corrections = column_ghosts(edges, other, west, inv_dx, spread)
+    border = border_of(west)
     for number in range(depth):
         here = slice(number * ROWS, (number + 1) * ROWS)
         for field in range(3):
-            if number < 32:
-                source, start = corrections[0][field], 4 * number
-            else:
-                source, start = corrections[1][field], 4 * (number - 32)
-            moved = jnp.where(border, turn_lanes(source, -(start + 2)), 0.0)
+            moved = border_part(corrections, border, number, field)
             prov[field, here, :] = prov_in[field, here, :] + moved
     add_row_ghosts(prov, sent1, got1, (ROWS - 1) * (1 - odd), 2 * odd - 1, mask, inv_dy, spread, 1.0)
 
 
 def finish_kernel(
-    prov_in, solve, middle, mine, ghost, mask, inv_dy, spread,
+    prov_in, solve, middle, mine, ghost, edges, other, mask, inv_dx, inv_dy, spread,
     temp_new, uvel_new, vvel_new, prov, work, turned, sems
 ):
     depth = prov.shape[1] // ROWS
@@ -289,9 +283,13 @@
     fold = lax.axis_index("lat") == lax.axis_size("lat") - 1
     lane = lane_index(7 * depth)
     lane = jnp.where(fold, LANES - 1 - lane, lane)
-    turned[...] = jnp.take_along_axis(ghost[...], lane, axis=1, mode="promise_in_bounds")
+    turned[...] = jnp.take_along_axis(ghost[: 7 * depth, :], lane, axis=1, mode="promise_in_bounds")
     flip = jnp.where(fold, -1.0, 1.0)
     add_row_ghosts(prov, mine, turned, (ROWS - 1) * odd, 1 - 2 * odd, mask, inv_dy, spread, flip)
+
+    west = lax.rem(lax.axis_index("lon"), 2) == 0
+    corrections = column_ghosts(edges, other, west, inv_dx, spread)
+    border = border_of(west)
 
     outs = (temp_new, uvel_new, vvel_new)
     zero = jnp.zeros((ROWS, LANES), jnp.float32)
@@ -301,7 +299,8 @@
             here = slice(number * ROWS, (number + 1) * ROWS)
             inverse, carry = solve[0, here, :], solve[1, here, :]
             for field in range(3):
-                value = inverse * prov[field, here, :] + carry * values[side][field]
+                known = prov[field, here, :] + border_part(corrections, border, number, field)
+                value = inverse * known + carry * values[side][field]
                 values[side][field] = value
                 work[field, here, :] = value
     above, below = half - 1, half
@@ -383,56 +382,75 @@
         return pltpu.VMEM(shape, dtype)
 
     limit = pltpu.CompilerParams(vmem_limit_bytes=16 << 20)
+    cheap = pl.CostEstimate(flops=1, bytes_accessed=1, transcendentals=0)
     both = ("lat", "lon")
     lon_first, lon_second, lat_first, lat_second = exchange_routes(lats, lons)
+    inputs = [pltpu.with_memory_space_constraint(x, pltpu.HBM) for x in (temp, uvel, vvel, wet_mask)]
     sent2 = pl.pallas_call(
         fold_pack_kernel,
         name="fold_pack",
-        out_shape=f32(7 * depth, lanes),
+        out_shape=f32(7 * depth + TILE, lanes),
         in_specs=[HBM] * 4,
         out_specs=VMEM,
         scratch_shapes=[vmem(depth * TILE, lanes)] * 3
         + [vmem(depth * TILE, lanes, dtype=jnp.int32), pltpu.SemaphoreType.DMA((4,))],
         compiler_params=limit,
-    )(temp, uvel, vvel, wet_mask)
+        cost_estimate=cheap,
+    )(*inputs)
     got2 = lax.ppermute(sent2, both, lat_second)
     temp, uvel, vvel, vert_mixing, wet_mask = (
         x.reshape(flat, lanes) for x in (temp, uvel, vvel, vert_mixing, wet_mask)
     )
-    sent1, edges = pl.pallas_call(
-        pack_kernel,
-        name="pack",
-        out_shape=(f32(7 * depth, lanes), f32((TAIL + 1) * rows, lanes)),
-        in_specs=[VMEM] * 4,
-        out_specs=(VMEM,) * 2,
-        compiler_params=limit,
-    )(temp, uvel, vvel, wet_mask)
+    sent1 = pl.pallas_call(
+        rows_pack_kernel,
+        name="rows_pack",
+        out_shape=f32(7 * depth, lanes),
+        in_specs=[VMEM] * 4 + [pl.BlockSpec(memory_space=pl.ANY)],
+        out_specs=VMEM,
+        compiler_params=limit,
+        cost_estimate=cheap,
+    )(temp, uvel, vvel, wet_mask, sent2)
     got1 = lax.ppermute(sent1, both, lat_first)
-    east2 = lax.ppermute(edges, both, lon_second)
-    east1 = lax.ppermute(edges, both, lon_first)
-    prov, solve, middle = pl.pallas_call(
+    edges, longer, solve, middle = pl.pallas_call(
+        columns_kernel,
+        name="columns",
+        out_shape=(
+            f32((TAIL + 1) * rows, lanes),
+            f32((TAIL + 1) * rows + TILE, lanes),
+            f32(3, flat, lanes),
+            f32(rows, lanes),
+        ),
+        in_specs=[VMEM] * 6,
+        out_specs=(VMEM,) * 4,
+        compiler_params=limit,
+        cost_estimate=cheap,
+    )(temp, uvel, vvel, wet_mask, vert_mixing, levels)
+    second = lax.ppermute(longer, both, lon_second)
+    first = lax.ppermute(edges, both, lon_first)
+    prov = pl.pallas_call(
         interior_kernel,
         name="interior",
-        out_shape=(f32(3, flat, lanes), f32(3, flat, lanes), f32(rows, lanes)),
-        in_specs=[VMEM] * 10,
-        out_specs=(VMEM,) * 3,
-        compiler_params=limit,
-        cost_estimate=pl.CostEstimate(flops=20_000_000, bytes_accessed=6_000_000, transcendentals=0),
-    )(temp, uvel, vvel, wet_mask, vert_mixing, inv_dx, inv_dy, horiz_mixing, coriolis, levels)
+        out_shape=f32(3, flat, lanes),
+        in_specs=[VMEM] * 8,
+        out_specs=VMEM,
+        compiler_params=limit,
+        cost_estimate=cheap,
+    )(temp, uvel, vvel, wet_mask, inv_dx, inv_dy, horiz_mixing, coriolis)
     prov = pl.pallas_call(
         ghosts_kernel,
         name="ghosts",
         out_shape=f32(3, flat, lanes),
-        in_specs=[VMEM] * 10,
+        in_specs=[VMEM] * 9,
         out_specs=VMEM,
         input_output_aliases={0: 0},
         compiler_params=limit,
-    )(prov, sent1, got1, edges, east1, east2, wet_mask, inv_dx, inv_dy, horiz_mixing)
+        cost_estimate=cheap,
+    )(prov, sent1, got1, edges, first, wet_mask, inv_dx, inv_dy, horiz_mixing)
     outs = pl.pallas_call(
         finish_kernel,
         name="finish",
         out_shape=(f32(flat, lanes),) * 3 + (f32(3, flat, lanes),),
-        in_specs=[VMEM] * 8,
+        in_specs=[VMEM] * 11,
         out_specs=(HBM,) * 3 + (VMEM,),
         input_output_aliases={0: 3},
         scratch_shapes=[
@@ -441,7 +459,8 @@
             pltpu.SemaphoreType.DMA((9,)),
         ],
         compiler_params=limit,
-    )(prov, solve, middle, sent2, got2, wet_mask, inv_dy, horiz_mixing)
+        cost_estimate=cheap,
+    )(prov, solve, middle, sent2, got2, edges, second, wet_mask, inv_dx, inv_dy, horiz_mixing)
     return tuple(x.reshape(depth, rows, lanes) for x in outs[:3])
 
 

time: 18.4 us -> 15.9 us (0.86)
  the two profiles are of different devices: /device:TPU:15 before, /device:TPU:0 now
where the time goes in v4:
time: 15.9 us; the launch traced here: 15.8 us
  starting transfers between devices  7.11 us (45%)
  Pallas kernels  6.84 us (43%)
  waiting for transfers between devices  0.99 us (6%)
  between operations  0.79 us (5%)
    ppermute x1, starting transfers between devices, per_device(): got1 = lax.ppermute(sent1, both, lat_first)  4.04 us
    ppermute x1, starting transfers between devices, per_device(): second = lax.ppermute(longer, both, lon_second)  2.55 us
    pallas_call x1, Pallas kernels, per_device(): pl.pallas_call(interior_kernel, name='interior', out_shape=f32(3, flat, l...  2.34 us
    pallas_call x1, Pallas kernels, per_device(): pl.pallas_call(finish_kernel, name='finish', out_shape=(f32(flat, lanes),...  1.73 us
    pallas_call x1, Pallas kernels, per_device(): pl.pallas_call(fold_pack_kernel, name='fold_pack', out_shape=f32(7 * dept...  1.3 us
    ppermute x1, waiting for transfers between devices, per_device(): got1 = lax.ppermute(sent1, both, lat_first)  0.98 us
    pallas_call x1, Pallas kernels, per_device(): pl.pallas_call(ghosts_kernel, name='ghosts', out_shape=f32(3, flat, lanes...  0.92 us
    ppermute x1, starting transfers between devices, per_device(): got2 = lax.ppermute(sent2, both, lat_second)  0.52 us
  transfers between devices with their start and end apart: 4, of which 1 were waited for; matrix products, arithmetic and copies ran while one was open for 0% of the time, Pallas kernels for 24%

profile of v4, /device:TPU:0, one launch (start us, length us, event | category | flops | bytes accessed | tf_op | source)
XLA Modules:
  0.0 15.8 jit_solution(1845272581750645796)
XLA Ops:
  0.6 0.0 copy-start
  0.6 0.0 copy-start.3
  0.7 0.0 copy-start.2
  0.7 0.0 copy-start.1
  0.7 1.3 %fold_pack.1.after.mine = f32[288,128]{1,0:T(8,128)S(1)} custom-call(f32[40,16,128]{2,1,0:T(8,128)} %temp.1, f32[40,16,128]{2,1,0:T(8,128)} %uvel.1, f32[40,16,128]{2,1,0:T(8,128)} %vvel.1, s32[40,16,128]{2,1,0:T(8,128)} %mask.1), custom_call_target="tpu_custom_call" | custom-call | flops 1 | bytes 1 | tf_op jit(solution)/shard_map/fold_pack/pallas_call | solution.py:389
  2.0 0.5 %collective-permute-start.2 = (f32[288,128]{1,0:T(8,128)S(1)}, f32[288,128]{1,0:T(8,128)S(1)}, u32[]{:S(2)}, u32[]{:S(2)}) collective-permute-start(f32[288,128]{1,0:T(8,128)S(1)} %fold_pack.1.after.mine), channel_id=1, source_target_pairs={{8,16},{16,8},{9,17},{17,9},{10,18},{18,10},{11,19},{19,11},{12,20... | collective-permute-start | bytes 442376 | tf_op jit(solution)/shard_map/ppermute | solution.py:400
  2.5 0.0 copy-done
  2.5 0.0 copy-done.3
  2.5 0.0 copy-done.2
  2.5 0.0 copy-done.1
  2.5 0.0 copy-start.4
  2.5 0.0 copy-start.8
  2.5 0.1 rows_pack.1.sent1
  2.6 4.0 %collective-permute-start = (f32[280,128]{1,0:T(8,128)S(1)}, f32[280,128]{1,0:T(8,128)S(1)}, u32[]{:S(2)}, u32[]{:S(2)}) collective-permute-start(f32[280,128]{1,0:T(8,128)S(1)} %rows_pack.1.sent1), channel_id=1, source_target_pairs={{0,8},{8,0},{1,9},{9,1},{2,10},{10,2},{3,11},{11,3},{4,12},{12,4},... | collective-permute-start | bytes 430088 | tf_op jit(solution)/shard_map/ppermute | solution.py:413
  6.7 0.0 copy-done.4
  6.7 0.0 copy-done.8
  6.7 0.0 copy-start.5
  6.7 0.0 copy-start.6
  6.7 0.0 copy-start.7
  6.7 0.0 copy-start.9
  6.7 0.5 %columns.1 = (f32[80,128]{1,0:T(8,128)S(1)}, f32[88,128]{1,0:T(8,128)S(1)}, f32[3,640,128]{2,1,0:T(8,128)S(1)}, f32[16,128]{1,0:T(8,128)S(1)}) custom-call(f32[640,128]{1,0:T(8,128)S(1)} %bitcast.14, f32[640,128]{1,0:T(8,128)S(1)} %bitcast.17, f32[640,128]{1,0:T(8,128)S(1)} %bitcast.20, s32[640,128]{1,0:T(8,128)S(1)} %bitcast.9, f32[640,128]{1,0:T(8,128)S(1)} %bitcast.22, ...), custom_call_target="tpu_custom_call" | custom-call | flops 1 | bytes 1 | tf_op jit(solution)/shard_map/columns/pallas_call | solution.py:414
  7.2 2.5 %collective-permute-start.3 = (f32[88,128]{1,0:T(8,128)S(1)}, f32[88,128]{1,0:T(8,128)S(1)}, u32[]{:S(2)}, u32[]{:S(2)}) collective-permute-start(f32[88,128]{1,0:T(8,128)S(1)} %get-tuple-element.13), channel_id=1, source_target_pairs={{1,2},{2,1},{3,4},{4,3},{5,6},{6,5},{7,0},{0,7},{9,10},{10,9},{11,... | collective-permute-start | bytes 135176 | tf_op jit(solution)/shard_map/ppermute | solution.py:428
  9.7 0.0 collective-permute-start.1
  9.7 0.0 copy-done.5
  9.7 0.0 copy-done.6
  9.7 0.0 copy-done.7
  9.8 0.0 copy-done.9
  9.8 2.3 %interior.1.prov_in = f32[3,640,128]{2,1,0:T(8,128)S(1)} custom-call(f32[640,128]{1,0:T(8,128)S(1)} %bitcast.15, f32[640,128]{1,0:T(8,128)S(1)} %bitcast.18, f32[640,128]{1,0:T(8,128)S(1)} %bitcast.21, s32[640,128]{1,0:T(8,128)S(1)} %bitcast.10, f32[16,128]{1,0:T(8,128)S(1)} %copy-done.5, f32[16,128]{1,0:T(8,128)S(1)} %copy-done.6, f32[16,128]{1,0:T(8,128)S(1)} %copy-done.7, ...), custom_call_target="tpu_custom_call" | custom-call | flops 1 | bytes 1 | tf_op jit(solution)/shard_map/interior/pallas_call | solution.py:430
  12.1 0.0 collective-permute-done.1.other
  12.1 1.0 %collective-permute-done.got1 = f32[280,128]{1,0:T(8,128)S(1)} collective-permute-done((f32[280,128]{1,0:T(8,128)S(1)}, f32[280,128]{1,0:T(8,128)S(1)}, u32[]{:S(2)}, u32[]{:S(2)}) %collective-permute-start) | collective-permute-done | bytes 143392 | tf_op jit(solution)/shard_map/ppermute | solution.py:413
  13.1 0.9 %ghosts.1.prov_in = f32[3,640,128]{2,1,0:T(8,128)S(1)} custom-call(f32[3,640,128]{2,1,0:T(8,128)S(1)} %interior.1.prov_in, f32[280,128]{1,0:T(8,128)S(1)} %rows_pack.1.sent1, f32[280,128]{1,0:T(8,128)S(1)} %collective-permute-done.got1, f32[80,128]{1,0:T(8,128)S(1)} %get-tuple-element.10.edges, ...), custom_call_target="tpu_custom_call", output_to_operand_aliasing={{}: (0, {})} | custom-call | flops 1 | bytes 1 | tf_op jit(solution)/shard_map/ghosts/pallas_call | solution.py:439
  14.0 0.0 collective-permute-done.3.other
  14.0 0.0 collective-permute-done.2.ghost
  14.1 1.7 %finish.1 = (f32[640,128]{1,0:T(8,128)}, f32[640,128]{1,0:T(8,128)}, f32[640,128]{1,0:T(8,128)}, f32[3,640,128]{2,1,0:T(8,128)S(1)}) custom-call(f32[3,640,128]{2,1,0:T(8,128)S(1)} %ghosts.1.prov_in, f32[3,640,128]{2,1,0:T(8,128)S(1)} %get-tuple-element.11.solve, f32[16,128]{1,0:T(8,128)S(1)} %get-tuple-element.12.middle, ...), custom_call_target="tpu_custom_call", output_to_operand_aliasing={{3}: (0, {})} | custom-call | flops 1 | bytes 1 | tf_op jit(solution)/shard_map/finish/pallas_call | solution.py:449
Async XLA Ops:
  0.6 1.9 %copy-start = (s32[40,16,128]{2,1,0:T(8,128)S(1)}, s32[40,16,128]{2,1,0:T(8,128)}, u32[]{:S(2)}) copy-start(s32[40,16,128]{2,1,0:T(8,128)} %mask.1) | copy-start | bytes 983044
  0.6 1.9 %copy-start.3 = (f32[40,16,128]{2,1,0:T(8,128)S(1)}, f32[40,16,128]{2,1,0:T(8,128)}, u32[]{:S(2)}) copy-start(f32[40,16,128]{2,1,0:T(8,128)} %vvel.1) | copy-start | bytes 983044
  0.7 1.9 %copy-start.2 = (f32[40,16,128]{2,1,0:T(8,128)S(1)}, f32[40,16,128]{2,1,0:T(8,128)}, u32[]{:S(2)}) copy-start(f32[40,16,128]{2,1,0:T(8,128)} %uvel.1) | copy-start | bytes 983044
  0.7 1.8 %copy-start.1 = (f32[40,16,128]{2,1,0:T(8,128)S(1)}, f32[40,16,128]{2,1,0:T(8,128)}, u32[]{:S(2)}) copy-start(f32[40,16,128]{2,1,0:T(8,128)} %temp.1) | copy-start | bytes 983044
  2.0 12.1 %collective-permute-start.2 = (f32[288,128]{1,0:T(8,128)S(1)}, f32[288,128]{1,0:T(8,128)S(1)}, u32[]{:S(2)}, u32[]{:S(2)}) collective-permute-start(f32[288,128]{1,0:T(8,128)S(1)} %fold_pack.1.after.mine), channel_id=1, source_target_pairs={{8,16},{16,8},{9,17},{17,9},{10,18},{18,10},{11,19},{19,11},{12,20... | collective-permute-start | bytes 442376 | tf_op jit(solution)/shard_map/ppermute | solution.py:400
  2.5 4.2 %copy-start.4 = (f32[40,16,128]{2,1,0:T(8,128)S(1)}, f32[40,16,128]{2,1,0:T(8,128)}, u32[]{:S(2)}) copy-start(f32[40,16,128]{2,1,0:T(8,128)} %param.13) | copy-start | bytes 983044
  2.5 4.2 %copy-start.8 = (s32[16,128]{1,0:T(8,128)S(1)}, s32[16,128]{1,0:T(8,128)}, u32[]{:S(2)}) copy-start(s32[16,128]{1,0:T(8,128)} %levels.1) | copy-start | bytes 24580
  2.6 10.5 %collective-permute-start = (f32[280,128]{1,0:T(8,128)S(1)}, f32[280,128]{1,0:T(8,128)S(1)}, u32[]{:S(2)}, u32[]{:S(2)}) collective-permute-start(f32[280,128]{1,0:T(8,128)S(1)} %rows_pack.1.sent1), channel_id=1, source_target_pairs={{0,8},{8,0},{1,9},{9,1},{2,10},{10,2},{3,11},{11,3},{4,12},{12,4},... | collective-permute-start | bytes 430088 | tf_op jit(solution)/shard_map/ppermute | solution.py:413
  6.7 3.1 %copy-start.5 = (f32[16,128]{1,0:T(8,128)S(1)}, f32[16,128]{1,0:T(8,128)}, u32[]{:S(2)}) copy-start(f32[16,128]{1,0:T(8,128)} %inv_dx.5) | copy-start | bytes 24580
  6.7 3.1 %copy-start.6 = (f32[16,128]{1,0:T(8,128)S(1)}, f32[16,128]{1,0:T(8,128)}, u32[]{:S(2)}) copy-start(f32[16,128]{1,0:T(8,128)} %inv_dy.5) | copy-start | bytes 24580
  6.7 3.1 %copy-start.7 = (f32[16,128]{1,0:T(8,128)S(1)}, f32[16,128]{1,0:T(8,128)}, u32[]{:S(2)}) copy-start(f32[16,128]{1,0:T(8,128)} %spread.5) | copy-start | bytes 24580
  6.7 3.1 %copy-start.9 = (f32[16,128]{1,0:T(8,128)S(1)}, f32[16,128]{1,0:T(8,128)}, u32[]{:S(2)}) copy-start(f32[16,128]{1,0:T(8,128)} %coriolis.1) | copy-start | bytes 24580
  7.2 6.8 %collective-permute-start.3 = (f32[88,128]{1,0:T(8,128)S(1)}, f32[88,128]{1,0:T(8,128)S(1)}, u32[]{:S(2)}, u32[]{:S(2)}) collective-permute-start(f32[88,128]{1,0:T(8,128)S(1)} %get-tuple-element.13), channel_id=1, source_target_pairs={{1,2},{2,1},{3,4},{4,3},{5,6},{6,5},{7,0},{0,7},{9,10},{10,9},{11,... | collective-permute-start | bytes 135176 | tf_op jit(solution)/shard_map/ppermute | solution.py:428
  9.7 2.4 %collective-permute-start.1 = (f32[80,128]{1,0:T(8,128)S(1)}, f32[80,128]{1,0:T(8,128)S(1)}, u32[]{:S(2)}, u32[]{:S(2)}) collective-permute-start(f32[80,128]{1,0:T(8,128)S(1)} %get-tuple-element.10.edges), channel_id=1, source_target_pairs={{0,1},{1,0},{2,3},{3,2},{4,5},{5,4},{6,7},{7,6},{8,9},{9,8},{10,11... | collective-permute-start | bytes 122888 | tf_op jit(solution)/shard_map/ppermute | solution.py:429

commit v5 on v4

--- a/solution.py
+++ b/solution.py
@@ -1,3 +1,5 @@
+import functools
+
 import jax
 import jax.numpy as jnp
 from jax import lax
@@ -9,6 +11,7 @@
 LANES = 128
 TILE = 8
 TAIL = 4
+ORDER = (2, 1)
 VMEM = pl.BlockSpec(memory_space=pltpu.VMEM)
 HBM = pl.BlockSpec(memory_space=pltpu.HBM)
 
@@ -68,7 +71,18 @@
     out[7 * depth :, :] = jnp.zeros((TILE, LANES), jnp.float32)
 
 
-def rows_pack_kernel(temp, uvel, vvel, mask, after, first):
+def own_slabs(fields, depth):
+    group = lane_index(ROWS) // 4
+    slabs = [jnp.zeros((ROWS, LANES), jnp.float32)] * (TAIL + 1)
+    for number in range(depth):
+        for index, field in enumerate(fields):
+            slab, start = slab_place(number, index)
+            moved = turn_lanes(level(field, number).astype(jnp.float32), start + 2)
+            slabs[slab] = jnp.where(group == start // 4, moved, slabs[slab])
+    return slabs
+
+
+def edges_pack_kernel(temp, uvel, vvel, mask, after, first, zonal1, zonal2, edges):
     depth = temp.shape[0] // ROWS
     odd = lax.rem(lax.axis_index("lat"), 2)
     near = (ROWS - 1) * (1 - odd)
@@ -78,10 +92,27 @@
         first[base : base + depth, :] = field[level_rows(near, depth), :]
         first[base + depth : base + 2 * depth, :] = field[level_rows(far, depth), :]
     first[6 * depth : 7 * depth, :] = mask[level_rows(near, depth), :].astype(jnp.float32)
-
-
-def columns_kernel(temp, uvel, vvel, mask, mixing, levels, edges, longer, solve, middle):
-    depth = temp.shape[0] // ROWS
+    slabs = own_slabs((temp, uvel, vvel, mask), depth)
+    for number, slab in enumerate(slabs):
+        edges[number * ROWS : (number + 1) * ROWS, :] = slab
+    lane = lane_index(ROWS)
+    lon_odd = lax.rem(lax.axis_index("lon"), 2)
+    for out, column in ((zonal1, 2 * lon_odd), (zonal2, 2 - 2 * lon_odd)):
+        source = 4 * (lane % 64 // 2) + lane % 2 + column
+
+        def chosen(x):
+            return jnp.take_along_axis(x, source, axis=1, mode="promise_in_bounds")
+
+        for pair in range(2):
+            both = jnp.where(lane < 64, chosen(slabs[2 * pair]), chosen(slabs[2 * pair + 1]))
+            out[pair * ROWS : (pair + 1) * ROWS, :] = both
+        out[2 * ROWS : 3 * ROWS, :] = chosen(slabs[TAIL])
+        if out is zonal2:
+            out[3 * ROWS :, :] = jnp.zeros((TILE, LANES), jnp.float32)
+
+
+def columns_kernel(mixing, levels, solve, middle):
+    depth = mixing.shape[0] // ROWS
     half = depth // 2
     active = levels[...]
     zero = jnp.zeros((ROWS, LANES), jnp.float32)
@@ -91,8 +122,6 @@
             return jnp.where(number + 1 < active, level(mixing, number + 1), 0.0)
         return zero
 
-    group = lane_index(ROWS) // 4
-    slabs = [zero] * (TAIL + 1)
     chains = [zero, zero]
     for step in range(half):
         for side, number in enumerate((step, depth - 1 - step)):
@@ -104,16 +133,7 @@
             solve[0, here, :] = inverse
             solve[1, here, :] = done * inverse
             solve[2, here, :] = chains[side]
-            for index, field in enumerate((temp, uvel, vvel, mask)):
-                block = level(field, number).astype(jnp.float32)
-                slab, start = slab_place(number, index)
-                moved = turn_lanes(block, start + 2)
-                slabs[slab] = jnp.where(group == start // 4, moved, slabs[slab])
     middle[...] = 1.0 / (1.0 - chains[0] * chains[1])
-    for number, slab in enumerate(slabs):
-        edges[number * ROWS : (number + 1) * ROWS, :] = slab
-        longer[number * ROWS : (number + 1) * ROWS, :] = slab
-    longer[(TAIL + 1) * ROWS :, :] = jnp.zeros((TILE, LANES), jnp.float32)
 
 
 def interior_kernel(
@@ -180,16 +200,16 @@
             target[level_rows(row, depth), :] = q + total
 
 
-def add_row_ghosts(prov, mine, ghost, near, odd_sign, mask, inv_dy, spread, flip):
-    depth = prov.shape[1] // ROWS
-    far = near + odd_sign
-    side = odd_sign.astype(jnp.float32)
+def add_row_ghosts(work, stride, near, base, mine, ghost, inner, mask, inv_dy, spread, flip):
+    depth = work.shape[1] // stride
+    far = near + inner
+    side = inner.astype(jnp.float32)
     wet = piece(mine, 6, depth)
     face = piece(ghost, 6, depth) * wet
-    face_next = wet * mask[level_rows(far, depth), :].astype(jnp.float32)
-    inv0 = inv_dy[pl.ds(near, 1), :]
-    inv1 = inv_dy[pl.ds(far, 1), :] * side
-    mix0 = spread[pl.ds(near, 1), :] * inv0 * inv0
+    face_next = wet * mask[level_rows(base + far, depth), :].astype(jnp.float32)
+    inv0 = inv_dy[pl.ds(base + near, 1), :]
+    inv1 = inv_dy[pl.ds(base + far, 1), :] * side
+    mix0 = spread[pl.ds(base + near, 1), :] * inv0 * inv0
     inv0 = inv0 * side
     speed = face * (piece(ghost, 4, depth) * flip + piece(mine, 4, depth)) * (1.0 / 24.0)
     speed_next = face_next * (piece(mine, 4, depth) + piece(mine, 5, depth)) * (1.0 / 24.0)
@@ -201,9 +221,10 @@
         o1 = piece(mine, 2 * number + 1, depth)
         advect = speed * (7.0 * (g0 + o0) - (g1 + o1))
         reach = speed_next * g0
-        view = prov.at[number]
-        view[level_rows(near, depth), :] += inv0 * (advect + reach) + mix0 * (face * (g0 - o0))
-        view[level_rows(far, depth), :] -= inv1 * reach
+        view = work.at[number]
+        at_near, at_far = (pl.ds(row, depth, stride=stride) for row in (near, far))
+        view[at_near, :] += inv0 * (advect + reach) + mix0 * (face * (g0 - o0))
+        view[at_far, :] -= inv1 * reach
 
 
 def column_ghosts(edges, other, west, inv_dx, spread):
@@ -222,7 +243,15 @@
     wide = wide * side.astype(jnp.float32)
     own = [level(edges, s) for s in range(TAIL + 1)]
     ghost = quad * side < jnp.where(west, 2, -1)
-    both = [jnp.where(ghost, level(other, s), own[s]) for s in range(TAIL + 1)]
+    lane = lane_index(ROWS)
+    place = 2 * (lane // 4) + lane % 2
+
+    def spread_out(x, offset):
+        return jnp.take_along_axis(x, place + offset, axis=1, mode="promise_in_bounds")
+
+    theirs = [spread_out(level(other, s // 2), 64 * (s % 2)) for s in range(TAIL)]
+    theirs.append(spread_out(level(other, 2), 0))
+    both = [jnp.where(ghost, theirs[s], own[s]) for s in range(TAIL + 1)]
     near_lane = quad == jnp.where(west, 2, 1)
 
     def split(slabs):
@@ -246,11 +275,6 @@
     return corrections
 
 
-def border_of(west):
-    lane = lane_index(ROWS)
-    return jnp.where(west, lane, LANES - 1 - lane) < 2
-
-
 def border_part(corrections, border, number, field):
     if number < 32:
         source, start = corrections[0][field], 4 * number
@@ -259,91 +283,97 @@
     return jnp.where(border, turn_lanes(source, -(start + 2)), 0.0)
 
 
-def ghosts_kernel(prov_in, sent1, got1, edges, other, mask, inv_dx, inv_dy, spread, prov):
+def ghosts_kernel(prov_in, edges, first, second, inv_dx, spread, prov):
     depth = prov.shape[1] // ROWS
-    odd = lax.rem(lax.axis_index("lat"), 2)
-    west = lax.rem(lax.axis_index("lon"), 2) == 1
-    corrections = column_ghosts(edges, other, west, inv_dx, spread)
-    border = border_of(west)
+    odd = lax.rem(lax.axis_index("lon"), 2) == 1
+    one = column_ghosts(edges, first, odd, inv_dx, spread)
+    two = column_ghosts(edges, second, jnp.logical_not(odd), inv_dx, spread)
+    lane = lane_index(ROWS)
+    from_first = lane % 4 // 2 == lax.rem(lax.axis_index("lon"), 2)
+    corrections = [
+        [jnp.where(from_first, a, b) for a, b in zip(part1, part2)] for part1, part2 in zip(one, two)
+    ]
+    border = (lane < 2) | (lane >= LANES - 2)
     for number in range(depth):
         here = slice(number * ROWS, (number + 1) * ROWS)
         for field in range(3):
             moved = border_part(corrections, border, number, field)
             prov[field, here, :] = prov_in[field, here, :] + moved
-    add_row_ghosts(prov, sent1, got1, (ROWS - 1) * (1 - odd), 2 * odd - 1, mask, inv_dy, spread, 1.0)
-
-
-def finish_kernel(
-    prov_in, solve, middle, mine, ghost, edges, other, mask, inv_dx, inv_dy, spread,
-    temp_new, uvel_new, vvel_new, prov, work, turned, sems
-):
+
+
+def half_kernel(partner, *refs):
+    prov, solve, middle, mine, ghost, mask, inv_dy, spread = refs[:8]
+    outs = refs[-6:-3]
+    work, turned, sems = refs[-3:]
     depth = prov.shape[1] // ROWS
     half = depth // 2
     odd = lax.rem(lax.axis_index("lat"), 2)
-    fold = lax.axis_index("lat") == lax.axis_size("lat") - 1
-    lane = lane_index(7 * depth)
-    lane = jnp.where(fold, LANES - 1 - lane, lane)
-    turned[...] = jnp.take_along_axis(ghost[: 7 * depth, :], lane, axis=1, mode="promise_in_bounds")
-    flip = jnp.where(fold, -1.0, 1.0)
-    add_row_ghosts(prov, mine, turned, (ROWS - 1) * odd, 1 - 2 * odd, mask, inv_dy, spread, flip)
-
-    west = lax.rem(lax.axis_index("lon"), 2) == 0
-    corrections = column_ghosts(edges, other, west, inv_dx, spread)
-    border = border_of(west)
-
-    outs = (temp_new, uvel_new, vvel_new)
-    zero = jnp.zeros((ROWS, LANES), jnp.float32)
+    north = odd if partner == 2 else 1 - odd
+    base = pl.multiple_of(north * TILE, TILE)
+    near = (TILE - 1) * north
+    inner = 1 - 2 * north
+    flip = 1.0
+    if partner == 2:
+        fold = lax.axis_index("lat") == lax.axis_size("lat") - 1
+        lane = lane_index(7 * depth)
+        lane = jnp.where(fold, LANES - 1 - lane, lane)
+        turned[...] = jnp.take_along_axis(ghost[: 7 * depth, :], lane, axis=1, mode="promise_in_bounds")
+        flip = jnp.where(fold, -1.0, 1.0)
+        ghost = turned
+
+    def rows_at(number):
+        return pl.ds(pl.multiple_of(number * ROWS + base, TILE), TILE)
+
+    def tile(number):
+        return slice(number * TILE, (number + 1) * TILE)
+
+    for number in range(depth):
+        for field in range(3):
+            work[field, tile(number), :] = prov[field, rows_at(number), :]
+    add_row_ghosts(work, TILE, near, base, mine, ghost, inner, mask, inv_dy, spread, flip)
+
+    zero = jnp.zeros((TILE, LANES), jnp.float32)
     values = [[zero] * 3, [zero] * 3]
     for step in range(half):
         for side, number in enumerate((step, depth - 1 - step)):
-            here = slice(number * ROWS, (number + 1) * ROWS)
-            inverse, carry = solve[0, here, :], solve[1, here, :]
+            inverse, carry = solve[0, rows_at(number), :], solve[1, rows_at(number), :]
             for field in range(3):
-                known = prov[field, here, :] + border_part(corrections, border, number, field)
-                value = inverse * known + carry * values[side][field]
+                value = inverse * work[field, tile(number), :] + carry * values[side][field]
                 values[side][field] = value
-                work[field, here, :] = value
+                work[field, tile(number), :] = value
     above, below = half - 1, half
-    gain = solve[2, above * ROWS : (above + 1) * ROWS, :]
-    scale = middle[...]
+    gain = solve[2, rows_at(above), :]
+    scale = middle[pl.ds(base, TILE), :]
+    tops = [scale * (values[0][field] + gain * values[1][field]) for field in range(3)]
     for field in range(3):
-        top = scale * (values[0][field] + gain * values[1][field])
-        values[1][field] = top
-        values[0][field] = None
-    tops = values[1]
-    for field in range(3):
-        work[field, above * ROWS : (above + 1) * ROWS, :] = tops[field]
+        work[field, tile(above), :] = tops[field]
     chains = [list(tops), list(tops)]
     copies = []
+
+    def store(start, stop):
+        for field in range(3):
+            source = work.at[field, pl.ds(start * TILE, (stop - start) * TILE), :]
+            target = outs[field].at[pl.ds(start, stop - start), pl.ds(base, TILE), :]
+            copy = pltpu.make_async_copy(
+                source.reshape(stop - start, TILE, LANES), target, sems.at[len(copies)]
+            )
+            copy.start()
+            copies.append(copy)
+
     for step in range(half):
         for side, number in enumerate((above - 1 - step, below + step)):
             if number < 0:
                 continue
-            here = slice(number * ROWS, (number + 1) * ROWS)
-            gain = solve[2, here, :]
+            gain = solve[2, rows_at(number), :]
             for field in range(3):
-                value = work[field, here, :] + gain * chains[side][field]
+                value = work[field, tile(number), :] + gain * chains[side][field]
                 chains[side][field] = value
-                work[field, here, :] = value
+                work[field, tile(number), :] = value
         if step == half // 2 - 1:
             low, high = above - 1 - step, below + step + 1
-            for field in range(3):
-                rows = pl.ds(low * ROWS, (high - low) * ROWS)
-                copies.append(
-                    pltpu.make_async_copy(
-                        work.at[field, rows, :], outs[field].at[rows, :], sems.at[field]
-                    )
-                )
-                copies[-1].start()
-    for field in range(3):
-        for part, (start, stop) in enumerate(((0, low), (high, depth))):
-            rows = pl.ds(start * ROWS, (stop - start) * ROWS)
-            copies.append(
-                pltpu.make_async_copy(
-                    work.at[field, rows, :], outs[field].at[rows, :], sems.at[3 + 2 * field + part]
-                )
-            )
-            copies[-1].start()
+            store(low, high)
+    store(0, low)
+    store(high, depth)
     for copy in copies:
         copy.wait()
 
@@ -401,32 +431,33 @@
     temp, uvel, vvel, vert_mixing, wet_mask = (
         x.reshape(flat, lanes) for x in (temp, uvel, vvel, vert_mixing, wet_mask)
     )
-    sent1 = pl.pallas_call(
-        rows_pack_kernel,
-        name="rows_pack",
-        out_shape=f32(7 * depth, lanes),
+    slab_rows = (TAIL + 1) * rows
+    sent1, zonal1, zonal2, edges = pl.pallas_call(
+        edges_pack_kernel,
+        name="edges_pack",
+        out_shape=(
+            f32(7 * depth, lanes),
+            f32(3 * rows, lanes),
+            f32(3 * rows + TILE, lanes),
+            f32(slab_rows, lanes),
+        ),
         in_specs=[VMEM] * 4 + [pl.BlockSpec(memory_space=pl.ANY)],
-        out_specs=VMEM,
+        out_specs=(VMEM,) * 4,
         compiler_params=limit,
         cost_estimate=cheap,
     )(temp, uvel, vvel, wet_mask, sent2)
     got1 = lax.ppermute(sent1, both, lat_first)
-    edges, longer, solve, middle = pl.pallas_call(
+    second = lax.ppermute(zonal2, both, lon_second)
+    first = lax.ppermute(zonal1, both, lon_first)
+    solve, middle = pl.pallas_call(
         columns_kernel,
         name="columns",
-        out_shape=(
-            f32((TAIL + 1) * rows, lanes),
-            f32((TAIL + 1) * rows + TILE, lanes),
-            f32(3, flat, lanes),
-            f32(rows, lanes),
-        ),
-        in_specs=[VMEM] * 6,
-        out_specs=(VMEM,) * 4,
+        out_shape=(f32(3, flat, lanes), f32(rows, lanes)),
+        in_specs=[VMEM] * 2,
+        out_specs=(VMEM,) * 2,
         compiler_params=limit,
         cost_estimate=cheap,
-    )(temp, uvel, vvel, wet_mask, vert_mixing, levels)
-    second = lax.ppermute(longer, both, lon_second)
-    first = lax.ppermute(edges, both, lon_first)
+    )(vert_mixing, levels)
     prov = pl.pallas_call(
         interior_kernel,
         name="interior",
@@ -440,28 +471,31 @@
         ghosts_kernel,
         name="ghosts",
         out_shape=f32(3, flat, lanes),
-        in_specs=[VMEM] * 9,
+        in_specs=[VMEM] * 6,
         out_specs=VMEM,
         input_output_aliases={0: 0},
         compiler_params=limit,
         cost_estimate=cheap,
-    )(prov, sent1, got1, edges, first, wet_mask, inv_dx, inv_dy, horiz_mixing)
-    outs = pl.pallas_call(
-        finish_kernel,
-        name="finish",
-        out_shape=(f32(flat, lanes),) * 3 + (f32(3, flat, lanes),),
-        in_specs=[VMEM] * 11,
-        out_specs=(HBM,) * 3 + (VMEM,),
-        input_output_aliases={0: 3},
-        scratch_shapes=[
-            vmem(3, flat, lanes),
-            vmem(7 * depth, lanes),
-            pltpu.SemaphoreType.DMA((9,)),
-        ],
-        compiler_params=limit,
-        cost_estimate=cheap,
-    )(prov, solve, middle, sent2, got2, edges, second, wet_mask, inv_dx, inv_dy, horiz_mixing)
-    return tuple(x.reshape(depth, rows, lanes) for x in outs[:3])
+    )(prov, edges, first, second, inv_dx, horiz_mixing)
+    outs = ()
+    for partner in ORDER:
+        mine, ghost = (sent1, got1) if partner == 1 else (sent2, got2)
+        outs = pl.pallas_call(
+            functools.partial(half_kernel, partner),
+            name="half" + str(partner),
+            out_shape=(f32(depth, rows, lanes),) * 3,
+            in_specs=[VMEM] * 8 + [HBM] * len(outs),
+            out_specs=(HBM,) * 3,
+            input_output_aliases={8 + i: i for i in range(len(outs))},
+            scratch_shapes=[
+                vmem(3, depth * TILE, lanes),
+                vmem(7 * depth, lanes),
+                pltpu.SemaphoreType.DMA((9,)),
+            ],
+            compiler_params=limit,
+            cost_estimate=cheap,
+        )(prov, solve, middle, mine, ghost, wet_mask, inv_dy, horiz_mixing, *outs)
+    return outs
 
 
 def solution(mesh):

time: 15.9 us -> 15.8 us (level)
  the two profiles are of different devices: /device:TPU:0 before, /device:TPU:1 now
where the time goes in v5:
time: 15.8 us; the launch traced here: 15.6 us
  Pallas kernels  7.25 us (46%)
  starting transfers between devices  6.95 us (44%)
  between operations  0.76 us (5%)
  local copies, waits for them, and re-layouts  0.64 us (4%)
    ppermute x1, starting transfers between devices, per_device(): got1 = lax.ppermute(sent1, both, lat_first)  3.11 us
    ppermute x1, starting transfers between devices, per_device(): second = lax.ppermute(zonal2, both, lon_second)  2.42 us
    pallas_call x1, Pallas kernels, per_device(): pl.pallas_call(interior_kernel, name='interior', out_shape=f32(3, flat, l...  2.2 us
    pallas_call x2, Pallas kernels, per_device(): pl.pallas_call(functools.partial(half_kernel, partner), name='half' + str...  2.19 us
    pallas_call x1, Pallas kernels, per_device(): pl.pallas_call(fold_pack_kernel, name='fold_pack', out_shape=f32(7 * dept...  1.3 us
    ppermute x1, starting transfers between devices, per_device(): first = lax.ppermute(zonal1, both, lon_first)  1.3 us
    pallas_call x1, Pallas kernels, per_device(): pl.pallas_call(ghosts_kernel, name='ghosts', out_shape=f32(3, flat, lanes...  0.78 us
    unnamed x20, local copies, waits for them, and re-layouts  0.64 us
  transfers between devices with their start and end apart: 4, of which 0 were waited for; matrix products, arithmetic and copies ran while one was open for 0% of the time, Pallas kernels for 31%

profile of v5, /device:TPU:1, one launch (start us, length us, event | category | flops | bytes accessed | tf_op | source)
XLA Modules:
  0.0 15.6 jit_solution(9463121767682118695)
XLA Ops:
  0.6 0.0 copy-start
  0.6 0.0 copy-start.3
  0.7 0.0 copy-start.2
  0.7 0.0 copy-start.1
  0.7 1.3 %fold_pack.1.after.refs_3_ = f32[288,128]{1,0:T(8,128)S(1)} custom-call(f32[40,16,128]{2,1,0:T(8,128)} %temp.1, f32[40,16,128]{2,1,0:T(8,128)} %uvel.1, f32[40,16,128]{2,1,0:T(8,128)} %vvel.1, s32[40,16,128]{2,1,0:T(8,128)} %mask.1), custom_call_target="tpu_custom_call" | custom-call | flops 1 | bytes 1 | tf_op jit(solution)/shard_map/fold_pack/pallas_call | solution.py:419
  2.0 0.1 collective-permute-start.3
  2.1 0.0 copy-done
  2.1 0.0 copy-done.3
  2.1 0.0 copy-done.2
  2.1 0.1 copy-done.1
  2.2 0.0 copy-start.4
  2.2 0.0 copy-start.9
  2.2 0.6 %edges_pack.1 = (f32[280,128]{1,0:T(8,128)S(1)}, f32[48,128]{1,0:T(8,128)S(1)}, f32[56,128]{1,0:T(8,128)S(1)}, f32[80,128]{1,0:T(8,128)S(1)}) custom-call(f32[640,128]{1,0:T(8,128)S(1)} %bitcast.9, f32[640,128]{1,0:T(8,128)S(1)} %bitcast.11, f32[640,128]{1,0:T(8,128)S(1)} %bitcast.13, s32[640,128]{1,0:T(8,128)S(1)} %bitcast.5, ...), custom_call_target="tpu_custom_call" | custom-call | flops 1 | bytes 1 | tf_op jit(solution)/shard_map/edges_pack/pallas_call | solution.py:435
  2.8 3.1 %collective-permute-start.2 = (f32[280,128]{1,0:T(8,128)S(1)}, f32[280,128]{1,0:T(8,128)S(1)}, u32[]{:S(2)}, u32[]{:S(2)}) collective-permute-start(f32[280,128]{1,0:T(8,128)S(1)} %get-tuple-element.17.refs_3_), channel_id=1, source_target_pairs={{0,8},{8,0},{1,9},{9,1},{2,10},{10,2},{3,11},{11,3},{4,12},{12,4},... | collective-permute-start | bytes 430088 | tf_op jit(solution)/shard_map/ppermute | solution.py:449
  5.9 2.4 %collective-permute-start.1 = (f32[56,128]{1,0:T(8,128)S(1)}, f32[56,128]{1,0:T(8,128)S(1)}, u32[]{:S(2)}, u32[]{:S(2)}) collective-permute-start(f32[56,128]{1,0:T(8,128)S(1)} %get-tuple-element.14), channel_id=1, source_target_pairs={{1,2},{2,1},{3,4},{4,3},{5,6},{6,5},{7,0},{0,7},{9,10},{10,9},{11,... | collective-permute-start | bytes 86024 | tf_op jit(solution)/shard_map/ppermute | solution.py:450
  8.3 1.3 %collective-permute-start = (f32[48,128]{1,0:T(8,128)S(1)}, f32[48,128]{1,0:T(8,128)S(1)}, u32[]{:S(2)}, u32[]{:S(2)}) collective-permute-start(f32[48,128]{1,0:T(8,128)S(1)} %get-tuple-element.13), channel_id=1, source_target_pairs={{0,1},{1,0},{2,3},{3,2},{4,5},{5,4},{6,7},{7,6},{8,9},{9,8},{10,11... | collective-permute-start | bytes 73736 | tf_op jit(solution)/shard_map/ppermute | solution.py:451
  9.6 0.0 copy-done.4
  9.6 0.0 copy-done.9
  9.6 0.0 copy-start.5
  9.6 0.0 copy-start.6
  9.6 0.0 copy-start.7
  9.7 0.0 copy-start.8
  9.7 0.2 %columns.1 = (f32[3,640,128]{2,1,0:T(8,128)S(1)}, f32[16,128]{1,0:T(8,128)S(1)}) custom-call(f32[640,128]{1,0:T(8,128)S(1)} %bitcast.15, s32[16,128]{1,0:T(8,128)S(1)} %copy-done.9), custom_call_target="tpu_custom_call" | custom-call | flops 1 | bytes 1 | tf_op jit(solution)/shard_map/columns/pallas_call | solution.py:452
  9.9 0.5 %copy-done.5 = f32[16,128]{1,0:T(8,128)S(1)} copy-done((f32[16,128]{1,0:T(8,128)S(1)}, f32[16,128]{1,0:T(8,128)}, u32[]{:S(2)}) %copy-start.5) | copy-done | bytes 8216
  10.3 0.0 copy-done.6
  10.3 0.0 copy-done.7
  10.4 0.0 copy-done.8
  10.4 2.2 %interior.1.prov_in = f32[3,640,128]{2,1,0:T(8,128)S(1)} custom-call(f32[640,128]{1,0:T(8,128)S(1)} %bitcast.10, f32[640,128]{1,0:T(8,128)S(1)} %bitcast.12, f32[640,128]{1,0:T(8,128)S(1)} %bitcast.14, s32[640,128]{1,0:T(8,128)S(1)} %bitcast.6, f32[16,128]{1,0:T(8,128)S(1)} %copy-done.7, f32[16,128]{1,0:T(8,128)S(1)} %copy-done.6, f32[16,128]{1,0:T(8,128)S(1)} %copy-done.5, ...), custom_call_target="tpu_custom_call" | custom-call | flops 1 | bytes 1 | tf_op jit(solution)/shard_map/interior/pallas_call | solution.py:461
  12.6 0.0 collective-permute-done.first
  12.6 0.0 collective-permute-done.1.second
  12.6 0.8 %ghosts.1.refs_0_ = f32[3,640,128]{2,1,0:T(8,128)S(1)} custom-call(f32[3,640,128]{2,1,0:T(8,128)S(1)} %interior.1.prov_in, f32[80,128]{1,0:T(8,128)S(1)} %get-tuple-element.12.edges, f32[48,128]{1,0:T(8,128)S(1)} %collective-permute-done.first, f32[56,128]{1,0:T(8,128)S(1)} %collective-permute-done.1.second, ...), custom_call_target="tpu_custom_call", output_to_operand_aliasing={{}: (0, {})} | custom-call | flops 1 | bytes 1 | tf_op jit(solution)/shard_map/ghosts/pallas_call | solution.py:470
  13.4 0.0 collective-permute-done.3.refs_4_
  13.4 1.1 %half2.1 = (f32[40,16,128]{2,1,0:T(8,128)}, f32[40,16,128]{2,1,0:T(8,128)}, f32[40,16,128]{2,1,0:T(8,128)}) custom-call(f32[3,640,128]{2,1,0:T(8,128)S(1)} %ghosts.1.refs_0_, f32[3,640,128]{2,1,0:T(8,128)S(1)} %get-tuple-element.15.refs_1_, f32[16,128]{1,0:T(8,128)S(1)} %get-tuple-element.16.refs_2_, f32[288,128]{1,0:T(8,128)S(1)} %fold_pack.1.after.refs_3_, ...), custom_call_target="tpu_custom_call" | custom-call | flops 1 | bytes 1 | tf_op jit(solution)/shard_map/half2/pallas_call | solution.py:483
  14.5 0.0 collective-permute-done.2.refs_4_
  14.5 1.1 %half1.1 = (f32[40,16,128]{2,1,0:T(8,128)}, f32[40,16,128]{2,1,0:T(8,128)}, f32[40,16,128]{2,1,0:T(8,128)}) custom-call(f32[3,640,128]{2,1,0:T(8,128)S(1)} %ghosts.1.refs_0_, f32[3,640,128]{2,1,0:T(8,128)S(1)} %get-tuple-element.15.refs_1_, f32[16,128]{1,0:T(8,128)S(1)} %get-tuple-element.16.refs_2_, ...), custom_call_target="tpu_custom_call", output_to_operand_aliasing={{0}: (8, {}), {1}: (9, {}), {2}: (10, {})} | custom-call | flops 1 | bytes 1 | tf_op jit(solution)/shard_map/half1/pallas_call | solution.py:483
Async XLA Ops:
  0.6 1.5 %copy-start = (s32[40,16,128]{2,1,0:T(8,128)S(1)}, s32[40,16,128]{2,1,0:T(8,128)}, u32[]{:S(2)}) copy-start(s32[40,16,128]{2,1,0:T(8,128)} %mask.1) | copy-start | bytes 983044
  0.6 1.5 %copy-start.3 = (f32[40,16,128]{2,1,0:T(8,128)S(1)}, f32[40,16,128]{2,1,0:T(8,128)}, u32[]{:S(2)}) copy-start(f32[40,16,128]{2,1,0:T(8,128)} %vvel.1) | copy-start | bytes 983044
  0.7 1.5 %copy-start.2 = (f32[40,16,128]{2,1,0:T(8,128)S(1)}, f32[40,16,128]{2,1,0:T(8,128)}, u32[]{:S(2)}) copy-start(f32[40,16,128]{2,1,0:T(8,128)} %uvel.1) | copy-start | bytes 983044
  0.7 1.6 %copy-start.1 = (f32[40,16,128]{2,1,0:T(8,128)S(1)}, f32[40,16,128]{2,1,0:T(8,128)}, u32[]{:S(2)}) copy-start(f32[40,16,128]{2,1,0:T(8,128)} %temp.1) | copy-start | bytes 983044
  2.0 11.4 %collective-permute-start.3 = (f32[288,128]{1,0:T(8,128)S(1)}, f32[288,128]{1,0:T(8,128)S(1)}, u32[]{:S(2)}, u32[]{:S(2)}) collective-permute-start(f32[288,128]{1,0:T(8,128)S(1)} %fold_pack.1.after.refs_3_), channel_id=1, source_target_pairs={{8,16},{16,8},{9,17},{17,9},{10,18},{18,10},{11,19},{19,11},{12,20... | collective-permute-start | bytes 442376 | tf_op jit(solution)/shard_map/ppermute | solution.py:430
  2.2 7.4 %copy-start.4 = (f32[40,16,128]{2,1,0:T(8,128)S(1)}, f32[40,16,128]{2,1,0:T(8,128)}, u32[]{:S(2)}) copy-start(f32[40,16,128]{2,1,0:T(8,128)} %param.13) | copy-start | bytes 983044
  2.2 7.4 %copy-start.9 = (s32[16,128]{1,0:T(8,128)S(1)}, s32[16,128]{1,0:T(8,128)}, u32[]{:S(2)}) copy-start(s32[16,128]{1,0:T(8,128)} %levels.1) | copy-start | bytes 24580
  2.8 11.7 %collective-permute-start.2 = (f32[280,128]{1,0:T(8,128)S(1)}, f32[280,128]{1,0:T(8,128)S(1)}, u32[]{:S(2)}, u32[]{:S(2)}) collective-permute-start(f32[280,128]{1,0:T(8,128)S(1)} %get-tuple-element.17.refs_3_), channel_id=1, source_target_pairs={{0,8},{8,0},{1,9},{9,1},{2,10},{10,2},{3,11},{11,3},{4,12},{12,4},... | collective-permute-start | bytes 430088 | tf_op jit(solution)/shard_map/ppermute | solution.py:449
  5.9 6.7 %collective-permute-start.1 = (f32[56,128]{1,0:T(8,128)S(1)}, f32[56,128]{1,0:T(8,128)S(1)}, u32[]{:S(2)}, u32[]{:S(2)}) collective-permute-start(f32[56,128]{1,0:T(8,128)S(1)} %get-tuple-element.14), channel_id=1, source_target_pairs={{1,2},{2,1},{3,4},{4,3},{5,6},{6,5},{7,0},{0,7},{9,10},{10,9},{11,... | collective-permute-start | bytes 86024 | tf_op jit(solution)/shard_map/ppermute | solution.py:450
  8.3 4.3 %collective-permute-start = (f32[48,128]{1,0:T(8,128)S(1)}, f32[48,128]{1,0:T(8,128)S(1)}, u32[]{:S(2)}, u32[]{:S(2)}) collective-permute-start(f32[48,128]{1,0:T(8,128)S(1)} %get-tuple-element.13), channel_id=1, source_target_pairs={{0,1},{1,0},{2,3},{3,2},{4,5},{5,4},{6,7},{7,6},{8,9},{9,8},{10,11... | collective-permute-start | bytes 73736 | tf_op jit(solution)/shard_map/ppermute | solution.py:451
  9.6 0.7 %copy-start.5 = (f32[16,128]{1,0:T(8,128)S(1)}, f32[16,128]{1,0:T(8,128)}, u32[]{:S(2)}) copy-start(f32[16,128]{1,0:T(8,128)} %refs_7_.3) | copy-start | bytes 24580
  9.6 0.7 %copy-start.6 = (f32[16,128]{1,0:T(8,128)S(1)}, f32[16,128]{1,0:T(8,128)}, u32[]{:S(2)}) copy-start(f32[16,128]{1,0:T(8,128)} %refs_6_.3) | copy-start | bytes 24580
  9.6 0.7 %copy-start.7 = (f32[16,128]{1,0:T(8,128)S(1)}, f32[16,128]{1,0:T(8,128)}, u32[]{:S(2)}) copy-start(f32[16,128]{1,0:T(8,128)} %inv_dx.3) | copy-start | bytes 24580
  9.7 0.7 %copy-start.8 = (f32[16,128]{1,0:T(8,128)S(1)}, f32[16,128]{1,0:T(8,128)}, u32[]{:S(2)}) copy-start(f32[16,128]{1,0:T(8,128)} %coriolis.1) | copy-start | bytes 24580

commit v6 on v5

--- a/solution.py
+++ b/solution.py
@@ -1,5 +1,3 @@
-import functools
-
 import jax
 import jax.numpy as jnp
 from jax import lax
@@ -11,7 +9,7 @@
 LANES = 128
 TILE = 8
 TAIL = 4
-ORDER = (2, 1)
+STORE_AFTER = (4, 11, 19)
 VMEM = pl.BlockSpec(memory_space=pltpu.VMEM)
 HBM = pl.BlockSpec(memory_space=pltpu.HBM)
 
@@ -42,33 +40,43 @@
     return TAIL, 32 * field + 4 * (number - 32)
 
 
-def fold_pack_kernel(temp, uvel, vvel, mask, out, half0, half1, half2, halfm, sems):
+def sends_north(exchange):
+    return jnp.where(lax.rem(lax.axis_index("lat"), 3) == exchange, 1, 0)
+
+
+def first_rows_kernel(
+    temp, uvel, vvel, mask, dx_in, dy_in, spread_in, turn_in, levels_in,
+    out, dx, dy, spread, turn, levels, half0, half1, half2, halfm, sems
+):
     depth = temp.shape[0]
-    odd = lax.rem(lax.axis_index("lat"), 2)
+    north = sends_north(0)
     copies = []
-    for number, (field, half) in enumerate(
-        zip((temp, uvel, vvel, mask), (half0, half1, half2, halfm))
-    ):
+    for field, half in ((temp, half0), (uvel, half1), (vvel, half2), (mask, halfm)):
         copies.append(
             pltpu.make_async_copy(
-                field.at[:, pl.ds(pl.multiple_of(odd * TILE, TILE), TILE), :],
+                field.at[:, pl.ds(pl.multiple_of(north * TILE, TILE), TILE), :],
                 half.reshape(depth, TILE, LANES),
-                sems.at[number],
+                sems.at[len(copies)],
             )
         )
+    for plane, target in (
+        (dx_in, dx), (dy_in, dy), (spread_in, spread), (turn_in, turn), (levels_in, levels)
+    ):
+        copies.append(pltpu.make_async_copy(plane, target, sems.at[len(copies)]))
     for copy in copies:
         copy.start()
-    near = (TILE - 1) * odd
-    far = near + 1 - 2 * odd
-    keep = jnp.where(lax.axis_index("lat") == 0, 0.0, 1.0)
+    near = (TILE - 1) * north
+    far = near + 1 - 2 * north
+    out[7 * depth :, :] = jnp.zeros((2 * TILE, LANES), jnp.float32)
     for number, half in enumerate((half0, half1, half2)):
         copies[number].wait()
         base = 2 * depth * number
-        out[base : base + depth, :] = half[pl.ds(near, depth, stride=TILE), :] * keep
-        out[base + depth : base + 2 * depth, :] = half[pl.ds(far, depth, stride=TILE), :] * keep
+        out[base : base + depth, :] = half[pl.ds(near, depth, stride=TILE), :]
+        out[base + depth : base + 2 * depth, :] = half[pl.ds(far, depth, stride=TILE), :]
     copies[3].wait()
-    out[6 * depth : 7 * depth, :] = halfm[pl.ds(near, depth, stride=TILE), :].astype(jnp.float32) * keep
-    out[7 * depth :, :] = jnp.zeros((TILE, LANES), jnp.float32)
+    out[6 * depth : 7 * depth, :] = halfm[pl.ds(near, depth, stride=TILE), :].astype(jnp.float32)
+    for copy in copies[4:]:
+        copy.wait()
 
 
 def own_slabs(fields, depth):
@@ -82,16 +90,18 @@
     return slabs
 
 
-def edges_pack_kernel(temp, uvel, vvel, mask, after, first, zonal1, zonal2, edges):
+def edges_pack_kernel(temp, uvel, vvel, mask, after, second, third, zonal1, zonal2, edges):
     depth = temp.shape[0] // ROWS
-    odd = lax.rem(lax.axis_index("lat"), 2)
-    near = (ROWS - 1) * (1 - odd)
-    far = near + 2 * odd - 1
-    for number, field in enumerate((temp, uvel, vvel)):
-        base = 2 * depth * number
-        first[base : base + depth, :] = field[level_rows(near, depth), :]
-        first[base + depth : base + 2 * depth, :] = field[level_rows(far, depth), :]
-    first[6 * depth : 7 * depth, :] = mask[level_rows(near, depth), :].astype(jnp.float32)
+    for exchange, out in ((1, second), (2, third)):
+        north = sends_north(exchange)
+        near = (ROWS - 1) * north
+        far = near + 1 - 2 * north
+        for number, field in enumerate((temp, uvel, vvel)):
+            base = 2 * depth * number
+            out[base : base + depth, :] = field[level_rows(near, depth), :]
+            out[base + depth : base + 2 * depth, :] = field[level_rows(far, depth), :]
+        out[6 * depth : 7 * depth, :] = mask[level_rows(near, depth), :].astype(jnp.float32)
+    second[7 * depth :, :] = jnp.zeros((TILE, LANES), jnp.float32)
     slabs = own_slabs((temp, uvel, vvel, mask), depth)
     for number, slab in enumerate(slabs):
         edges[number * ROWS : (number + 1) * ROWS, :] = slab
@@ -200,29 +210,29 @@
             target[level_rows(row, depth), :] = q + total
 
 
-def add_row_ghosts(work, stride, near, base, mine, ghost, inner, mask, inv_dy, spread, flip):
-    depth = work.shape[1] // stride
-    far = near + inner
-    side = inner.astype(jnp.float32)
-    wet = piece(mine, 6, depth)
+def add_row_ghosts(prov, fields, mask, ghost, near, inv_dy, spread, flip):
+    depth = prov.shape[1] // ROWS
+    far, side = (1, 1.0) if near == 0 else (near - 1, -1.0)
+    at_near, at_far = level_rows(near, depth), level_rows(far, depth)
+    wet = mask[at_near, :].astype(jnp.float32)
     face = piece(ghost, 6, depth) * wet
-    face_next = wet * mask[level_rows(base + far, depth), :].astype(jnp.float32)
-    inv0 = inv_dy[pl.ds(base + near, 1), :]
-    inv1 = inv_dy[pl.ds(base + far, 1), :] * side
-    mix0 = spread[pl.ds(base + near, 1), :] * inv0 * inv0
+    face_next = wet * mask[at_far, :].astype(jnp.float32)
+    inv0 = inv_dy[near : near + 1, :]
+    inv1 = inv_dy[far : far + 1, :] * side
+    mix0 = spread[near : near + 1, :] * inv0 * inv0
     inv0 = inv0 * side
-    speed = face * (piece(ghost, 4, depth) * flip + piece(mine, 4, depth)) * (1.0 / 24.0)
-    speed_next = face_next * (piece(mine, 4, depth) + piece(mine, 5, depth)) * (1.0 / 24.0)
+    v0 = fields[2][at_near, :]
+    speed = face * (piece(ghost, 4, depth) * flip + v0) * (1.0 / 24.0)
+    speed_next = face_next * (v0 + fields[2][at_far, :]) * (1.0 / 24.0)
     for number in range(3):
         sign = 1.0 if number == 0 else flip
         g0 = piece(ghost, 2 * number, depth) * sign
         g1 = piece(ghost, 2 * number + 1, depth) * sign
-        o0 = piece(mine, 2 * number, depth)
-        o1 = piece(mine, 2 * number + 1, depth)
+        o0 = fields[number][at_near, :]
+        o1 = fields[number][at_far, :]
         advect = speed * (7.0 * (g0 + o0) - (g1 + o1))
         reach = speed_next * g0
-        view = work.at[number]
-        at_near, at_far = (pl.ds(row, depth, stride=stride) for row in (near, far))
+        view = prov.at[number]
         view[at_near, :] += inv0 * (advect + reach) + mix0 * (face * (g0 - o0))
         view[at_far, :] -= inv1 * reach
 
@@ -283,97 +293,101 @@
     return jnp.where(border, turn_lanes(source, -(start + 2)), 0.0)
 
 
-def ghosts_kernel(prov_in, edges, first, second, inv_dx, spread, prov):
-    depth = prov.shape[1] // ROWS
+def first_columns_kernel(edges, first, inv_dx, spread, out):
     odd = lax.rem(lax.axis_index("lon"), 2) == 1
-    one = column_ghosts(edges, first, odd, inv_dx, spread)
-    two = column_ghosts(edges, second, jnp.logical_not(odd), inv_dx, spread)
-    lane = lane_index(ROWS)
-    from_first = lane % 4 // 2 == lax.rem(lax.axis_index("lon"), 2)
-    corrections = [
-        [jnp.where(from_first, a, b) for a, b in zip(part1, part2)] for part1, part2 in zip(one, two)
-    ]
-    border = (lane < 2) | (lane >= LANES - 2)
-    for number in range(depth):
-        here = slice(number * ROWS, (number + 1) * ROWS)
+    for part, slabs in enumerate(column_ghosts(edges, first, odd, inv_dx, spread)):
         for field in range(3):
-            moved = border_part(corrections, border, number, field)
-            prov[field, here, :] = prov_in[field, here, :] + moved
-
-
-def half_kernel(partner, *refs):
-    prov, solve, middle, mine, ghost, mask, inv_dy, spread = refs[:8]
-    outs = refs[-6:-3]
-    work, turned, sems = refs[-3:]
+            place = (3 * part + field) * ROWS
+            out[place : place + ROWS, :] = slabs[field]
+
+
+def finish_kernel(
+    prov_in, solve, middle, temp, uvel, vvel, mask, got0, got1, got2, edges, packed, second,
+    inv_dx, inv_dy, spread, temp_new, uvel_new, vvel_new, prov, work, south, north, sems
+):
     depth = prov.shape[1] // ROWS
     half = depth // 2
-    odd = lax.rem(lax.axis_index("lat"), 2)
-    north = odd if partner == 2 else 1 - odd
-    base = pl.multiple_of(north * TILE, TILE)
-    near = (TILE - 1) * north
-    inner = 1 - 2 * north
-    flip = 1.0
-    if partner == 2:
-        fold = lax.axis_index("lat") == lax.axis_size("lat") - 1
-        lane = lane_index(7 * depth)
-        lane = jnp.where(fold, LANES - 1 - lane, lane)
-        turned[...] = jnp.take_along_axis(ghost[: 7 * depth, :], lane, axis=1, mode="promise_in_bounds")
-        flip = jnp.where(fold, -1.0, 1.0)
-        ghost = turned
-
-    def rows_at(number):
-        return pl.ds(pl.multiple_of(number * ROWS + base, TILE), TILE)
-
-    def tile(number):
-        return slice(number * TILE, (number + 1) * TILE)
-
-    for number in range(depth):
-        for field in range(3):
-            work[field, tile(number), :] = prov[field, rows_at(number), :]
-    add_row_ghosts(work, TILE, near, base, mine, ghost, inner, mask, inv_dy, spread, flip)
-
-    zero = jnp.zeros((TILE, LANES), jnp.float32)
+    used = slice(0, 7 * depth)
+    lat = lax.axis_index("lat")
+    fold = lat == lax.axis_size("lat") - 1
+
+    def received(exchange):
+        return jnp.where(
+            exchange == 0, got0[used, :], jnp.where(exchange == 1, got1[used, :], got2[used, :])
+        )
+
+    lane = lane_index(7 * depth)
+    lane = jnp.where(fold, LANES - 1 - lane, lane)
+    north[...] = jnp.take_along_axis(received(lax.rem(lat, 3)), lane, axis=1, mode="promise_in_bounds")
+    south[...] = jnp.where(lat == 0, 0.0, received(lax.rem(lat + 2, 3)))
+    flip = jnp.where(fold, -1.0, 1.0)
+    fields = (temp, uvel, vvel)
+    add_row_ghosts(prov, fields, mask, south, 0, inv_dy, spread, 1.0)
+    add_row_ghosts(prov, fields, mask, north, ROWS - 1, inv_dy, spread, flip)
+
+    odd = lax.rem(lax.axis_index("lon"), 2)
+    lane = lane_index(ROWS)
+    from_first = lane % 4 // 2 == odd
+    corrections = []
+    for part, slabs in enumerate(column_ghosts(edges, second, odd == 0, inv_dx, spread)):
+        corrections.append(
+            [jnp.where(from_first, level(packed, 3 * part + f), slabs[f]) for f in range(3)]
+        )
+    border = (lane < 2) | (lane >= LANES - 2)
+
+    def border_part(number, field):
+        part, start = (0, 4 * number) if number < 32 else (1, 4 * (number - 32))
+        return jnp.where(border, turn_lanes(corrections[part][field], -(start + 2)), 0.0)
+
+    outs = (temp_new, uvel_new, vvel_new)
+    zero = jnp.zeros((ROWS, LANES), jnp.float32)
     values = [[zero] * 3, [zero] * 3]
     for step in range(half):
         for side, number in enumerate((step, depth - 1 - step)):
-            inverse, carry = solve[0, rows_at(number), :], solve[1, rows_at(number), :]
+            here = slice(number * ROWS, (number + 1) * ROWS)
+            inverse, carry = solve[0, here, :], solve[1, here, :]
             for field in range(3):
-                value = inverse * work[field, tile(number), :] + carry * values[side][field]
+                known = prov[field, here, :] + border_part(number, field)
+                value = inverse * known + carry * values[side][field]
                 values[side][field] = value
-                work[field, tile(number), :] = value
+                work[field, here, :] = value
     above, below = half - 1, half
-    gain = solve[2, rows_at(above), :]
-    scale = middle[pl.ds(base, TILE), :]
+    gain = level(solve.at[2], above)
+    scale = middle[...]
     tops = [scale * (values[0][field] + gain * values[1][field]) for field in range(3)]
     for field in range(3):
-        work[field, tile(above), :] = tops[field]
+        work[field, above * ROWS : (above + 1) * ROWS, :] = tops[field]
     chains = [list(tops), list(tops)]
     copies = []
 
     def store(start, stop):
+        rows = pl.ds(start * ROWS, (stop - start) * ROWS)
         for field in range(3):
-            source = work.at[field, pl.ds(start * TILE, (stop - start) * TILE), :]
-            target = outs[field].at[pl.ds(start, stop - start), pl.ds(base, TILE), :]
             copy = pltpu.make_async_copy(
-                source.reshape(stop - start, TILE, LANES), target, sems.at[len(copies)]
+                work.at[field, rows, :], outs[field].at[rows, :], sems.at[len(copies)]
             )
             copy.start()
             copies.append(copy)
 
+    low, high = half, half
     for step in range(half):
         for side, number in enumerate((above - 1 - step, below + step)):
             if number < 0:
                 continue
-            gain = solve[2, rows_at(number), :]
+            here = slice(number * ROWS, (number + 1) * ROWS)
+            gain = solve[2, here, :]
             for field in range(3):
-                value = work[field, tile(number), :] + gain * chains[side][field]
+                value = work[field, here, :] + gain * chains[side][field]
                 chains[side][field] = value
-                work[field, tile(number), :] = value
-        if step == half // 2 - 1:
-            low, high = above - 1 - step, below + step + 1
-            store(low, high)
-    store(0, low)
-    store(high, depth)
+                work[field, here, :] = value
+        if step in STORE_AFTER:
+            start, stop = max(above - 1 - step, 0), below + step + 1
+            if low == high:
+                store(start, stop)
+            else:
+                store(start, low)
+                store(high, stop)
+            low, high = start, stop
     for copy in copies:
         copy.wait()
 
@@ -386,14 +400,20 @@
     def at(lat, lon):
         return lat * lons + lon % lons
 
-    every = range(lons)
     lon_first = [(at(l, c), at(l, c + 1)) for l in range(lats) for c in range(0, lons, 2)]
     lon_second = [(at(l, c), at(l, c + 1)) for l in range(lats) for c in range(1, lons, 2)]
-    lat_first = [(at(l, c), at(l + 1, c)) for l in range(0, lats, 2) for c in every]
-    lat_second = [(at(l, c), at(l + 1, c)) for l in range(1, lats - 1, 2) for c in every]
-    lat_second += [(at(lats - 1, c), at(lats - 1, lons - 1 - c)) for c in range(lons // 2)]
-    lat_second += [(at(0, c), at(0, c + 1)) for c in range(0, lons, 2)]
-    return [swaps(pairs) for pairs in (lon_first, lon_second, lat_first, lat_second)]
+    routes = [swaps(lon_first), swaps(lon_second)]
+    for exchange in range(3):
+        pairs, idle = [], set(range(lats))
+        for l in range(exchange, lats, 3):
+            if l == lats - 1:
+                pairs += [(at(l, c), at(l, lons - 1 - c)) for c in range(lons // 2)]
+            else:
+                pairs += [(at(l, c), at(l + 1, c)) for c in range(lons)]
+            idle -= {l, l + 1}
+        pairs += [(at(l, c), at(l, c + 1)) for l in sorted(idle) for c in range(0, lons, 2)]
+        routes.append(swaps(pairs))
+    return routes
 
 
 def per_device(
@@ -402,7 +422,7 @@
     depth, rows, lanes = temp.shape
     assert (rows, lanes) == (ROWS, LANES) and depth == 40
     lats, lons = lax.axis_size("lat"), lax.axis_size("lon")
-    assert lats % 2 == 0 and lons % 2 == 0
+    assert lons % 2 == 0
     flat = depth * rows
 
     def f32(*shape):
@@ -414,41 +434,45 @@
     limit = pltpu.CompilerParams(vmem_limit_bytes=16 << 20)
     cheap = pl.CostEstimate(flops=1, bytes_accessed=1, transcendentals=0)
     both = ("lat", "lon")
-    lon_first, lon_second, lat_first, lat_second = exchange_routes(lats, lons)
-    inputs = [pltpu.with_memory_space_constraint(x, pltpu.HBM) for x in (temp, uvel, vvel, wet_mask)]
-    sent2 = pl.pallas_call(
-        fold_pack_kernel,
-        name="fold_pack",
-        out_shape=f32(7 * depth + TILE, lanes),
-        in_specs=[HBM] * 4,
-        out_specs=VMEM,
+    zonal_first, zonal_second, *meridional = exchange_routes(lats, lons)
+    arrays = (temp, uvel, vvel, wet_mask, inv_dx, inv_dy, horiz_mixing, coriolis, levels)
+    arrays = [pltpu.with_memory_space_constraint(x, pltpu.HBM) for x in arrays]
+    sent0, inv_dx, inv_dy, horiz_mixing, coriolis, levels = pl.pallas_call(
+        first_rows_kernel,
+        name="first_rows",
+        out_shape=(f32(7 * depth + 2 * TILE, lanes),)
+        + (f32(rows, lanes),) * 4
+        + (jax.ShapeDtypeStruct((rows, lanes), jnp.int32),),
+        in_specs=[HBM] * 9,
+        out_specs=(VMEM,) * 6,
         scratch_shapes=[vmem(depth * TILE, lanes)] * 3
-        + [vmem(depth * TILE, lanes, dtype=jnp.int32), pltpu.SemaphoreType.DMA((4,))],
+        + [vmem(depth * TILE, lanes, dtype=jnp.int32), pltpu.SemaphoreType.DMA((9,))],
         compiler_params=limit,
         cost_estimate=cheap,
-    )(*inputs)
-    got2 = lax.ppermute(sent2, both, lat_second)
+    )(*arrays)
+    got0 = lax.ppermute(sent0, both, meridional[0])
     temp, uvel, vvel, vert_mixing, wet_mask = (
         x.reshape(flat, lanes) for x in (temp, uvel, vvel, vert_mixing, wet_mask)
     )
-    slab_rows = (TAIL + 1) * rows
-    sent1, zonal1, zonal2, edges = pl.pallas_call(
+    sent1, sent2, zonal1, zonal2, edges = pl.pallas_call(
         edges_pack_kernel,
         name="edges_pack",
         out_shape=(
+            f32(7 * depth + TILE, lanes),
             f32(7 * depth, lanes),
             f32(3 * rows, lanes),
             f32(3 * rows + TILE, lanes),
-            f32(slab_rows, lanes),
+            f32((TAIL + 1) * rows, lanes),
         ),
         in_specs=[VMEM] * 4 + [pl.BlockSpec(memory_space=pl.ANY)],
-        out_specs=(VMEM,) * 4,
+        out_specs=(VMEM,) * 5,
         compiler_params=limit,
         cost_estimate=cheap,
-    )(temp, uvel, vvel, wet_mask, sent2)
-    got1 = lax.ppermute(sent1, both, lat_first)
-    second = lax.ppermute(zonal2, both, lon_second)
-    first = lax.ppermute(zonal1, both, lon_first)
+    )(temp, uvel, vvel, wet_mask, sent0)
+    got1 = lax.ppermute(sent1, both, meridional[1])
+    got2 = lax.ppermute(sent2, both, meridional[2])
+    second = lax.ppermute(zonal2, both, zonal_second)
+    first = lax.ppermute(zonal1, both, zonal_first)
     solve, middle = pl.pallas_call(
         columns_kernel,
         name="columns",
@@ -467,35 +491,35 @@
         compiler_params=limit,
         cost_estimate=cheap,
     )(temp, uvel, vvel, wet_mask, inv_dx, inv_dy, horiz_mixing, coriolis)
-    prov = pl.pallas_call(
-        ghosts_kernel,
-        name="ghosts",
-        out_shape=f32(3, flat, lanes),
-        in_specs=[VMEM] * 6,
+    packed = pl.pallas_call(
+        first_columns_kernel,
+        name="first_columns",
+        out_shape=f32(6 * rows, lanes),
+        in_specs=[VMEM] * 4,
         out_specs=VMEM,
-        input_output_aliases={0: 0},
         compiler_params=limit,
         cost_estimate=cheap,
-    )(prov, edges, first, second, inv_dx, horiz_mixing)
-    outs = ()
-    for partner in ORDER:
-        mine, ghost = (sent1, got1) if partner == 1 else (sent2, got2)
-        outs = pl.pallas_call(
-            functools.partial(half_kernel, partner),
-            name="half" + str(partner),
-            out_shape=(f32(depth, rows, lanes),) * 3,
-            in_specs=[VMEM] * 8 + [HBM] * len(outs),
-            out_specs=(HBM,) * 3,
-            input_output_aliases={8 + i: i for i in range(len(outs))},
-            scratch_shapes=[
-                vmem(3, depth * TILE, lanes),
-                vmem(7 * depth, lanes),
-                pltpu.SemaphoreType.DMA((9,)),
-            ],
-            compiler_params=limit,
-            cost_estimate=cheap,
-        )(prov, solve, middle, mine, ghost, wet_mask, inv_dy, horiz_mixing, *outs)
-    return outs
+    )(edges, first, inv_dx, horiz_mixing)
+    outs = pl.pallas_call(
+        finish_kernel,
+        name="finish",
+        out_shape=(f32(flat, lanes),) * 3 + (f32(3, flat, lanes),),
+        in_specs=[VMEM] * 16,
+        out_specs=(HBM,) * 3 + (VMEM,),
+        input_output_aliases={0: 3},
+        scratch_shapes=[
+            vmem(3, flat, lanes),
+            vmem(7 * depth, lanes),
+            vmem(7 * depth, lanes),
+            pltpu.SemaphoreType.DMA((15,)),
+        ],
+        compiler_params=limit,
+        cost_estimate=cheap,
+    )(
+        prov, solve, middle, temp, uvel, vvel, wet_mask, got0, got1, got2, edges, packed, second,
+        inv_dx, inv_dy, horiz_mixing,
+    )
+    return tuple(x.reshape(depth, rows, lanes) for x in outs[:3])
 
 
 def solution(mesh):

time: 15.8 us -> 15.1 us (0.956)
  the two profiles are of different devices: /device:TPU:1 before, /device:TPU:4 now
where the time goes in v6:
time: 15.1 us; the launch traced here: 15 us
  Pallas kernels  6.93 us (46%)
  starting transfers between devices  5.2 us (34%)
  waiting for transfers between devices  2 us (13%)
  between operations  0.74 us (5%)
    ppermute x1, starting transfers between devices, per_device(): got2 = lax.ppermute(sent2, both, meridional[2])  3.68 us
    pallas_call x1, Pallas kernels, per_device(): pl.pallas_call(interior_kernel, name='interior', out_shape=f32(3, flat, l...  2.49 us
    ppermute x1, waiting for transfers between devices, per_device(): second = lax.ppermute(zonal2, both, zonal_second)  1.99 us
    pallas_call x1, Pallas kernels, per_device(): pl.pallas_call(finish_kernel, name='finish', out_shape=(f32(flat, lanes),...  1.91 us
    ppermute x1, starting transfers between devices, per_device(): got1 = lax.ppermute(sent1, both, meridional[1])  1.44 us
    pallas_call x1, Pallas kernels, per_device(): pl.pallas_call(first_rows_kernel, name='first_rows', out_shape=(f32(7 * d...  1.36 us
    pallas_call x1, Pallas kernels, per_device(): pl.pallas_call(edges_pack_kernel, name='edges_pack', out_shape=(f32(7 * d...  0.59 us
    pallas_call x1, Pallas kernels, per_device(): pl.pallas_call(first_columns_kernel, name='first_columns', out_shape=f32(...  0.38 us
  transfers between devices with their start and end apart: 5, of which 1 were waited for; matrix products, arithmetic and copies ran while one was open for 0% of the time, Pallas kernels for 24%

profile of v6, /device:TPU:4, one launch (start us, length us, event | category | flops | bytes accessed | tf_op | source)
XLA Modules:
  0.0 15.0 jit_solution(3751147082573914839)
XLA Ops:
  0.6 0.0 copy-start.3
  0.6 0.0 copy-start.2
  0.7 0.0 copy-start.1
  0.7 0.0 copy-start
  0.7 1.4 %first_rows.1 = (f32[296,128]{1,0:T(8,128)S(1)}, f32[16,128]{1,0:T(8,128)S(1)}, f32[16,128]{1,0:T(8,128)S(1)}, f32[16,128]{1,0:T(8,128)S(1)}, f32[16,128]{1,0:T(8,128)S(1)}, /*index=5*/s32[16,128]{1,0:T(8,128)S(1)}) custom-call(f32[40,16,128]{2,1,0:T(8,128)} %temp.1, f32[40,16,128]{2,1,0:T(8,128)} %uvel.1, f32[40,16,128]{2,1,0:T(8,128)} %vvel.1, ...), custom_call_target="tpu_custom_call" | custom-call | flops 1 | bytes 1 | tf_op jit(solution)/shard_map/first_rows/pallas_call | solution.py:440
  2.0 0.1 collective-permute-start
  2.1 0.0 copy-done.3
  2.1 0.0 copy-done.2
  2.1 0.0 copy-done.1
  2.1 0.1 copy-done
  2.2 0.0 copy-start.4
  2.2 0.6 %edges_pack.1 = (f32[288,128]{1,0:T(8,128)S(1)}, f32[280,128]{1,0:T(8,128)S(1)}, f32[48,128]{1,0:T(8,128)S(1)}, f32[56,128]{1,0:T(8,128)S(1)}, f32[80,128]{1,0:T(8,128)S(1)}) custom-call(f32[640,128]{1,0:T(8,128)S(1)} %bitcast.8, f32[640,128]{1,0:T(8,128)S(1)} %bitcast.11, f32[640,128]{1,0:T(8,128)S(1)} %bitcast.14, s32[640,128]{1,0:T(8,128)S(1)} %bitcast.17, ...), custom_call_target="tpu_custom_call" | custom-call | flops 1 | bytes 1 | tf_op jit(solution)/shard_map/edges_pack/pallas_call | solution.py:457
  2.8 1.4 %collective-permute-start.1 = (f32[288,128]{1,0:T(8,128)S(1)}, f32[288,128]{1,0:T(8,128)S(1)}, u32[]{:S(2)}, u32[]{:S(2)}) collective-permute-start(f32[288,128]{1,0:T(8,128)S(1)} %get-tuple-element.27), channel_id=1, source_target_pairs={{8,16},{16,8},{9,17},{17,9},{10,18},{18,10},{11,19},{19,11},{12,20... | collective-permute-start | bytes 442376 | tf_op jit(solution)/shard_map/ppermute | solution.py:472
  4.3 3.7 %collective-permute-start.2 = (f32[280,128]{1,0:T(8,128)S(1)}, f32[280,128]{1,0:T(8,128)S(1)}, u32[]{:S(2)}, u32[]{:S(2)}) collective-permute-start(f32[280,128]{1,0:T(8,128)S(1)} %get-tuple-element.28), channel_id=1, source_target_pairs={{16,24},{24,16},{17,25},{25,17},{18,26},{26,18},{19,27},{27,19},{2... | collective-permute-start | bytes 430088 | tf_op jit(solution)/shard_map/ppermute | solution.py:473
  8.0 0.0 collective-permute-start.4
  8.0 0.0 collective-permute-start.3
  8.0 0.0 copy-done.4
  8.0 0.2 %columns.1 = (f32[3,640,128]{2,1,0:T(8,128)S(1)}, f32[16,128]{1,0:T(8,128)S(1)}) custom-call(f32[640,128]{1,0:T(8,128)S(1)} %bitcast.20, s32[16,128]{1,0:T(8,128)S(1)} %get-tuple-element.23.levels), custom_call_target="tpu_custom_call" | custom-call | flops 1 | bytes 1 | tf_op jit(solution)/shard_map/columns/pallas_call | solution.py:476
  8.2 2.5 %interior.1.prov_in = f32[3,640,128]{2,1,0:T(8,128)S(1)} custom-call(f32[640,128]{1,0:T(8,128)S(1)} %bitcast.9, f32[640,128]{1,0:T(8,128)S(1)} %bitcast.12, f32[640,128]{1,0:T(8,128)S(1)} %bitcast.15, s32[640,128]{1,0:T(8,128)S(1)} %bitcast.18, f32[16,128]{1,0:T(8,128)S(1)} %get-tuple-element.19.inv_dx, f32[16,128]{1,0:T(8,128)S(1)} %get-tuple-element.20.inv_dy, ...), custom_call_target="tpu_custom_call" | custom-call | flops 1 | bytes 1 | tf_op jit(solution)/shard_map/interior/pallas_call | solution.py:485
  10.7 0.0 collective-permute-done.3.first
  10.7 0.4 %first_columns.1.packed = f32[96,128]{1,0:T(8,128)S(1)} custom-call(f32[80,128]{1,0:T(8,128)S(1)} %get-tuple-element.29.edges, f32[48,128]{1,0:T(8,128)S(1)} %collective-permute-done.3.first, f32[16,128]{1,0:T(8,128)S(1)} %get-tuple-element.19.inv_dx, f32[16,128]{1,0:T(8,128)S(1)} %get-tuple-element.21.spread), custom_call_target="tpu_custom_call" | custom-call | flops 1 | bytes 1 | tf_op jit(solution)/shard_map/first_columns/pallas_call | solution.py:494
  11.1 2.0 %collective-permute-done.4.second = f32[56,128]{1,0:T(8,128)S(1)} collective-permute-done((f32[56,128]{1,0:T(8,128)S(1)}, f32[56,128]{1,0:T(8,128)S(1)}, u32[]{:S(2)}, u32[]{:S(2)}) %collective-permute-start.4) | collective-permute-done | bytes 28704 | tf_op jit(solution)/shard_map/ppermute | solution.py:474
  13.1 0.0 collective-permute-done.2.got2
  13.1 0.0 collective-permute-done.1.got1
  13.1 0.0 collective-permute-done.got0
  13.1 1.9 %finish.1 = (f32[640,128]{1,0:T(8,128)}, f32[640,128]{1,0:T(8,128)}, f32[640,128]{1,0:T(8,128)}, f32[3,640,128]{2,1,0:T(8,128)S(1)}) custom-call(f32[3,640,128]{2,1,0:T(8,128)S(1)} %interior.1.prov_in, f32[3,640,128]{2,1,0:T(8,128)S(1)} %get-tuple-element.24.solve, f32[16,128]{1,0:T(8,128)S(1)} %get-tuple-element.25.middle, ...), custom_call_target="tpu_custom_call", output_to_operand_aliasing={{3}: (0, {})} | custom-call | flops 1 | bytes 1 | tf_op jit(solution)/shard_map/finish/pallas_call | solution.py:503
Async XLA Ops:
  0.6 1.5 %copy-start.3 = (s32[40,16,128]{2,1,0:T(8,128)S(1)}, s32[40,16,128]{2,1,0:T(8,128)}, u32[]{:S(2)}) copy-start(s32[40,16,128]{2,1,0:T(8,128)} %mask.1) | copy-start | bytes 983044
  0.6 1.5 %copy-start.2 = (f32[40,16,128]{2,1,0:T(8,128)S(1)}, f32[40,16,128]{2,1,0:T(8,128)}, u32[]{:S(2)}) copy-start(f32[40,16,128]{2,1,0:T(8,128)} %vvel.1) | copy-start | bytes 983044
  0.7 1.5 %copy-start.1 = (f32[40,16,128]{2,1,0:T(8,128)S(1)}, f32[40,16,128]{2,1,0:T(8,128)}, u32[]{:S(2)}) copy-start(f32[40,16,128]{2,1,0:T(8,128)} %uvel.1) | copy-start | bytes 983044
  0.7 1.6 %copy-start = (f32[40,16,128]{2,1,0:T(8,128)S(1)}, f32[40,16,128]{2,1,0:T(8,128)}, u32[]{:S(2)}) copy-start(f32[40,16,128]{2,1,0:T(8,128)} %temp.1) | copy-start | bytes 983044
  2.0 11.0 %collective-permute-start = (f32[296,128]{1,0:T(8,128)S(1)}, f32[296,128]{1,0:T(8,128)S(1)}, u32[]{:S(2)}, u32[]{:S(2)}) collective-permute-start(f32[296,128]{1,0:T(8,128)S(1)} %get-tuple-element.26.after), channel_id=1, source_target_pairs={{0,8},{8,0},{1,9},{9,1},{2,10},{10,2},{3,11},{11,3},{4,12},{12,4},... | collective-permute-start | bytes 454664 | tf_op jit(solution)/shard_map/ppermute | solution.py:453
  2.2 5.7 %copy-start.4 = (f32[40,16,128]{2,1,0:T(8,128)S(1)}, f32[40,16,128]{2,1,0:T(8,128)}, u32[]{:S(2)}) copy-start(f32[40,16,128]{2,1,0:T(8,128)} %param.13) | copy-start | bytes 983044
  2.8 10.2 %collective-permute-start.1 = (f32[288,128]{1,0:T(8,128)S(1)}, f32[288,128]{1,0:T(8,128)S(1)}, u32[]{:S(2)}, u32[]{:S(2)}) collective-permute-start(f32[288,128]{1,0:T(8,128)S(1)} %get-tuple-element.27), channel_id=1, source_target_pairs={{8,16},{16,8},{9,17},{17,9},{10,18},{18,10},{11,19},{19,11},{12,20... | collective-permute-start | bytes 442376 | tf_op jit(solution)/shard_map/ppermute | solution.py:472
  4.3 8.8 %collective-permute-start.2 = (f32[280,128]{1,0:T(8,128)S(1)}, f32[280,128]{1,0:T(8,128)S(1)}, u32[]{:S(2)}, u32[]{:S(2)}) collective-permute-start(f32[280,128]{1,0:T(8,128)S(1)} %get-tuple-element.28), channel_id=1, source_target_pairs={{16,24},{24,16},{17,25},{25,17},{18,26},{26,18},{19,27},{27,19},{2... | collective-permute-start | bytes 430088 | tf_op jit(solution)/shard_map/ppermute | solution.py:473
  8.0 5.1 %collective-permute-start.4 = (f32[56,128]{1,0:T(8,128)S(1)}, f32[56,128]{1,0:T(8,128)S(1)}, u32[]{:S(2)}, u32[]{:S(2)}) collective-permute-start(f32[56,128]{1,0:T(8,128)S(1)} %get-tuple-element.31), channel_id=1, source_target_pairs={{1,2},{2,1},{3,4},{4,3},{5,6},{6,5},{7,0},{0,7},{9,10},{10,9},{11,... | collective-permute-start | bytes 86024 | tf_op jit(solution)/shard_map/ppermute | solution.py:474
  8.0 2.7 %collective-permute-start.3 = (f32[48,128]{1,0:T(8,128)S(1)}, f32[48,128]{1,0:T(8,128)S(1)}, u32[]{:S(2)}, u32[]{:S(2)}) collective-permute-start(f32[48,128]{1,0:T(8,128)S(1)} %get-tuple-element.30), channel_id=1, source_target_pairs={{0,1},{1,0},{2,3},{3,2},{4,5},{5,4},{6,7},{7,6},{8,9},{9,8},{10,11... | collective-permute-start | bytes 73736 | tf_op jit(solution)/shard_map/ppermute | solution.py:475

commit v7 on v6

--- a/solution.py
+++ b/solution.py
@@ -1,3 +1,5 @@
+import functools
+
 import jax
 import jax.numpy as jnp
 from jax import lax
@@ -46,36 +48,24 @@
 
 def first_rows_kernel(
     temp, uvel, vvel, mask, dx_in, dy_in, spread_in, turn_in, levels_in,
-    out, dx, dy, spread, turn, levels, half0, half1, half2, halfm, sems
+    out, dx, dy, spread, turn, levels, wet, sems
 ):
     depth = temp.shape[0]
     north = sends_north(0)
-    copies = []
-    for field, half in ((temp, half0), (uvel, half1), (vvel, half2), (mask, halfm)):
-        copies.append(
-            pltpu.make_async_copy(
-                field.at[:, pl.ds(pl.multiple_of(north * TILE, TILE), TILE), :],
-                half.reshape(depth, TILE, LANES),
-                sems.at[len(copies)],
-            )
-        )
-    for plane, target in (
-        (dx_in, dx), (dy_in, dy), (spread_in, spread), (turn_in, turn), (levels_in, levels)
-    ):
-        copies.append(pltpu.make_async_copy(plane, target, sems.at[len(copies)]))
+    near = (ROWS - 1) * north
+    far = near + 1 - 2 * north
+    moves = [(mask.at[:, near, :], wet)]
+    for number, field in enumerate((temp, uvel, vvel)):
+        for place, row in ((2 * number, near), (2 * number + 1, far)):
+            moves.append((field.at[:, row, :], out.at[place * depth : (place + 1) * depth, :]))
+    moves += [(dx_in, dx), (dy_in, dy), (spread_in, spread), (turn_in, turn), (levels_in, levels)]
+    copies = [pltpu.make_async_copy(*move, sems.at[i]) for i, move in enumerate(moves)]
     for copy in copies:
         copy.start()
-    near = (TILE - 1) * north
-    far = near + 1 - 2 * north
     out[7 * depth :, :] = jnp.zeros((2 * TILE, LANES), jnp.float32)
-    for number, half in enumerate((half0, half1, half2)):
-        copies[number].wait()
-        base = 2 * depth * number
-        out[base : base + depth, :] = half[pl.ds(near, depth, stride=TILE), :]
-        out[base + depth : base + 2 * depth, :] = half[pl.ds(far, depth, stride=TILE), :]
-    copies[3].wait()
-    out[6 * depth : 7 * depth, :] = halfm[pl.ds(near, depth, stride=TILE), :].astype(jnp.float32)
-    for copy in copies[4:]:
+    copies[0].wait()
+    out[6 * depth : 7 * depth, :] = wet[...].astype(jnp.float32)
+    for copy in copies[1:]:
         copy.wait()
 
 
@@ -146,68 +136,69 @@
     middle[...] = 1.0 / (1.0 - chains[0] * chains[1])
 
 
-def interior_kernel(
-    temp, uvel, vvel, mask, inv_dx, inv_dy, spread, coriolis, prov
-):
+def interior_kernel(temp, uvel, vvel, mask, inv_dx, inv_dy, spread, coriolis, prov):
     depth = temp.shape[0] // ROWS
-    lane = lane_index(depth)
-
-    def rows_of(ref, row):
-        return ref[level_rows(row, depth), :]
-
-    def wet_of(row):
-        return rows_of(mask, row).astype(jnp.float32)
-
-    fields = (temp, uvel, vvel)
-    advect_south = [0.0] * 3
-    spread_south = [0.0] * 3
-    for row in range(ROWS):
-        one = slice(row, row + 1)
-        scale = inv_dx[one, :]
-        spread_x = spread[one, :] * scale * scale
-        scale = scale * (-1.0 / 24.0)
-        wet = wet_of(row)
+    lane = lane_index(ROWS)
+    row = lax.broadcasted_iota(jnp.int32, (ROWS, LANES), 0)
+    spread_x = spread[...] * inv_dx[...] * inv_dx[...]
+    spread_y = spread[...] * inv_dy[...] * inv_dy[...]
+    scale_x = inv_dx[...] * (-1.0 / 24.0)
+    scale_y = inv_dy[...] * (-1.0 / 24.0)
+    turn = coriolis[...]
+
+    def shifted_rows(ref, number, count):
+        start = number * ROWS + count
+        if start < 0 or start + ROWS > ref.shape[0]:
+            return pltpu.roll(level(ref, number), -count % ROWS, 0)
+        return ref[start : start + ROWS, :]
+
+    def weights(face_low, face_high, speed_low, speed_high):
+        return (
+            speed_low,
+            face_low - speed_high - 7.0 * speed_low,
+            7.0 * (speed_high - speed_low) - face_low - face_high,
+            face_high + speed_low + 7.0 * speed_high,
+            -speed_high,
+        )
+
+    for number in range(depth):
+        here = slice(number * ROWS, (number + 1) * ROWS)
+        wet = level(mask, number).astype(jnp.float32)
+        u, v = level(uvel, number), level(vvel, number)
         face_w = wet * jnp.where(lane >= 1, turn_lanes(wet, 1), 0.0)
         face_e = wet * jnp.where(lane < LANES - 1, turn_lanes(wet, -1), 0.0)
-        u = rows_of(uvel, row)
-        speed_w = scale * face_w * (turn_lanes(u, 1) + u)
-        speed_e = scale * face_e * (turn_lanes(u, -1) + u)
-        face_w = spread_x * face_w
-        face_e = spread_x * face_e
-        scale_y = inv_dy[one, :]
-        spread_y = spread[one, :] * scale_y * scale_y
-        scale_y = scale_y * (-1.0 / 24.0)
-        if row + 1 < ROWS:
-            face_n = wet * wet_of(row + 1)
-            speed_n = face_n * (rows_of(vvel, row) + rows_of(vvel, row + 1))
-        turn = wet * coriolis[one, :]
-        for number, field in enumerate(fields):
-            q = rows_of(field, row)
-            west, east = turn_lanes(q, 1), turn_lanes(q, -1)
-            value_w = 7.0 * (west + q) - (turn_lanes(q, 2) + east)
-            value_e = 7.0 * (east + q) - (west + turn_lanes(q, -2))
-            total = speed_e * value_e - speed_w * value_w + face_e * (east - q) - face_w * (q - west)
-            if row + 1 < ROWS:
-                north = rows_of(field, row + 1)
-                outer = None
-                if row >= 1:
-                    outer = rows_of(field, row - 1)
-                if row + 2 < ROWS:
-                    beyond = rows_of(field, row + 2)
-                    outer = beyond if outer is None else outer + beyond
-                advect_north = speed_n * (7.0 * (q + north) - outer)
-                spread_north = face_n * (north - q)
-            else:
-                advect_north, spread_north = 0.0, 0.0
-            total = total + scale_y * (advect_north - advect_south[number])
-            total = total + spread_y * (spread_north - spread_south[number])
-            advect_south[number], spread_south[number] = advect_north, spread_north
-            if number == 1:
-                total = total + turn * rows_of(vvel, row)
-            if number == 2:
-                total = total - turn * u
-            target = prov.at[number]
-            target[level_rows(row, depth), :] = q + total
+        face_s = wet * jnp.where(row >= 1, shifted_rows(mask, number, -1).astype(jnp.float32), 0.0)
+        face_n = wet * jnp.where(row < ROWS - 1, shifted_rows(mask, number, 1).astype(jnp.float32), 0.0)
+        west2, west, here_x, east, east2 = weights(
+            spread_x * face_w,
+            spread_x * face_e,
+            scale_x * face_w * (turn_lanes(u, 1) + u),
+            scale_x * face_e * (turn_lanes(u, -1) + u),
+        )
+        south2, south, here_y, north, north2 = weights(
+            spread_y * face_s,
+            spread_y * face_n,
+            scale_y * face_s * (shifted_rows(vvel, number, -1) + v),
+            scale_y * face_n * (shifted_rows(vvel, number, 1) + v),
+        )
+        south2 = jnp.where(row >= 2, south2, 0.0)
+        south = jnp.where(row >= 1, south, 0.0)
+        north = jnp.where(row < ROWS - 1, north, 0.0)
+        north2 = jnp.where(row < ROWS - 2, north2, 0.0)
+        middle = 1.0 + here_x + here_y
+        wet_turn = wet * turn
+        for index, ref in enumerate((temp, uvel, vvel)):
+            q = level(ref, number)
+            total = middle * q
+            total += west * turn_lanes(q, 1) + east * turn_lanes(q, -1)
+            total += west2 * turn_lanes(q, 2) + east2 * turn_lanes(q, -2)
+            total += south * shifted_rows(ref, number, -1) + north * shifted_rows(ref, number, 1)
+            total += south2 * shifted_rows(ref, number, -2) + north2 * shifted_rows(ref, number, 2)
+            if index == 1:
+                total += wet_turn * v
+            if index == 2:
+                total -= wet_turn * u
+            prov[index, here, :] = total
 
 
 def add_row_ghosts(prov, fields, mask, ghost, near, inv_dy, spread, flip):
@@ -293,17 +284,17 @@
     return jnp.where(border, turn_lanes(source, -(start + 2)), 0.0)
 
 
-def first_columns_kernel(edges, first, inv_dx, spread, out):
-    odd = lax.rem(lax.axis_index("lon"), 2) == 1
-    for part, slabs in enumerate(column_ghosts(edges, first, odd, inv_dx, spread)):
+def columns_ghosts_kernel(parity, edges, other, inv_dx, spread, out):
+    west = lax.rem(lax.axis_index("lon"), 2) == parity
+    for part, slabs in enumerate(column_ghosts(edges, other, west, inv_dx, spread)):
         for field in range(3):
             place = (3 * part + field) * ROWS
             out[place : place + ROWS, :] = slabs[field]
 
 
 def finish_kernel(
-    prov_in, solve, middle, temp, uvel, vvel, mask, got0, got1, got2, edges, packed, second,
-    inv_dx, inv_dy, spread, temp_new, uvel_new, vvel_new, prov, work, south, north, sems
+    prov_in, solve, middle, temp, uvel, vvel, mask, got0, got1, got2, packed1, packed2,
+    inv_dy, spread, temp_new, uvel_new, vvel_new, prov, work, south, north, sems
 ):
     depth = prov.shape[1] // ROWS
     half = depth // 2
@@ -325,14 +316,12 @@
     add_row_ghosts(prov, fields, mask, south, 0, inv_dy, spread, 1.0)
     add_row_ghosts(prov, fields, mask, north, ROWS - 1, inv_dy, spread, flip)
 
-    odd = lax.rem(lax.axis_index("lon"), 2)
     lane = lane_index(ROWS)
-    from_first = lane % 4 // 2 == odd
-    corrections = []
-    for part, slabs in enumerate(column_ghosts(edges, second, odd == 0, inv_dx, spread)):
-        corrections.append(
-            [jnp.where(from_first, level(packed, 3 * part + f), slabs[f]) for f in range(3)]
-        )
+    from_first = lane % 4 // 2 == lax.rem(lax.axis_index("lon"), 2)
+    corrections = [
+        [jnp.where(from_first, level(packed1, place), level(packed2, place)) for place in range(part, part + 3)]
+        for part in (0, 3)
+    ]
     border = (lane < 2) | (lane >= LANES - 2)
 
     def border_part(number, field):
@@ -445,8 +434,7 @@
         + (jax.ShapeDtypeStruct((rows, lanes), jnp.int32),),
         in_specs=[HBM] * 9,
         out_specs=(VMEM,) * 6,
-        scratch_shapes=[vmem(depth * TILE, lanes)] * 3
-        + [vmem(depth * TILE, lanes, dtype=jnp.int32), pltpu.SemaphoreType.DMA((9,))],
+        scratch_shapes=[vmem(depth, lanes, dtype=jnp.int32), pltpu.SemaphoreType.DMA((12,))],
         compiler_params=limit,
         cost_estimate=cheap,
     )(*arrays)
@@ -491,20 +479,23 @@
         compiler_params=limit,
         cost_estimate=cheap,
     )(temp, uvel, vvel, wet_mask, inv_dx, inv_dy, horiz_mixing, coriolis)
-    packed = pl.pallas_call(
-        first_columns_kernel,
-        name="first_columns",
-        out_shape=f32(6 * rows, lanes),
-        in_specs=[VMEM] * 4,
-        out_specs=VMEM,
-        compiler_params=limit,
-        cost_estimate=cheap,
-    )(edges, first, inv_dx, horiz_mixing)
+    packed1, packed2 = (
+        pl.pallas_call(
+            functools.partial(columns_ghosts_kernel, parity),
+            name="columns_ghosts" + str(parity),
+            out_shape=f32(6 * rows, lanes),
+            in_specs=[VMEM] * 4,
+            out_specs=VMEM,
+            compiler_params=limit,
+            cost_estimate=cost,
+        )(edges, other, inv_dx, horiz_mixing)
+        for parity, other, cost in ((1, first, cheap), (0, second, cheap))
+    )
     outs = pl.pallas_call(
         finish_kernel,
         name="finish",
         out_shape=(f32(flat, lanes),) * 3 + (f32(3, flat, lanes),),
-        in_specs=[VMEM] * 16,
+        in_specs=[VMEM] * 14,
         out_specs=(HBM,) * 3 + (VMEM,),
         input_output_aliases={0: 3},
         scratch_shapes=[
@@ -516,8 +507,8 @@
         compiler_params=limit,
         cost_estimate=cheap,
     )(
-        prov, solve, middle, temp, uvel, vvel, wet_mask, got0, got1, got2, edges, packed, second,
-        inv_dx, inv_dy, horiz_mixing,
+        prov, solve, middle, temp, uvel, vvel, wet_mask, got0, got1, got2, packed1, packed2,
+        inv_dy, horiz_mixing,
     )
     return tuple(x.reshape(depth, rows, lanes) for x in outs[:3])
 

time: 15.1 us -> 15 us (level)
  Pallas kernels: 6.93 us -> 5.75 us
  waiting for transfers between devices: 2 us -> 3.02 us
    ppermute x1, waiting for transfers between devices: 1.99 us -> 3.01 us  [per_device(): second = lax.ppermute(zonal2, both, zonal_second)]
    pallas_call x1, Pallas kernels: 2.49 us -> 1.47 us  [per_device(): pl.pallas_call(interior_kernel, name='interior', out_shape=f32(3, flat, l...]
    pallas_call x1 -> x2, Pallas kernels: 0.38 us -> 0.75 us  [per_device(): pl.pallas_call(functools.partial(columns_ghosts_kernel, parity), name='co...]
    pallas_call x1, Pallas kernels: 1.36 us -> 1.04 us  [per_device(): pl.pallas_call(first_rows_kernel, name='first_rows', out_shape=(f32(7 * d...]
    pallas_call x1, Pallas kernels: 1.91 us -> 1.72 us  [per_device(): pl.pallas_call(finish_kernel, name='finish', out_shape=(f32(flat, lanes),...]
  transfers between devices with their start and end apart: 5 -> 5, of which waited for: 1 -> 1; matrix products, arithmetic and copies ran while one was open for 0% -> 0% of each run, Pallas kernels for 24% -> 20%
where the time goes in v7:
time: 15 us; the launch traced here: 14.8 us
  Pallas kernels  5.75 us (38%)
  starting transfers between devices  5.09 us (34%)
  waiting for transfers between devices  3.02 us (20%)
  between operations  0.75 us (5%)
  local copies, waits for them, and re-layouts  0.22 us (1%)
    ppermute x1, starting transfers between devices, per_device(): got2 = lax.ppermute(sent2, both, meridional[2])  3.54 us
    ppermute x1, waiting for transfers between devices, per_device(): second = lax.ppermute(zonal2, both, zonal_second)  3.01 us
    pallas_call x1, Pallas kernels, per_device(): pl.pallas_call(finish_kernel, name='finish', out_shape=(f32(flat, lanes),...  1.72 us
    ppermute x1, starting transfers between devices, per_device(): got1 = lax.ppermute(sent1, both, meridional[1])  1.48 us
    pallas_call x1, Pallas kernels, per_device(): pl.pallas_call(interior_kernel, name='interior', out_shape=f32(3, flat, l...  1.47 us
    pallas_call x1, Pallas kernels, per_device(): pl.pallas_call(first_rows_kernel, name='first_rows', out_shape=(f32(7 * d...  1.04 us
    pallas_call x2, Pallas kernels, per_device(): pl.pallas_call(functools.partial(columns_ghosts_kernel, parity), name='co...  0.75 us
    pallas_call x1, Pallas kernels, per_device(): pl.pallas_call(edges_pack_kernel, name='edges_pack', out_shape=(f32(7 * d...  0.58 us
  transfers between devices with their start and end apart: 5, of which 1 were waited for; matrix products, arithmetic and copies ran while one was open for 0% of the time, Pallas kernels for 20%

profile of v7, /device:TPU:4, one launch (start us, length us, event | category | flops | bytes accessed | tf_op | source)
XLA Modules:
  0.0 14.8 jit_solution(726544302070752166)
XLA Ops:
  0.6 0.0 copy-start.3
  0.6 0.0 copy-start.2
  0.7 0.0 copy-start.1
  0.7 0.0 copy-start
  0.7 1.0 %first_rows.1 = (f32[296,128]{1,0:T(8,128)S(1)}, f32[16,128]{1,0:T(8,128)S(1)}, f32[16,128]{1,0:T(8,128)S(1)}, f32[16,128]{1,0:T(8,128)S(1)}, f32[16,128]{1,0:T(8,128)S(1)}, /*index=5*/s32[16,128]{1,0:T(8,128)S(1)}) custom-call(f32[40,16,128]{2,1,0:T(8,128)} %temp.1, f32[40,16,128]{2,1,0:T(8,128)} %uvel.1, f32[40,16,128]{2,1,0:T(8,128)} %vvel.1, ...), custom_call_target="tpu_custom_call" | custom-call | flops 1 | bytes 1 | tf_op jit(solution)/shard_map/first_rows/pallas_call | solution.py:429
  1.7 0.1 collective-permute-start
  1.8 0.0 copy-done.3
  1.8 0.0 copy-done.2
  1.8 0.1 copy-done.1
  1.9 0.1 copy-done
  2.0 0.0 copy-start.4
  2.0 0.6 %edges_pack.1 = (f32[288,128]{1,0:T(8,128)S(1)}, f32[280,128]{1,0:T(8,128)S(1)}, f32[48,128]{1,0:T(8,128)S(1)}, f32[56,128]{1,0:T(8,128)S(1)}, f32[80,128]{1,0:T(8,128)S(1)}) custom-call(f32[640,128]{1,0:T(8,128)S(1)} %bitcast.8, f32[640,128]{1,0:T(8,128)S(1)} %bitcast.11, f32[640,128]{1,0:T(8,128)S(1)} %bitcast.14, s32[640,128]{1,0:T(8,128)S(1)} %bitcast.17, ...), custom_call_target="tpu_custom_call" | custom-call | flops 1 | bytes 1 | tf_op jit(solution)/shard_map/edges_pack/pallas_call | solution.py:445
  2.6 1.5 %collective-permute-start.1 = (f32[288,128]{1,0:T(8,128)S(1)}, f32[288,128]{1,0:T(8,128)S(1)}, u32[]{:S(2)}, u32[]{:S(2)}) collective-permute-start(f32[288,128]{1,0:T(8,128)S(1)} %get-tuple-element.27), channel_id=1, source_target_pairs={{8,16},{16,8},{9,17},{17,9},{10,18},{18,10},{11,19},{19,11},{12,20... | collective-permute-start | bytes 442376 | tf_op jit(solution)/shard_map/ppermute | solution.py:460
  4.1 3.5 %collective-permute-start.2 = (f32[280,128]{1,0:T(8,128)S(1)}, f32[280,128]{1,0:T(8,128)S(1)}, u32[]{:S(2)}, u32[]{:S(2)}) collective-permute-start(f32[280,128]{1,0:T(8,128)S(1)} %get-tuple-element.28), channel_id=1, source_target_pairs={{16,24},{24,16},{17,25},{25,17},{18,26},{26,18},{19,27},{27,19},{2... | collective-permute-start | bytes 430088 | tf_op jit(solution)/shard_map/ppermute | solution.py:461
  7.6 0.0 collective-permute-start.4
  7.6 0.0 collective-permute-start.3
  7.6 0.0 copy-done.4
  7.6 0.2 %columns.1 = (f32[3,640,128]{2,1,0:T(8,128)S(1)}, f32[16,128]{1,0:T(8,128)S(1)}) custom-call(f32[640,128]{1,0:T(8,128)S(1)} %bitcast.20, s32[16,128]{1,0:T(8,128)S(1)} %get-tuple-element.23.levels), custom_call_target="tpu_custom_call" | custom-call | flops 1 | bytes 1 | tf_op jit(solution)/shard_map/columns/pallas_call | solution.py:464
  7.8 1.5 %interior.1.prov_in = f32[3,640,128]{2,1,0:T(8,128)S(1)} custom-call(f32[640,128]{1,0:T(8,128)S(1)} %bitcast.9, f32[640,128]{1,0:T(8,128)S(1)} %bitcast.12, f32[640,128]{1,0:T(8,128)S(1)} %bitcast.15, s32[640,128]{1,0:T(8,128)S(1)} %bitcast.18, f32[16,128]{1,0:T(8,128)S(1)} %get-tuple-element.19.inv_dx, f32[16,128]{1,0:T(8,128)S(1)} %get-tuple-element.20.inv_dy, ...), custom_call_target="tpu_custom_call" | custom-call | flops 1 | bytes 1 | tf_op jit(solution)/shard_map/interior/pallas_call | solution.py:473
  9.3 0.0 collective-permute-done.3.other
  9.3 0.4 %columns_ghosts1.1.packed1 = f32[96,128]{1,0:T(8,128)S(1)} custom-call(f32[80,128]{1,0:T(8,128)S(1)} %get-tuple-element.29.edges, f32[48,128]{1,0:T(8,128)S(1)} %collective-permute-done.3.other, f32[16,128]{1,0:T(8,128)S(1)} %get-tuple-element.19.inv_dx, f32[16,128]{1,0:T(8,128)S(1)} %get-tuple-element.21.spread), custom_call_target="tpu_custom_call" | custom-call | flops 1 | bytes 1 | tf_op jit(solution)/shard_map/columns_ghosts1/pallas_call | solution.py:483
  9.7 3.0 %collective-permute-done.4.other = f32[56,128]{1,0:T(8,128)S(1)} collective-permute-done((f32[56,128]{1,0:T(8,128)S(1)}, f32[56,128]{1,0:T(8,128)S(1)}, u32[]{:S(2)}, u32[]{:S(2)}) %collective-permute-start.4) | collective-permute-done | bytes 28704 | tf_op jit(solution)/shard_map/ppermute | solution.py:462
  12.7 0.4 %columns_ghosts0.1.packed2 = f32[96,128]{1,0:T(8,128)S(1)} custom-call(f32[80,128]{1,0:T(8,128)S(1)} %get-tuple-element.29.edges, f32[56,128]{1,0:T(8,128)S(1)} %collective-permute-done.4.other, f32[16,128]{1,0:T(8,128)S(1)} %get-tuple-element.19.inv_dx, f32[16,128]{1,0:T(8,128)S(1)} %get-tuple-element.21.spread), custom_call_target="tpu_custom_call" | custom-call | flops 1 | bytes 1 | tf_op jit(solution)/shard_map/columns_ghosts0/pallas_call | solution.py:483
  13.1 0.0 collective-permute-done.2.got2
  13.1 0.0 collective-permute-done.1.got1
  13.1 0.0 collective-permute-done.got0
  13.1 1.7 %finish.1 = (f32[640,128]{1,0:T(8,128)}, f32[640,128]{1,0:T(8,128)}, f32[640,128]{1,0:T(8,128)}, f32[3,640,128]{2,1,0:T(8,128)S(1)}) custom-call(f32[3,640,128]{2,1,0:T(8,128)S(1)} %interior.1.prov_in, f32[3,640,128]{2,1,0:T(8,128)S(1)} %get-tuple-element.24.solve, f32[16,128]{1,0:T(8,128)S(1)} %get-tuple-element.25.middle, ...), custom_call_target="tpu_custom_call", output_to_operand_aliasing={{3}: (0, {})} | custom-call | flops 1 | bytes 1 | tf_op jit(solution)/shard_map/finish/pallas_call | solution.py:494
Async XLA Ops:
  0.6 1.2 %copy-start.3 = (s32[40,16,128]{2,1,0:T(8,128)S(1)}, s32[40,16,128]{2,1,0:T(8,128)}, u32[]{:S(2)}) copy-start(s32[40,16,128]{2,1,0:T(8,128)} %mask.1) | copy-start | bytes 983044
  0.6 1.2 %copy-start.2 = (f32[40,16,128]{2,1,0:T(8,128)S(1)}, f32[40,16,128]{2,1,0:T(8,128)}, u32[]{:S(2)}) copy-start(f32[40,16,128]{2,1,0:T(8,128)} %vvel.1) | copy-start | bytes 983044
  0.7 1.3 %copy-start.1 = (f32[40,16,128]{2,1,0:T(8,128)S(1)}, f32[40,16,128]{2,1,0:T(8,128)}, u32[]{:S(2)}) copy-start(f32[40,16,128]{2,1,0:T(8,128)} %uvel.1) | copy-start | bytes 983044
  0.7 1.4 %copy-start = (f32[40,16,128]{2,1,0:T(8,128)S(1)}, f32[40,16,128]{2,1,0:T(8,128)}, u32[]{:S(2)}) copy-start(f32[40,16,128]{2,1,0:T(8,128)} %temp.1) | copy-start | bytes 983044
  1.7 11.4 %collective-permute-start = (f32[296,128]{1,0:T(8,128)S(1)}, f32[296,128]{1,0:T(8,128)S(1)}, u32[]{:S(2)}, u32[]{:S(2)}) collective-permute-start(f32[296,128]{1,0:T(8,128)S(1)} %get-tuple-element.26.after), channel_id=1, source_target_pairs={{0,8},{8,0},{1,9},{9,1},{2,10},{10,2},{3,11},{11,3},{4,12},{12,4},... | collective-permute-start | bytes 454664 | tf_op jit(solution)/shard_map/ppermute | solution.py:441
  2.0 5.6 %copy-start.4 = (f32[40,16,128]{2,1,0:T(8,128)S(1)}, f32[40,16,128]{2,1,0:T(8,128)}, u32[]{:S(2)}) copy-start(f32[40,16,128]{2,1,0:T(8,128)} %param.13) | copy-start | bytes 983044
  2.6 10.5 %collective-permute-start.1 = (f32[288,128]{1,0:T(8,128)S(1)}, f32[288,128]{1,0:T(8,128)S(1)}, u32[]{:S(2)}, u32[]{:S(2)}) collective-permute-start(f32[288,128]{1,0:T(8,128)S(1)} %get-tuple-element.27), channel_id=1, source_target_pairs={{8,16},{16,8},{9,17},{17,9},{10,18},{18,10},{11,19},{19,11},{12,20... | collective-permute-start | bytes 442376 | tf_op jit(solution)/shard_map/ppermute | solution.py:460
  4.1 9.0 %collective-permute-start.2 = (f32[280,128]{1,0:T(8,128)S(1)}, f32[280,128]{1,0:T(8,128)S(1)}, u32[]{:S(2)}, u32[]{:S(2)}) collective-permute-start(f32[280,128]{1,0:T(8,128)S(1)} %get-tuple-element.28), channel_id=1, source_target_pairs={{16,24},{24,16},{17,25},{25,17},{18,26},{26,18},{19,27},{27,19},{2... | collective-permute-start | bytes 430088 | tf_op jit(solution)/shard_map/ppermute | solution.py:461
  7.6 5.1 %collective-permute-start.4 = (f32[56,128]{1,0:T(8,128)S(1)}, f32[56,128]{1,0:T(8,128)S(1)}, u32[]{:S(2)}, u32[]{:S(2)}) collective-permute-start(f32[56,128]{1,0:T(8,128)S(1)} %get-tuple-element.31), channel_id=1, source_target_pairs={{1,2},{2,1},{3,4},{4,3},{5,6},{6,5},{7,0},{0,7},{9,10},{10,9},{11,... | collective-permute-start | bytes 86024 | tf_op jit(solution)/shard_map/ppermute | solution.py:462
  7.6 1.7 %collective-permute-start.3 = (f32[48,128]{1,0:T(8,128)S(1)}, f32[48,128]{1,0:T(8,128)S(1)}, u32[]{:S(2)}, u32[]{:S(2)}) collective-permute-start(f32[48,128]{1,0:T(8,128)S(1)} %get-tuple-element.30), channel_id=1, source_target_pairs={{0,1},{1,0},{2,3},{3,2},{4,5},{5,4},{6,7},{7,6},{8,9},{9,8},{10,11... | collective-permute-start | bytes 73736 | tf_op jit(solution)/shard_map/ppermute | solution.py:463

commit v8 on v7

--- a/solution.py
+++ b/solution.py
@@ -62,7 +62,7 @@
     copies = [pltpu.make_async_copy(*move, sems.at[i]) for i, move in enumerate(moves)]
     for copy in copies:
         copy.start()
-    out[7 * depth :, :] = jnp.zeros((2 * TILE, LANES), jnp.float32)
+    out[7 * depth :, :] = jnp.zeros((TILE, LANES), jnp.float32)
     copies[0].wait()
     out[6 * depth : 7 * depth, :] = wet[...].astype(jnp.float32)
     for copy in copies[1:]:
@@ -429,7 +429,7 @@
     sent0, inv_dx, inv_dy, horiz_mixing, coriolis, levels = pl.pallas_call(
         first_rows_kernel,
         name="first_rows",
-        out_shape=(f32(7 * depth + 2 * TILE, lanes),)
+        out_shape=(f32(7 * depth + TILE, lanes),)
         + (f32(rows, lanes),) * 4
         + (jax.ShapeDtypeStruct((rows, lanes), jnp.int32),),
         in_specs=[HBM] * 9,
@@ -489,7 +489,7 @@
             compiler_params=limit,
             cost_estimate=cost,
         )(edges, other, inv_dx, horiz_mixing)
-        for parity, other, cost in ((1, first, cheap), (0, second, cheap))
+        for parity, other, cost in ((1, first, cheap), (0, second, pl.CostEstimate(flops=1250000000, bytes_accessed=1, transcendentals=0)))
     )
     outs = pl.pallas_call(
         finish_kernel,

time: 15 us -> 14 us (0.933)
  the two profiles are of different devices: /device:TPU:4 before, /device:TPU:22 now
where the time goes in v8:
time: 14 us; the launch traced here: 13.8 us
  Pallas kernels  5.76 us (41%)
  starting transfers between devices  3.79 us (27%)
  waiting for transfers between devices  3.32 us (24%)
  between operations  0.74 us (5%)
  local copies, waits for them, and re-layouts  0.22 us (2%)
    ppermute x1, waiting for transfers between devices, per_device(): second = lax.ppermute(zonal2, both, zonal_second)  3.31 us
    pallas_call x1, Pallas kernels, per_device(): pl.pallas_call(finish_kernel, name='finish', out_shape=(f32(flat, lanes),...  1.72 us
    pallas_call x1, Pallas kernels, per_device(): pl.pallas_call(interior_kernel, name='interior', out_shape=f32(3, flat, l...  1.46 us
    ppermute x1, starting transfers between devices, per_device(): first = lax.ppermute(zonal1, both, zonal_first)  1.41 us
    ppermute x1, starting transfers between devices, per_device(): second = lax.ppermute(zonal2, both, zonal_second)  1.26 us
    pallas_call x1, Pallas kernels, per_device(): pl.pallas_call(first_rows_kernel, name='first_rows', out_shape=(f32(7 * d...  1.04 us
    pallas_call x2, Pallas kernels, per_device(): pl.pallas_call(functools.partial(columns_ghosts_kernel, parity), name='co...  0.75 us
    ppermute x1, starting transfers between devices, per_device(): got2 = lax.ppermute(sent2, both, meridional[2])  0.67 us
  transfers between devices with their start and end apart: 5, of which 1 were waited for; matrix products, arithmetic and copies ran while one was open for 0% of the time, Pallas kernels for 22%

profile of v8, /device:TPU:22, one launch (start us, length us, event | category | flops | bytes accessed | tf_op | source)
XLA Modules:
  0.0 13.8 jit_solution(1705592663886032718)
XLA Ops:
  0.6 0.0 copy-start.3
  0.6 0.0 copy-start.2
  0.7 0.0 copy-start.1
  0.7 0.0 copy-start
  0.7 1.0 %first_rows.1 = (f32[288,128]{1,0:T(8,128)S(1)}, f32[16,128]{1,0:T(8,128)S(1)}, f32[16,128]{1,0:T(8,128)S(1)}, f32[16,128]{1,0:T(8,128)S(1)}, f32[16,128]{1,0:T(8,128)S(1)}, /*index=5*/s32[16,128]{1,0:T(8,128)S(1)}) custom-call(f32[40,16,128]{2,1,0:T(8,128)} %temp.1, f32[40,16,128]{2,1,0:T(8,128)} %uvel.1, f32[40,16,128]{2,1,0:T(8,128)} %vvel.1, ...), custom_call_target="tpu_custom_call" | custom-call | flops 1 | bytes 1 | tf_op jit(solution)/shard_map/first_rows/pallas_call | solution.py:429
  1.7 0.1 collective-permute-start
  1.8 0.0 copy-done.3
  1.8 0.0 copy-done.2
  1.8 0.1 copy-done.1
  1.9 0.1 copy-done
  2.0 0.0 copy-start.4
  2.0 0.6 %edges_pack.1 = (f32[288,128]{1,0:T(8,128)S(1)}, f32[280,128]{1,0:T(8,128)S(1)}, f32[48,128]{1,0:T(8,128)S(1)}, f32[56,128]{1,0:T(8,128)S(1)}, f32[80,128]{1,0:T(8,128)S(1)}) custom-call(f32[640,128]{1,0:T(8,128)S(1)} %bitcast.8, f32[640,128]{1,0:T(8,128)S(1)} %bitcast.11, f32[640,128]{1,0:T(8,128)S(1)} %bitcast.14, s32[640,128]{1,0:T(8,128)S(1)} %bitcast.17, ...), custom_call_target="tpu_custom_call" | custom-call | flops 1 | bytes 1 | tf_op jit(solution)/shard_map/edges_pack/pallas_call | solution.py:445
  2.6 0.4 %collective-permute-start.1 = (f32[288,128]{1,0:T(8,128)S(1)}, f32[288,128]{1,0:T(8,128)S(1)}, u32[]{:S(2)}, u32[]{:S(2)}) collective-permute-start(f32[288,128]{1,0:T(8,128)S(1)} %get-tuple-element.27), channel_id=1, source_target_pairs={{8,16},{16,8},{9,17},{17,9},{10,18},{18,10},{11,19},{19,11},{12,20... | collective-permute-start | bytes 442376 | tf_op jit(solution)/shard_map/ppermute | solution.py:460
  3.0 1.3 %collective-permute-start.4 = (f32[56,128]{1,0:T(8,128)S(1)}, f32[56,128]{1,0:T(8,128)S(1)}, u32[]{:S(2)}, u32[]{:S(2)}) collective-permute-start(f32[56,128]{1,0:T(8,128)S(1)} %get-tuple-element.31), channel_id=1, source_target_pairs={{1,2},{2,1},{3,4},{4,3},{5,6},{6,5},{7,0},{0,7},{9,10},{10,9},{11,... | collective-permute-start | bytes 86024 | tf_op jit(solution)/shard_map/ppermute | solution.py:462
  4.3 0.7 %collective-permute-start.2 = (f32[280,128]{1,0:T(8,128)S(1)}, f32[280,128]{1,0:T(8,128)S(1)}, u32[]{:S(2)}, u32[]{:S(2)}) collective-permute-start(f32[280,128]{1,0:T(8,128)S(1)} %get-tuple-element.28), channel_id=1, source_target_pairs={{16,24},{24,16},{17,25},{25,17},{18,26},{26,18},{19,27},{27,19},{2... | collective-permute-start | bytes 430088 | tf_op jit(solution)/shard_map/ppermute | solution.py:461
  4.9 1.4 %collective-permute-start.3 = (f32[48,128]{1,0:T(8,128)S(1)}, f32[48,128]{1,0:T(8,128)S(1)}, u32[]{:S(2)}, u32[]{:S(2)}) collective-permute-start(f32[48,128]{1,0:T(8,128)S(1)} %get-tuple-element.30), channel_id=1, source_target_pairs={{0,1},{1,0},{2,3},{3,2},{4,5},{5,4},{6,7},{7,6},{8,9},{9,8},{10,11... | collective-permute-start | bytes 73736 | tf_op jit(solution)/shard_map/ppermute | solution.py:463
  6.3 0.0 copy-done.4
  6.3 0.2 %columns.1 = (f32[3,640,128]{2,1,0:T(8,128)S(1)}, f32[16,128]{1,0:T(8,128)S(1)}) custom-call(f32[640,128]{1,0:T(8,128)S(1)} %bitcast.20, s32[16,128]{1,0:T(8,128)S(1)} %get-tuple-element.23.levels), custom_call_target="tpu_custom_call" | custom-call | flops 1 | bytes 1 | tf_op jit(solution)/shard_map/columns/pallas_call | solution.py:464
  6.5 1.5 %interior.1.prov_in = f32[3,640,128]{2,1,0:T(8,128)S(1)} custom-call(f32[640,128]{1,0:T(8,128)S(1)} %bitcast.9, f32[640,128]{1,0:T(8,128)S(1)} %bitcast.12, f32[640,128]{1,0:T(8,128)S(1)} %bitcast.15, s32[640,128]{1,0:T(8,128)S(1)} %bitcast.18, f32[16,128]{1,0:T(8,128)S(1)} %get-tuple-element.19.inv_dx, f32[16,128]{1,0:T(8,128)S(1)} %get-tuple-element.20.inv_dy, ...), custom_call_target="tpu_custom_call" | custom-call | flops 1 | bytes 1 | tf_op jit(solution)/shard_map/interior/pallas_call | solution.py:473
  8.0 0.0 collective-permute-done.3.other
  8.0 0.4 %columns_ghosts1.1.packed1 = f32[96,128]{1,0:T(8,128)S(1)} custom-call(f32[80,128]{1,0:T(8,128)S(1)} %get-tuple-element.29.edges, f32[48,128]{1,0:T(8,128)S(1)} %collective-permute-done.3.other, f32[16,128]{1,0:T(8,128)S(1)} %get-tuple-element.19.inv_dx, f32[16,128]{1,0:T(8,128)S(1)} %get-tuple-element.21.spread), custom_call_target="tpu_custom_call" | custom-call | flops 1 | bytes 1 | tf_op jit(solution)/shard_map/columns_ghosts1/pallas_call | solution.py:483
  8.4 3.3 %collective-permute-done.4.other = f32[56,128]{1,0:T(8,128)S(1)} collective-permute-done((f32[56,128]{1,0:T(8,128)S(1)}, f32[56,128]{1,0:T(8,128)S(1)}, u32[]{:S(2)}, u32[]{:S(2)}) %collective-permute-start.4) | collective-permute-done | bytes 28704 | tf_op jit(solution)/shard_map/ppermute | solution.py:462
  11.7 0.4 %columns_ghosts0.1.packed2 = f32[96,128]{1,0:T(8,128)S(1)} custom-call(f32[80,128]{1,0:T(8,128)S(1)} %get-tuple-element.29.edges, f32[56,128]{1,0:T(8,128)S(1)} %collective-permute-done.4.other, f32[16,128]{1,0:T(8,128)S(1)} %get-tuple-element.19.inv_dx, f32[16,128]{1,0:T(8,128)S(1)} %get-tuple-element.21.spread), custom_call_target="tpu_custom_call" | custom-call | flops 1250000000 | bytes 1 | tf_op jit(solution)/shard_map/columns_ghosts0/pallas_call | solution.py:483
  12.1 0.0 collective-permute-done.2.got2
  12.1 0.0 collective-permute-done.got0
  12.1 0.0 collective-permute-done.1.got1
  12.1 1.7 %finish.1 = (f32[640,128]{1,0:T(8,128)}, f32[640,128]{1,0:T(8,128)}, f32[640,128]{1,0:T(8,128)}, f32[3,640,128]{2,1,0:T(8,128)S(1)}) custom-call(f32[3,640,128]{2,1,0:T(8,128)S(1)} %interior.1.prov_in, f32[3,640,128]{2,1,0:T(8,128)S(1)} %get-tuple-element.24.solve, f32[16,128]{1,0:T(8,128)S(1)} %get-tuple-element.25.middle, ...), custom_call_target="tpu_custom_call", output_to_operand_aliasing={{3}: (0, {})} | custom-call | flops 1 | bytes 1 | tf_op jit(solution)/shard_map/finish/pallas_call | solution.py:494
Async XLA Ops:
  0.6 1.2 %copy-start.3 = (s32[40,16,128]{2,1,0:T(8,128)S(1)}, s32[40,16,128]{2,1,0:T(8,128)}, u32[]{:S(2)}) copy-start(s32[40,16,128]{2,1,0:T(8,128)} %mask.1) | copy-start | bytes 983044
  0.6 1.2 %copy-start.2 = (f32[40,16,128]{2,1,0:T(8,128)S(1)}, f32[40,16,128]{2,1,0:T(8,128)}, u32[]{:S(2)}) copy-start(f32[40,16,128]{2,1,0:T(8,128)} %vvel.1) | copy-start | bytes 983044
  0.7 1.3 %copy-start.1 = (f32[40,16,128]{2,1,0:T(8,128)S(1)}, f32[40,16,128]{2,1,0:T(8,128)}, u32[]{:S(2)}) copy-start(f32[40,16,128]{2,1,0:T(8,128)} %uvel.1) | copy-start | bytes 983044
  0.7 1.4 %copy-start = (f32[40,16,128]{2,1,0:T(8,128)S(1)}, f32[40,16,128]{2,1,0:T(8,128)}, u32[]{:S(2)}) copy-start(f32[40,16,128]{2,1,0:T(8,128)} %temp.1) | copy-start | bytes 983044
  1.7 10.4 %collective-permute-start = (f32[288,128]{1,0:T(8,128)S(1)}, f32[288,128]{1,0:T(8,128)S(1)}, u32[]{:S(2)}, u32[]{:S(2)}) collective-permute-start(f32[288,128]{1,0:T(8,128)S(1)} %get-tuple-element.26.after), channel_id=1, source_target_pairs={{0,8},{8,0},{1,9},{9,1},{2,10},{10,2},{3,11},{11,3},{4,12},{12,4},... | collective-permute-start | bytes 442376 | tf_op jit(solution)/shard_map/ppermute | solution.py:441
  2.0 4.3 %copy-start.4 = (f32[40,16,128]{2,1,0:T(8,128)S(1)}, f32[40,16,128]{2,1,0:T(8,128)}, u32[]{:S(2)}) copy-start(f32[40,16,128]{2,1,0:T(8,128)} %param.13) | copy-start | bytes 983044
  2.6 9.5 %collective-permute-start.1 = (f32[288,128]{1,0:T(8,128)S(1)}, f32[288,128]{1,0:T(8,128)S(1)}, u32[]{:S(2)}, u32[]{:S(2)}) collective-permute-start(f32[288,128]{1,0:T(8,128)S(1)} %get-tuple-element.27), channel_id=1, source_target_pairs={{8,16},{16,8},{9,17},{17,9},{10,18},{18,10},{11,19},{19,11},{12,20... | collective-permute-start | bytes 442376 | tf_op jit(solution)/shard_map/ppermute | solution.py:460
  3.0 8.7 %collective-permute-start.4 = (f32[56,128]{1,0:T(8,128)S(1)}, f32[56,128]{1,0:T(8,128)S(1)}, u32[]{:S(2)}, u32[]{:S(2)}) collective-permute-start(f32[56,128]{1,0:T(8,128)S(1)} %get-tuple-element.31), channel_id=1, source_target_pairs={{1,2},{2,1},{3,4},{4,3},{5,6},{6,5},{7,0},{0,7},{9,10},{10,9},{11,... | collective-permute-start | bytes 86024 | tf_op jit(solution)/shard_map/ppermute | solution.py:462
  4.3 7.8 %collective-permute-start.2 = (f32[280,128]{1,0:T(8,128)S(1)}, f32[280,128]{1,0:T(8,128)S(1)}, u32[]{:S(2)}, u32[]{:S(2)}) collective-permute-start(f32[280,128]{1,0:T(8,128)S(1)} %get-tuple-element.28), channel_id=1, source_target_pairs={{16,24},{24,16},{17,25},{25,17},{18,26},{26,18},{19,27},{27,19},{2... | collective-permute-start | bytes 430088 | tf_op jit(solution)/shard_map/ppermute | solution.py:461
  4.9 3.1 %collective-permute-start.3 = (f32[48,128]{1,0:T(8,128)S(1)}, f32[48,128]{1,0:T(8,128)S(1)}, u32[]{:S(2)}, u32[]{:S(2)}) collective-permute-start(f32[48,128]{1,0:T(8,128)S(1)} %get-tuple-element.30), channel_id=1, source_target_pairs={{0,1},{1,0},{2,3},{3,2},{4,5},{5,4},{6,7},{7,6},{8,9},{9,8},{10,11... | collective-permute-start | bytes 73736 | tf_op jit(solution)/shard_map/ppermute | solution.py:463

commit v9 on v8

--- a/solution.py
+++ b/solution.py
@@ -1,5 +1,3 @@
-import functools
-
 import jax
 import jax.numpy as jnp
 from jax import lax
@@ -80,17 +78,21 @@
     return slabs
 
 
-def edges_pack_kernel(temp, uvel, vvel, mask, after, second, third, zonal1, zonal2, edges):
+def edges_pack_kernel(
+    temp, uvel, vvel, mask, after, second, third, zonal1, zonal2, edges, south, north
+):
     depth = temp.shape[0] // ROWS
-    for exchange, out in ((1, second), (2, third)):
-        north = sends_north(exchange)
-        near = (ROWS - 1) * north
-        far = near + 1 - 2 * north
+    for near, out in ((0, south), (ROWS - 1, north)):
+        far = 1 if near == 0 else near - 1
         for number, field in enumerate((temp, uvel, vvel)):
             base = 2 * depth * number
             out[base : base + depth, :] = field[level_rows(near, depth), :]
             out[base + depth : base + 2 * depth, :] = field[level_rows(far, depth), :]
         out[6 * depth : 7 * depth, :] = mask[level_rows(near, depth), :].astype(jnp.float32)
+        out[7 * depth :, :] = mask[level_rows(far, depth), :].astype(jnp.float32)
+    sent = slice(0, 7 * depth)
+    for exchange, out in ((1, second), (2, third)):
+        out[sent, :] = jnp.where(sends_north(exchange) == 1, north[sent, :], south[sent, :])
     second[7 * depth :, :] = jnp.zeros((TILE, LANES), jnp.float32)
     slabs = own_slabs((temp, uvel, vvel, mask), depth)
     for number, slab in enumerate(slabs):
@@ -136,7 +138,7 @@
     middle[...] = 1.0 / (1.0 - chains[0] * chains[1])
 
 
-def interior_kernel(temp, uvel, vvel, mask, inv_dx, inv_dy, spread, coriolis, prov):
+def interior_kernel(temp, uvel, vvel, mask, inv_dx, inv_dy, spread, coriolis, prov, zeros):
     depth = temp.shape[0] // ROWS
     lane = lane_index(ROWS)
     row = lax.broadcasted_iota(jnp.int32, (ROWS, LANES), 0)
@@ -199,33 +201,33 @@
             if index == 2:
                 total -= wet_turn * u
             prov[index, here, :] = total
-
-
-def add_row_ghosts(prov, fields, mask, ghost, near, inv_dy, spread, flip):
-    depth = prov.shape[1] // ROWS
+            zeros[index, here, :] = jnp.zeros((ROWS, LANES), jnp.float32)
+
+
+def put_row_ghosts(extra, mine, ghost, near, inv_dy, spread, flip):
+    depth = extra.shape[1] // ROWS
     far, side = (1, 1.0) if near == 0 else (near - 1, -1.0)
-    at_near, at_far = level_rows(near, depth), level_rows(far, depth)
-    wet = mask[at_near, :].astype(jnp.float32)
+    wet = piece(mine, 6, depth)
     face = piece(ghost, 6, depth) * wet
-    face_next = wet * mask[at_far, :].astype(jnp.float32)
+    face_next = wet * piece(mine, 7, depth)
     inv0 = inv_dy[near : near + 1, :]
-    inv1 = inv_dy[far : far + 1, :] * side
+    inv1 = inv_dy[far : far + 1, :] * -side
     mix0 = spread[near : near + 1, :] * inv0 * inv0
     inv0 = inv0 * side
-    v0 = fields[2][at_near, :]
+    v0 = piece(mine, 4, depth)
     speed = face * (piece(ghost, 4, depth) * flip + v0) * (1.0 / 24.0)
-    speed_next = face_next * (v0 + fields[2][at_far, :]) * (1.0 / 24.0)
+    speed_next = face_next * (v0 + piece(mine, 5, depth)) * (1.0 / 24.0)
     for number in range(3):
         sign = 1.0 if number == 0 else flip
         g0 = piece(ghost, 2 * number, depth) * sign
         g1 = piece(ghost, 2 * number + 1, depth) * sign
-        o0 = fields[number][at_near, :]
-        o1 = fields[number][at_far, :]
+        o0 = piece(mine, 2 * number, depth)
+        o1 = piece(mine, 2 * number + 1, depth)
         advect = speed * (7.0 * (g0 + o0) - (g1 + o1))
         reach = speed_next * g0
-        view = prov.at[number]
-        view[at_near, :] += inv0 * (advect + reach) + mix0 * (face * (g0 - o0))
-        view[at_far, :] -= inv1 * reach
+        view = extra.at[number]
+        view[level_rows(near, depth), :] = inv0 * (advect + reach) + mix0 * (face * (g0 - o0))
+        view[level_rows(far, depth), :] = inv1 * reach
 
 
 def column_ghosts(edges, other, west, inv_dx, spread):
@@ -284,8 +286,12 @@
     return jnp.where(border, turn_lanes(source, -(start + 2)), 0.0)
 
 
-def columns_ghosts_kernel(parity, edges, other, inv_dx, spread, out):
-    west = lax.rem(lax.axis_index("lon"), 2) == parity
+def arrived_kernel(other, out):
+    out[:TILE, :] = other[:TILE, :]
+
+
+def columns_ghosts_kernel(edges, other, inv_dx, spread, out):
+    west = lax.rem(lax.axis_index("lon"), 2) == 1
     for part, slabs in enumerate(column_ghosts(edges, other, west, inv_dx, spread)):
         for field in range(3):
             place = (3 * part + field) * ROWS
@@ -293,8 +299,8 @@
 
 
 def finish_kernel(
-    prov_in, solve, middle, temp, uvel, vvel, mask, got0, got1, got2, packed1, packed2,
-    inv_dy, spread, temp_new, uvel_new, vvel_new, prov, work, south, north, sems
+    prov, extra_in, solve, middle, own_south, own_north, got0, got1, got2, edges, packed, second,
+    inv_dx, inv_dy, spread, temp_new, uvel_new, vvel_new, extra, work, south, north, sems
 ):
     depth = prov.shape[1] // ROWS
     half = depth // 2
@@ -307,20 +313,21 @@
             exchange == 0, got0[used, :], jnp.where(exchange == 1, got1[used, :], got2[used, :])
         )
 
+    odd = lax.rem(lax.axis_index("lon"), 2)
+    columns = column_ghosts(edges, second, odd == 0, inv_dx, spread)
     lane = lane_index(7 * depth)
     lane = jnp.where(fold, LANES - 1 - lane, lane)
     north[...] = jnp.take_along_axis(received(lax.rem(lat, 3)), lane, axis=1, mode="promise_in_bounds")
     south[...] = jnp.where(lat == 0, 0.0, received(lax.rem(lat + 2, 3)))
     flip = jnp.where(fold, -1.0, 1.0)
-    fields = (temp, uvel, vvel)
-    add_row_ghosts(prov, fields, mask, south, 0, inv_dy, spread, 1.0)
-    add_row_ghosts(prov, fields, mask, north, ROWS - 1, inv_dy, spread, flip)
+    put_row_ghosts(extra, own_south, south, 0, inv_dy, spread, 1.0)
+    put_row_ghosts(extra, own_north, north, ROWS - 1, inv_dy, spread, flip)
 
     lane = lane_index(ROWS)
-    from_first = lane % 4 // 2 == lax.rem(lax.axis_index("lon"), 2)
+    from_first = lane % 4 // 2 == odd
     corrections = [
-        [jnp.where(from_first, level(packed1, place), level(packed2, place)) for place in range(part, part + 3)]
-        for part in (0, 3)
+        [jnp.where(from_first, level(packed, 3 * part + f), columns[part][f]) for f in range(3)]
+        for part in range(2)
     ]
     border = (lane < 2) | (lane >= LANES - 2)
 
@@ -336,7 +343,7 @@
             here = slice(number * ROWS, (number + 1) * ROWS)
             inverse, carry = solve[0, here, :], solve[1, here, :]
             for field in range(3):
-                known = prov[field, here, :] + border_part(number, field)
+                known = prov[field, here, :] + (extra[field, here, :] + border_part(number, field))
                 value = inverse * known + carry * values[side][field]
                 values[side][field] = value
                 work[field, here, :] = value
@@ -442,7 +449,7 @@
     temp, uvel, vvel, vert_mixing, wet_mask = (
         x.reshape(flat, lanes) for x in (temp, uvel, vvel, vert_mixing, wet_mask)
     )
-    sent1, sent2, zonal1, zonal2, edges = pl.pallas_call(
+    sent1, sent2, zonal1, zonal2, edges, own_south, own_north = pl.pallas_call(
         edges_pack_kernel,
         name="edges_pack",
         out_shape=(
@@ -451,9 +458,11 @@
             f32(3 * rows, lanes),
             f32(3 * rows + TILE, lanes),
             f32((TAIL + 1) * rows, lanes),
+            f32(8 * depth, lanes),
+            f32(8 * depth, lanes),
         ),
         in_specs=[VMEM] * 4 + [pl.BlockSpec(memory_space=pl.ANY)],
-        out_specs=(VMEM,) * 5,
+        out_specs=(VMEM,) * 7,
         compiler_params=limit,
         cost_estimate=cheap,
     )(temp, uvel, vvel, wet_mask, sent0)
@@ -470,34 +479,41 @@
         compiler_params=limit,
         cost_estimate=cheap,
     )(vert_mixing, levels)
-    prov = pl.pallas_call(
+    prov, zeros = pl.pallas_call(
         interior_kernel,
         name="interior",
-        out_shape=f32(3, flat, lanes),
+        out_shape=(f32(3, flat, lanes),) * 2,
         in_specs=[VMEM] * 8,
-        out_specs=VMEM,
+        out_specs=(VMEM,) * 2,
         compiler_params=limit,
         cost_estimate=cheap,
     )(temp, uvel, vvel, wet_mask, inv_dx, inv_dy, horiz_mixing, coriolis)
-    packed1, packed2 = (
-        pl.pallas_call(
-            functools.partial(columns_ghosts_kernel, parity),
-            name="columns_ghosts" + str(parity),
-            out_shape=f32(6 * rows, lanes),
-            in_specs=[VMEM] * 4,
-            out_specs=VMEM,
-            compiler_params=limit,
-            cost_estimate=cost,
-        )(edges, other, inv_dx, horiz_mixing)
-        for parity, other, cost in ((1, first, cheap), (0, second, pl.CostEstimate(flops=1250000000, bytes_accessed=1, transcendentals=0)))
-    )
+    packed = pl.pallas_call(
+        columns_ghosts_kernel,
+        name="columns_ghosts",
+        out_shape=f32(6 * rows, lanes),
+        in_specs=[VMEM] * 4,
+        out_specs=VMEM,
+        compiler_params=limit,
+        cost_estimate=cheap,
+    )(edges, first, inv_dx, horiz_mixing)
+    second = pl.pallas_call(
+        arrived_kernel,
+        name="arrived",
+        out_shape=f32(3 * rows + TILE, lanes),
+        in_specs=[VMEM],
+        out_specs=VMEM,
+        input_output_aliases={0: 0},
+        compiler_params=limit,
+        cost_estimate=pl.CostEstimate(flops=1250000000, bytes_accessed=1, transcendentals=0),
+    )(second)
     outs = pl.pallas_call(
         finish_kernel,
         name="finish",
         out_shape=(f32(flat, lanes),) * 3 + (f32(3, flat, lanes),),
-        in_specs=[VMEM] * 14,
+        in_specs=[VMEM] * 15,
         out_specs=(HBM,) * 3 + (VMEM,),
-        input_output_aliases={0: 3},
+        input_output_aliases={1: 3},
         scratch_shapes=[
             vmem(3, flat, lanes),
             vmem(7 * depth, lanes),
@@ -507,8 +523,8 @@
         compiler_params=limit,
         cost_estimate=cheap,
     )(
-        prov, solve, middle, temp, uvel, vvel, wet_mask, got0, got1, got2, packed1, packed2,
-        inv_dy, horiz_mixing,
+        prov, zeros, solve, middle, own_south, own_north, got0, got1, got2, edges, packed, second,
+        inv_dx, inv_dy, horiz_mixing,
     )
     return tuple(x.reshape(depth, rows, lanes) for x in outs[:3])
 

time: 14 us -> 13.9 us (level)
  the two profiles are of different devices: /device:TPU:22 before, /device:TPU:4 now
where the time goes in v9:
time: 13.9 us; the launch traced here: 13.7 us
  Pallas kernels  5.44 us (39%)
  starting transfers between devices  5.3 us (38%)
  waiting for transfers between devices  2.04 us (15%)
  between operations  0.73 us (5%)
  local copies, waits for them, and re-layouts  0.22 us (2%)
    ppermute x1, starting transfers between devices, per_device(): second = lax.ppermute(zonal2, both, zonal_second)  2.81 us
    ppermute x1, waiting for transfers between devices, per_device(): got2 = lax.ppermute(sent2, both, meridional[2])  2.03 us
    pallas_call x1, Pallas kernels, per_device(): pl.pallas_call(finish_kernel, name='finish', out_shape=(f32(flat, lanes),...  1.81 us
    pallas_call x1, Pallas kernels, per_device(): pl.pallas_call(interior_kernel, name='interior', out_shape=(f32(3, flat,...  1.48 us
    ppermute x1, starting transfers between devices, per_device(): got1 = lax.ppermute(sent1, both, meridional[1])  1.45 us
    pallas_call x1, Pallas kernels, per_device(): pl.pallas_call(first_rows_kernel, name='first_rows', out_shape=(f32(7 * d...  1.04 us
    ppermute x1, starting transfers between devices, per_device(): got2 = lax.ppermute(sent2, both, meridional[2])  0.97 us
    pallas_call x1, Pallas kernels, per_device(): pl.pallas_call(edges_pack_kernel, name='edges_pack', out_shape=(f32(7 * d...  0.54 us
  transfers between devices with their start and end apart: 5, of which 1 were waited for; matrix products, arithmetic and copies ran while one was open for 0% of the time, Pallas kernels for 19%

profile of v9, /device:TPU:4, one launch (start us, length us, event | category | flops | bytes accessed | tf_op | source)
XLA Modules:
  0.0 13.7 jit_solution(9421471628999909152)
XLA Ops:
  0.6 0.0 copy-start.3
  0.6 0.0 copy-start.2
  0.7 0.0 copy-start.1
  0.7 0.0 copy-start
  0.7 1.0 %first_rows.1 = (f32[288,128]{1,0:T(8,128)S(1)}, f32[16,128]{1,0:T(8,128)S(1)}, f32[16,128]{1,0:T(8,128)S(1)}, f32[16,128]{1,0:T(8,128)S(1)}, f32[16,128]{1,0:T(8,128)S(1)}, /*index=5*/s32[16,128]{1,0:T(8,128)S(1)}) custom-call(f32[40,16,128]{2,1,0:T(8,128)} %temp.1, f32[40,16,128]{2,1,0:T(8,128)} %uvel.1, f32[40,16,128]{2,1,0:T(8,128)} %vvel.1, ...), custom_call_target="tpu_custom_call" | custom-call | flops 1 | bytes 1 | tf_op jit(solution)/shard_map/first_rows/pallas_call | solution.py:436
  1.7 0.1 collective-permute-start
  1.8 0.0 copy-done.3
  1.8 0.0 copy-done.2
  1.8 0.1 copy-done.1
  1.9 0.1 copy-done
  2.0 0.0 copy-start.4
  2.0 0.5 %edges_pack.1 = (f32[288,128]{1,0:T(8,128)S(1)}, f32[280,128]{1,0:T(8,128)S(1)}, f32[48,128]{1,0:T(8,128)S(1)}, f32[56,128]{1,0:T(8,128)S(1)}, f32[80,128]{1,0:T...) custom-call(f32[640,128]{1,0:T(8,128)S(1)} %bitcast.8, f32[640,128]{1,0:T(8,128)S(1)} %bitcast.10, ...), custom_call_target="tpu_custom_call" | custom-call | flops 1 | bytes 1 | tf_op jit(solution)/shard_map/edges_pack/pallas_call | solution.py:452
  2.6 1.5 %collective-permute-start.1 = (f32[288,128]{1,0:T(8,128)S(1)}, f32[288,128]{1,0:T(8,128)S(1)}, u32[]{:S(2)}, u32[]{:S(2)}) collective-permute-start(f32[288,128]{1,0:T(8,128)S(1)} %get-tuple-element.35), channel_id=1, source_target_pairs={{8,16},{16,8},{9,17},{17,9},{10,18},{18,10},{11,19},{19,11},{12,20... | collective-permute-start | bytes 442376 | tf_op jit(solution)/shard_map/ppermute | solution.py:469
  4.0 2.8 %collective-permute-start.4 = (f32[56,128]{1,0:T(8,128)S(1)}, f32[56,128]{1,0:T(8,128)S(1)}, u32[]{:S(2)}, u32[]{:S(2)}) collective-permute-start(f32[56,128]{1,0:T(8,128)S(1)} %get-tuple-element.39), channel_id=1, source_target_pairs={{1,2},{2,1},{3,4},{4,3},{5,6},{6,5},{7,0},{0,7},{9,10},{10,9},{11,... | collective-permute-start | bytes 86024 | tf_op jit(solution)/shard_map/ppermute | solution.py:471
  6.8 1.0 %collective-permute-start.2 = (f32[280,128]{1,0:T(8,128)S(1)}, f32[280,128]{1,0:T(8,128)S(1)}, u32[]{:S(2)}, u32[]{:S(2)}) collective-permute-start(f32[280,128]{1,0:T(8,128)S(1)} %get-tuple-element.36), channel_id=1, source_target_pairs={{16,24},{24,16},{17,25},{25,17},{18,26},{26,18},{19,27},{27,19},{2... | collective-permute-start | bytes 430088 | tf_op jit(solution)/shard_map/ppermute | solution.py:470
  7.8 0.0 collective-permute-start.3
  7.8 0.0 copy-done.4
  7.8 0.2 %columns.1 = (f32[3,640,128]{2,1,0:T(8,128)S(1)}, f32[16,128]{1,0:T(8,128)S(1)}) custom-call(f32[640,128]{1,0:T(8,128)S(1)} %bitcast.16, s32[16,128]{1,0:T(8,128)S(1)} %get-tuple-element.29.levels), custom_call_target="tpu_custom_call" | custom-call | flops 1 | bytes 1 | tf_op jit(solution)/shard_map/columns/pallas_call | solution.py:473
  8.0 1.5 %interior.1 = (f32[3,640,128]{2,1,0:T(8,128)S(1)}, f32[3,640,128]{2,1,0:T(8,128)S(1)}) custom-call(f32[640,128]{1,0:T(8,128)S(1)} %bitcast.9, f32[640,128]{1,0:T(8,128)S(1)} %bitcast.11, f32[640,128]{1,0:T(8,128)S(1)} %bitcast.13, s32[640,128]{1,0:T(8,128)S(1)} %bitcast.15, f32[16,128]{1,0:T(8,128)S(1)} %get-tuple-element.23.inv_dx, ...), custom_call_target="tpu_custom_call" | custom-call | flops 1 | bytes 1 | tf_op jit(solution)/shard_map/interior/pallas_call | solution.py:482
  9.5 0.0 collective-permute-done.3.other
  9.5 0.4 %columns_ghosts.1.packed = f32[96,128]{1,0:T(8,128)S(1)} custom-call(f32[80,128]{1,0:T(8,128)S(1)} %get-tuple-element.37.edges, f32[48,128]{1,0:T(8,128)S(1)} %collective-permute-done.3.other, f32[16,128]{1,0:T(8,128)S(1)} %get-tuple-element.23.inv_dx, f32[16,128]{1,0:T(8,128)S(1)} %get-tuple-element.25.spread), custom_call_target="tpu_custom_call" | custom-call | flops 1 | bytes 1 | tf_op jit(solution)/shard_map/columns_ghosts/pallas_call | solution.py:491
  9.9 0.0 collective-permute-done.4.other
  9.9 2.0 %collective-permute-done.2.got2 = f32[280,128]{1,0:T(8,128)S(1)} collective-permute-done((f32[280,128]{1,0:T(8,128)S(1)}, f32[280,128]{1,0:T(8,128)S(1)}, u32[]{:S(2)}, u32[]{:S(2)}) %collective-permute-start.2) | collective-permute-done | bytes 143392 | tf_op jit(solution)/shard_map/ppermute | solution.py:470
  11.9 0.0 collective-permute-done.got0
  11.9 0.0 collective-permute-done.1.got1
  11.9 1.8 %finish.1 = (f32[640,128]{1,0:T(8,128)}, f32[640,128]{1,0:T(8,128)}, f32[640,128]{1,0:T(8,128)}, f32[3,640,128]{2,1,0:T(8,128)S(1)}) custom-call(f32[3,640,128]{2,1,0:T(8,128)S(1)} %get-tuple-element.27.prov, f32[3,640,128]{2,1,0:T(8,128)S(1)} %get-tuple-element.28.extra_in, ...), custom_call_target="tpu_custom_call", output_to_operand_aliasing={{3}: (1, {})} | custom-call | flops 1 | bytes 1 | tf_op jit(solution)/shard_map/finish/pallas_call | solution.py:510
  (1 shorter events, 0.0 us)
Async XLA Ops:
  0.6 1.2 %copy-start.3 = (s32[40,16,128]{2,1,0:T(8,128)S(1)}, s32[40,16,128]{2,1,0:T(8,128)}, u32[]{:S(2)}) copy-start(s32[40,16,128]{2,1,0:T(8,128)} %mask.1) | copy-start | bytes 983044
  0.6 1.2 %copy-start.2 = (f32[40,16,128]{2,1,0:T(8,128)S(1)}, f32[40,16,128]{2,1,0:T(8,128)}, u32[]{:S(2)}) copy-start(f32[40,16,128]{2,1,0:T(8,128)} %vvel.1) | copy-start | bytes 983044
  0.7 1.3 %copy-start.1 = (f32[40,16,128]{2,1,0:T(8,128)S(1)}, f32[40,16,128]{2,1,0:T(8,128)}, u32[]{:S(2)}) copy-start(f32[40,16,128]{2,1,0:T(8,128)} %uvel.1) | copy-start | bytes 983044
  0.7 1.4 %copy-start = (f32[40,16,128]{2,1,0:T(8,128)S(1)}, f32[40,16,128]{2,1,0:T(8,128)}, u32[]{:S(2)}) copy-start(f32[40,16,128]{2,1,0:T(8,128)} %temp.1) | copy-start | bytes 983044
  1.7 10.2 %collective-permute-start = (f32[288,128]{1,0:T(8,128)S(1)}, f32[288,128]{1,0:T(8,128)S(1)}, u32[]{:S(2)}, u32[]{:S(2)}) collective-permute-start(f32[288,128]{1,0:T(8,128)S(1)} %get-tuple-element.32.after), channel_id=1, source_target_pairs={{0,8},{8,0},{1,9},{9,1},{2,10},{10,2},{3,11},{11,3},{4,12},{12,4},... | collective-permute-start | bytes 442376 | tf_op jit(solution)/shard_map/ppermute | solution.py:448
  2.0 5.8 %copy-start.4 = (f32[40,16,128]{2,1,0:T(8,128)S(1)}, f32[40,16,128]{2,1,0:T(8,128)}, u32[]{:S(2)}) copy-start(f32[40,16,128]{2,1,0:T(8,128)} %param.13) | copy-start | bytes 983044
  2.6 9.4 %collective-permute-start.1 = (f32[288,128]{1,0:T(8,128)S(1)}, f32[288,128]{1,0:T(8,128)S(1)}, u32[]{:S(2)}, u32[]{:S(2)}) collective-permute-start(f32[288,128]{1,0:T(8,128)S(1)} %get-tuple-element.35), channel_id=1, source_target_pairs={{8,16},{16,8},{9,17},{17,9},{10,18},{18,10},{11,19},{19,11},{12,20... | collective-permute-start | bytes 442376 | tf_op jit(solution)/shard_map/ppermute | solution.py:469
  4.0 5.9 %collective-permute-start.4 = (f32[56,128]{1,0:T(8,128)S(1)}, f32[56,128]{1,0:T(8,128)S(1)}, u32[]{:S(2)}, u32[]{:S(2)}) collective-permute-start(f32[56,128]{1,0:T(8,128)S(1)} %get-tuple-element.39), channel_id=1, source_target_pairs={{1,2},{2,1},{3,4},{4,3},{5,6},{6,5},{7,0},{0,7},{9,10},{10,9},{11,... | collective-permute-start | bytes 86024 | tf_op jit(solution)/shard_map/ppermute | solution.py:471
  6.8 5.1 %collective-permute-start.2 = (f32[280,128]{1,0:T(8,128)S(1)}, f32[280,128]{1,0:T(8,128)S(1)}, u32[]{:S(2)}, u32[]{:S(2)}) collective-permute-start(f32[280,128]{1,0:T(8,128)S(1)} %get-tuple-element.36), channel_id=1, source_target_pairs={{16,24},{24,16},{17,25},{25,17},{18,26},{26,18},{19,27},{27,19},{2... | collective-permute-start | bytes 430088 | tf_op jit(solution)/shard_map/ppermute | solution.py:470
  7.8 1.7 %collective-permute-start.3 = (f32[48,128]{1,0:T(8,128)S(1)}, f32[48,128]{1,0:T(8,128)S(1)}, u32[]{:S(2)}, u32[]{:S(2)}) collective-permute-start(f32[48,128]{1,0:T(8,128)S(1)} %get-tuple-element.38), channel_id=1, source_target_pairs={{0,1},{1,0},{2,3},{3,2},{4,5},{5,4},{6,7},{7,6},{8,9},{9,8},{10,11... | collective-permute-start | bytes 73736 | tf_op jit(solution)/shard_map/ppermute | solution.py:472

commit v10 on v9

--- a/solution.py
+++ b/solution.py
@@ -9,7 +9,7 @@
 LANES = 128
 TILE = 8
 TAIL = 4
-STORE_AFTER = (4, 11, 19)
+STORE_AFTER = ((9, 19), (9, 19), (9, 19))
 VMEM = pl.BlockSpec(memory_space=pltpu.VMEM)
 HBM = pl.BlockSpec(memory_space=pltpu.HBM)
 
@@ -204,7 +204,7 @@
             zeros[index, here, :] = jnp.zeros((ROWS, LANES), jnp.float32)
 
 
-def put_row_ghosts(extra, mine, ghost, near, inv_dy, spread, flip):
+def row_ghosts(extra, mine, ghost, near, inv_dy, spread, flip):
     depth = extra.shape[1] // ROWS
     far, side = (1, 1.0) if near == 0 else (near - 1, -1.0)
     wet = piece(mine, 6, depth)
@@ -217,7 +217,8 @@
     v0 = piece(mine, 4, depth)
     speed = face * (piece(ghost, 4, depth) * flip + v0) * (1.0 / 24.0)
     speed_next = face_next * (v0 + piece(mine, 5, depth)) * (1.0 / 24.0)
-    for number in range(3):
+
+    def put(number):
         sign = 1.0 if number == 0 else flip
         g0 = piece(ghost, 2 * number, depth) * sign
         g1 = piece(ghost, 2 * number + 1, depth) * sign
@@ -228,6 +229,8 @@
         view = extra.at[number]
         view[level_rows(near, depth), :] = inv0 * (advect + reach) + mix0 * (face * (g0 - o0))
         view[level_rows(far, depth), :] = inv1 * reach
+
+    return put
 
 
 def column_ghosts(edges, other, west, inv_dx, spread):
@@ -320,8 +323,8 @@
     north[...] = jnp.take_along_axis(received(lax.rem(lat, 3)), lane, axis=1, mode="promise_in_bounds")
     south[...] = jnp.where(lat == 0, 0.0, received(lax.rem(lat + 2, 3)))
     flip = jnp.where(fold, -1.0, 1.0)
-    put_row_ghosts(extra, own_south, south, 0, inv_dy, spread, 1.0)
-    put_row_ghosts(extra, own_north, north, ROWS - 1, inv_dy, spread, flip)
+    put_south = row_ghosts(extra, own_south, south, 0, inv_dy, spread, 1.0)
+    put_north = row_ghosts(extra, own_north, north, ROWS - 1, inv_dy, spread, flip)
 
     lane = lane_index(ROWS)
     from_first = lane % 4 // 2 == odd
@@ -337,53 +340,40 @@
 
     outs = (temp_new, uvel_new, vvel_new)
     zero = jnp.zeros((ROWS, LANES), jnp.float32)
-    values = [[zero] * 3, [zero] * 3]
-    for step in range(half):
-        for side, number in enumerate((step, depth - 1 - step)):
-            here = slice(number * ROWS, (number + 1) * ROWS)
-            inverse, carry = solve[0, here, :], solve[1, here, :]
-            for field in range(3):
+    above, below = half - 1, half
+    copies = []
+    for field in range(3):
+        put_south(field)
+        put_north(field)
+        values = [zero, zero]
+        for step in range(half):
+            for side, number in enumerate((step, depth - 1 - step)):
+                here = slice(number * ROWS, (number + 1) * ROWS)
                 known = prov[field, here, :] + (extra[field, here, :] + border_part(number, field))
-                value = inverse * known + carry * values[side][field]
-                values[side][field] = value
-                work[field, here, :] = value
-    above, below = half - 1, half
-    gain = level(solve.at[2], above)
-    scale = middle[...]
-    tops = [scale * (values[0][field] + gain * values[1][field]) for field in range(3)]
-    for field in range(3):
-        work[field, above * ROWS : (above + 1) * ROWS, :] = tops[field]
-    chains = [list(tops), list(tops)]
-    copies = []
-
-    def store(start, stop):
-        rows = pl.ds(start * ROWS, (stop - start) * ROWS)
-        for field in range(3):
-            copy = pltpu.make_async_copy(
-                work.at[field, rows, :], outs[field].at[rows, :], sems.at[len(copies)]
-            )
-            copy.start()
-            copies.append(copy)
-
-    low, high = half, half
-    for step in range(half):
-        for side, number in enumerate((above - 1 - step, below + step)):
-            if number < 0:
-                continue
-            here = slice(number * ROWS, (number + 1) * ROWS)
-            gain = solve[2, here, :]
-            for field in range(3):
-                value = work[field, here, :] + gain * chains[side][field]
-                chains[side][field] = value
-                work[field, here, :] = value
-        if step in STORE_AFTER:
-            start, stop = max(above - 1 - step, 0), below + step + 1
-            if low == high:
-                store(start, stop)
-            else:
-                store(start, low)
-                store(high, stop)
-            low, high = start, stop
+                values[side] = solve[0, here, :] * known + solve[1, here, :] * values[side]
+                work[field, here, :] = values[side]
+        gain = level(solve.at[2], above)
+        top = middle[...] * (values[0] + gain * values[1])
+        work[field, above * ROWS : (above + 1) * ROWS, :] = top
+        chains = [top, top]
+        low, high = half, half
+        for step in range(half):
+            for side, number in enumerate((above - 1 - step, below + step)):
+                if number < 0:
+                    continue
+                here = slice(number * ROWS, (number + 1) * ROWS)
+                chains[side] = work[field, here, :] + solve[2, here, :] * chains[side]
+                work[field, here, :] = chains[side]
+            if step in STORE_AFTER[field]:
+                start, stop = max(above - 1 - step, 0), below + step + 1
+                for first, last in ((start, stop),) if low == high else ((start, low), (high, stop)):
+                    rows = pl.ds(first * ROWS, (last - first) * ROWS)
+                    copy = pltpu.make_async_copy(
+                        work.at[field, rows, :], outs[field].at[rows, :], sems.at[len(copies)]
+                    )
+                    copy.start()
+                    copies.append(copy)
+                low, high = start, stop
     for copy in copies:
         copy.wait()
 

time: 13.9 us -> 13.8 us (level)
  no operation moved by 1% of the time
where the time goes in v10:
time: 13.8 us; the launch traced here: 13.6 us
  Pallas kernels  5.33 us (39%)
  starting transfers between devices  5.3 us (38%)
  waiting for transfers between devices  2.04 us (15%)
  between operations  0.73 us (5%)
  local copies, waits for them, and re-layouts  0.22 us (2%)
    ppermute x1, starting transfers between devices, per_device(): second = lax.ppermute(zonal2, both, zonal_second)  2.81 us
    ppermute x1, waiting for transfers between devices, per_device(): got2 = lax.ppermute(sent2, both, meridional[2])  2.03 us
    pallas_call x1, Pallas kernels, per_device(): pl.pallas_call(finish_kernel, name='finish', out_shape=(f32(flat, lanes),...  1.7 us
    pallas_call x1, Pallas kernels, per_device(): pl.pallas_call(interior_kernel, name='interior', out_shape=(f32(3, flat,...  1.48 us
    ppermute x1, starting transfers between devices, per_device(): got1 = lax.ppermute(sent1, both, meridional[1])  1.45 us
    pallas_call x1, Pallas kernels, per_device(): pl.pallas_call(first_rows_kernel, name='first_rows', out_shape=(f32(7 * d...  1.04 us
    ppermute x1, starting transfers between devices, per_device(): got2 = lax.ppermute(sent2, both, meridional[2])  0.97 us
    pallas_call x1, Pallas kernels, per_device(): pl.pallas_call(edges_pack_kernel, name='edges_pack', out_shape=(f32(7 * d...  0.54 us
  transfers between devices with their start and end apart: 5, of which 1 were waited for; matrix products, arithmetic and copies ran while one was open for 0% of the time, Pallas kernels for 19%

profile of v10, /device:TPU:4, one launch (start us, length us, event | category | flops | bytes accessed | tf_op | source)
XLA Modules:
  0.0 13.6 jit_solution(4014763558053482454)
XLA Ops:
  0.6 0.0 copy-start.3
  0.6 0.0 copy-start.2
  0.7 0.0 copy-start.1
  0.7 0.0 copy-start
  0.7 1.0 %first_rows.1 = (f32[288,128]{1,0:T(8,128)S(1)}, f32[16,128]{1,0:T(8,128)S(1)}, f32[16,128]{1,0:T(8,128)S(1)}, f32[16,128]{1,0:T(8,128)S(1)}, f32[16,128]{1,0:T(8,128)S(1)}, /*index=5*/s32[16,128]{1,0:T(8,128)S(1)}) custom-call(f32[40,16,128]{2,1,0:T(8,128)} %temp.1, f32[40,16,128]{2,1,0:T(8,128)} %uvel.1, f32[40,16,128]{2,1,0:T(8,128)} %vvel.1, ...), custom_call_target="tpu_custom_call" | custom-call | flops 1 | bytes 1 | tf_op jit(solution)/shard_map/first_rows/pallas_call | solution.py:426
  1.7 0.1 collective-permute-start
  1.8 0.0 copy-done.3
  1.8 0.0 copy-done.2
  1.8 0.1 copy-done.1
  1.9 0.1 copy-done
  2.0 0.0 copy-start.4
  2.0 0.5 %edges_pack.1 = (f32[288,128]{1,0:T(8,128)S(1)}, f32[280,128]{1,0:T(8,128)S(1)}, f32[48,128]{1,0:T(8,128)S(1)}, f32[56,128]{1,0:T(8,128)S(1)}, f32[80,128]{1,0:T...) custom-call(f32[640,128]{1,0:T(8,128)S(1)} %bitcast.8, f32[640,128]{1,0:T(8,128)S(1)} %bitcast.10, ...), custom_call_target="tpu_custom_call" | custom-call | flops 1 | bytes 1 | tf_op jit(solution)/shard_map/edges_pack/pallas_call | solution.py:442
  2.6 1.5 %collective-permute-start.1 = (f32[288,128]{1,0:T(8,128)S(1)}, f32[288,128]{1,0:T(8,128)S(1)}, u32[]{:S(2)}, u32[]{:S(2)}) collective-permute-start(f32[288,128]{1,0:T(8,128)S(1)} %get-tuple-element.35), channel_id=1, source_target_pairs={{8,16},{16,8},{9,17},{17,9},{10,18},{18,10},{11,19},{19,11},{12,20... | collective-permute-start | bytes 442376 | tf_op jit(solution)/shard_map/ppermute | solution.py:459
  4.0 2.8 %collective-permute-start.4 = (f32[56,128]{1,0:T(8,128)S(1)}, f32[56,128]{1,0:T(8,128)S(1)}, u32[]{:S(2)}, u32[]{:S(2)}) collective-permute-start(f32[56,128]{1,0:T(8,128)S(1)} %get-tuple-element.39), channel_id=1, source_target_pairs={{1,2},{2,1},{3,4},{4,3},{5,6},{6,5},{7,0},{0,7},{9,10},{10,9},{11,... | collective-permute-start | bytes 86024 | tf_op jit(solution)/shard_map/ppermute | solution.py:461
  6.8 1.0 %collective-permute-start.2 = (f32[280,128]{1,0:T(8,128)S(1)}, f32[280,128]{1,0:T(8,128)S(1)}, u32[]{:S(2)}, u32[]{:S(2)}) collective-permute-start(f32[280,128]{1,0:T(8,128)S(1)} %get-tuple-element.36), channel_id=1, source_target_pairs={{16,24},{24,16},{17,25},{25,17},{18,26},{26,18},{19,27},{27,19},{2... | collective-permute-start | bytes 430088 | tf_op jit(solution)/shard_map/ppermute | solution.py:460
  7.8 0.0 collective-permute-start.3
  7.8 0.0 copy-done.4
  7.8 0.2 %columns.1 = (f32[3,640,128]{2,1,0:T(8,128)S(1)}, f32[16,128]{1,0:T(8,128)S(1)}) custom-call(f32[640,128]{1,0:T(8,128)S(1)} %bitcast.16, s32[16,128]{1,0:T(8,128)S(1)} %get-tuple-element.29.levels), custom_call_target="tpu_custom_call" | custom-call | flops 1 | bytes 1 | tf_op jit(solution)/shard_map/columns/pallas_call | solution.py:463
  8.0 1.5 %interior.1 = (f32[3,640,128]{2,1,0:T(8,128)S(1)}, f32[3,640,128]{2,1,0:T(8,128)S(1)}) custom-call(f32[640,128]{1,0:T(8,128)S(1)} %bitcast.9, f32[640,128]{1,0:T(8,128)S(1)} %bitcast.11, f32[640,128]{1,0:T(8,128)S(1)} %bitcast.13, s32[640,128]{1,0:T(8,128)S(1)} %bitcast.15, f32[16,128]{1,0:T(8,128)S(1)} %get-tuple-element.23.inv_dx, ...), custom_call_target="tpu_custom_call" | custom-call | flops 1 | bytes 1 | tf_op jit(solution)/shard_map/interior/pallas_call | solution.py:472
  9.5 0.0 collective-permute-done.3.other
  9.5 0.4 %columns_ghosts.1.packed = f32[96,128]{1,0:T(8,128)S(1)} custom-call(f32[80,128]{1,0:T(8,128)S(1)} %get-tuple-element.37.edges, f32[48,128]{1,0:T(8,128)S(1)} %collective-permute-done.3.other, f32[16,128]{1,0:T(8,128)S(1)} %get-tuple-element.23.inv_dx, f32[16,128]{1,0:T(8,128)S(1)} %get-tuple-element.25.spread), custom_call_target="tpu_custom_call" | custom-call | flops 1 | bytes 1 | tf_op jit(solution)/shard_map/columns_ghosts/pallas_call | solution.py:481
  9.9 0.0 collective-permute-done.4.other
  9.9 2.0 %collective-permute-done.2.got2 = f32[280,128]{1,0:T(8,128)S(1)} collective-permute-done((f32[280,128]{1,0:T(8,128)S(1)}, f32[280,128]{1,0:T(8,128)S(1)}, u32[]{:S(2)}, u32[]{:S(2)}) %collective-permute-start.2) | collective-permute-done | bytes 143392 | tf_op jit(solution)/shard_map/ppermute | solution.py:460
  11.9 0.0 collective-permute-done.got0
  11.9 0.0 collective-permute-done.1.got1
  11.9 1.7 %finish.1 = (f32[640,128]{1,0:T(8,128)}, f32[640,128]{1,0:T(8,128)}, f32[640,128]{1,0:T(8,128)}, f32[3,640,128]{2,1,0:T(8,128)S(1)}) custom-call(f32[3,640,128]{2,1,0:T(8,128)S(1)} %get-tuple-element.27.prov, f32[3,640,128]{2,1,0:T(8,128)S(1)} %get-tuple-element.28.extra_in, ...), custom_call_target="tpu_custom_call", output_to_operand_aliasing={{3}: (1, {})} | custom-call | flops 1 | bytes 1 | tf_op jit(solution)/shard_map/finish/pallas_call | solution.py:500
  (1 shorter events, 0.0 us)
Async XLA Ops:
  0.6 1.2 %copy-start.3 = (s32[40,16,128]{2,1,0:T(8,128)S(1)}, s32[40,16,128]{2,1,0:T(8,128)}, u32[]{:S(2)}) copy-start(s32[40,16,128]{2,1,0:T(8,128)} %mask.1) | copy-start | bytes 983044
  0.6 1.2 %copy-start.2 = (f32[40,16,128]{2,1,0:T(8,128)S(1)}, f32[40,16,128]{2,1,0:T(8,128)}, u32[]{:S(2)}) copy-start(f32[40,16,128]{2,1,0:T(8,128)} %vvel.1) | copy-start | bytes 983044
  0.7 1.3 %copy-start.1 = (f32[40,16,128]{2,1,0:T(8,128)S(1)}, f32[40,16,128]{2,1,0:T(8,128)}, u32[]{:S(2)}) copy-start(f32[40,16,128]{2,1,0:T(8,128)} %uvel.1) | copy-start | bytes 983044
  0.7 1.4 %copy-start = (f32[40,16,128]{2,1,0:T(8,128)S(1)}, f32[40,16,128]{2,1,0:T(8,128)}, u32[]{:S(2)}) copy-start(f32[40,16,128]{2,1,0:T(8,128)} %temp.1) | copy-start | bytes 983044
  1.7 10.2 %collective-permute-start = (f32[288,128]{1,0:T(8,128)S(1)}, f32[288,128]{1,0:T(8,128)S(1)}, u32[]{:S(2)}, u32[]{:S(2)}) collective-permute-start(f32[288,128]{1,0:T(8,128)S(1)} %get-tuple-element.32.after), channel_id=1, source_target_pairs={{0,8},{8,0},{1,9},{9,1},{2,10},{10,2},{3,11},{11,3},{4,12},{12,4},... | collective-permute-start | bytes 442376 | tf_op jit(solution)/shard_map/ppermute | solution.py:438
  2.0 5.8 %copy-start.4 = (f32[40,16,128]{2,1,0:T(8,128)S(1)}, f32[40,16,128]{2,1,0:T(8,128)}, u32[]{:S(2)}) copy-start(f32[40,16,128]{2,1,0:T(8,128)} %param.13) | copy-start | bytes 983044
  2.6 9.4 %collective-permute-start.1 = (f32[288,128]{1,0:T(8,128)S(1)}, f32[288,128]{1,0:T(8,128)S(1)}, u32[]{:S(2)}, u32[]{:S(2)}) collective-permute-start(f32[288,128]{1,0:T(8,128)S(1)} %get-tuple-element.35), channel_id=1, source_target_pairs={{8,16},{16,8},{9,17},{17,9},{10,18},{18,10},{11,19},{19,11},{12,20... | collective-permute-start | bytes 442376 | tf_op jit(solution)/shard_map/ppermute | solution.py:459
  4.0 5.9 %collective-permute-start.4 = (f32[56,128]{1,0:T(8,128)S(1)}, f32[56,128]{1,0:T(8,128)S(1)}, u32[]{:S(2)}, u32[]{:S(2)}) collective-permute-start(f32[56,128]{1,0:T(8,128)S(1)} %get-tuple-element.39), channel_id=1, source_target_pairs={{1,2},{2,1},{3,4},{4,3},{5,6},{6,5},{7,0},{0,7},{9,10},{10,9},{11,... | collective-permute-start | bytes 86024 | tf_op jit(solution)/shard_map/ppermute | solution.py:461
  6.8 5.1 %collective-permute-start.2 = (f32[280,128]{1,0:T(8,128)S(1)}, f32[280,128]{1,0:T(8,128)S(1)}, u32[]{:S(2)}, u32[]{:S(2)}) collective-permute-start(f32[280,128]{1,0:T(8,128)S(1)} %get-tuple-element.36), channel_id=1, source_target_pairs={{16,24},{24,16},{17,25},{25,17},{18,26},{26,18},{19,27},{27,19},{2... | collective-permute-start | bytes 430088 | tf_op jit(solution)/shard_map/ppermute | solution.py:460
  7.8 1.7 %collective-permute-start.3 = (f32[48,128]{1,0:T(8,128)S(1)}, f32[48,128]{1,0:T(8,128)S(1)}, u32[]{:S(2)}, u32[]{:S(2)}) collective-permute-start(f32[48,128]{1,0:T(8,128)S(1)} %get-tuple-element.38), channel_id=1, source_target_pairs={{0,1},{1,0},{2,3},{3,2},{4,5},{5,4},{6,7},{7,6},{8,9},{9,8},{10,11... | collective-permute-start | bytes 73736 | tf_op jit(solution)/shard_map/ppermute | solution.py:462

commit v11 on v10

--- a/solution.py
+++ b/solution.py
@@ -108,9 +108,11 @@
         for pair in range(2):
             both = jnp.where(lane < 64, chosen(slabs[2 * pair]), chosen(slabs[2 * pair + 1]))
             out[pair * ROWS : (pair + 1) * ROWS, :] = both
-        out[2 * ROWS : 3 * ROWS, :] = chosen(slabs[TAIL])
+        last = chosen(slabs[TAIL])
+        place = 2 * ROWS
+        out[place : place + TILE, :] = jnp.where(lane[:TILE] < 64, last[:TILE], last[TILE:])
         if out is zonal2:
-            out[3 * ROWS :, :] = jnp.zeros((TILE, LANES), jnp.float32)
+            out[place + TILE :, :] = jnp.zeros((TILE, LANES), jnp.float32)
 
 
 def columns_kernel(mixing, levels, solve, middle):
@@ -256,7 +258,9 @@
         return jnp.take_along_axis(x, place + offset, axis=1, mode="promise_in_bounds")
 
     theirs = [spread_out(level(other, s // 2), 64 * (s % 2)) for s in range(TAIL)]
-    theirs.append(spread_out(level(other, 2), 0))
+    halves = jnp.concatenate([other[2 * ROWS : 2 * ROWS + TILE, :]] * 2, axis=0)
+    bottom = lax.broadcasted_iota(jnp.int32, (ROWS, LANES), 0) // TILE
+    theirs.append(spread_out(halves, 64 * bottom))
     both = [jnp.where(ghost, theirs[s], own[s]) for s in range(TAIL + 1)]
     near_lane = quad == jnp.where(west, 2, 1)
 
@@ -445,8 +449,8 @@
         out_shape=(
             f32(7 * depth + TILE, lanes),
             f32(7 * depth, lanes),
+            f32(2 * rows + TILE, lanes),
             f32(3 * rows, lanes),
-            f32(3 * rows + TILE, lanes),
             f32((TAIL + 1) * rows, lanes),
             f32(8 * depth, lanes),
             f32(8 * depth, lanes),
@@ -490,12 +494,12 @@
     second = pl.pallas_call(
         arrived_kernel,
         name="arrived",
-        out_shape=f32(3 * rows + TILE, lanes),
+        out_shape=f32(3 * rows, lanes),
         in_specs=[VMEM],
         out_specs=VMEM,
         input_output_aliases={0: 0},
         compiler_params=limit,
-        cost_estimate=pl.CostEstimate(flops=1250000000, bytes_accessed=1, transcendentals=0),
+        cost_estimate=pl.CostEstimate(flops=1280000000, bytes_accessed=1, transcendentals=0),
     )(second)
     outs = pl.pallas_call(
         finish_kernel,

time: 13.8 us -> 13.9 us (level)
  no operation moved by 1% of the time
where the time goes in v11:
time: 13.9 us; the launch traced here: 13.7 us
  Pallas kernels  5.38 us (39%)
  starting transfers between devices  5.35 us (38%)
  waiting for transfers between devices  2.03 us (15%)
  between operations  0.74 us (5%)
  local copies, waits for them, and re-layouts  0.22 us (2%)
    ppermute x1, starting transfers between devices, per_device(): second = lax.ppermute(zonal2, both, zonal_second)  2.81 us
    ppermute x1, waiting for transfers between devices, per_device(): got2 = lax.ppermute(sent2, both, meridional[2])  2.02 us
    pallas_call x1, Pallas kernels, per_device(): pl.pallas_call(finish_kernel, name='finish', out_shape=(f32(flat, lanes),...  1.75 us
    ppermute x1, starting transfers between devices, per_device(): got1 = lax.ppermute(sent1, both, meridional[1])  1.5 us
    pallas_call x1, Pallas kernels, per_device(): pl.pallas_call(interior_kernel, name='interior', out_shape=(f32(3, flat,...  1.48 us
    pallas_call x1, Pallas kernels, per_device(): pl.pallas_call(first_rows_kernel, name='first_rows', out_shape=(f32(7 * d...  1.04 us
    ppermute x1, starting transfers between devices, per_device(): got2 = lax.ppermute(sent2, both, meridional[2])  0.97 us
    pallas_call x1, Pallas kernels, per_device(): pl.pallas_call(edges_pack_kernel, name='edges_pack', out_shape=(f32(7 * d...  0.54 us
  transfers between devices with their start and end apart: 5, of which 1 were waited for; matrix products, arithmetic and copies ran while one was open for 0% of the time, Pallas kernels for 19%

profile of v11, /device:TPU:4, one launch (start us, length us, event | category | flops | bytes accessed | tf_op | source)
XLA Modules:
  0.0 13.7 jit_solution(11598421014096939005)
XLA Ops:
  0.6 0.0 copy-start.3
  0.6 0.0 copy-start.2
  0.7 0.0 copy-start.1
  0.7 0.0 copy-start
  0.7 1.0 %first_rows.1 = (f32[288,128]{1,0:T(8,128)S(1)}, f32[16,128]{1,0:T(8,128)S(1)}, f32[16,128]{1,0:T(8,128)S(1)}, f32[16,128]{1,0:T(8,128)S(1)}, f32[16,128]{1,0:T(8,128)S(1)}, /*index=5*/s32[16,128]{1,0:T(8,128)S(1)}) custom-call(f32[40,16,128]{2,1,0:T(8,128)} %temp.1, f32[40,16,128]{2,1,0:T(8,128)} %uvel.1, f32[40,16,128]{2,1,0:T(8,128)} %vvel.1, ...), custom_call_target="tpu_custom_call" | custom-call | flops 1 | bytes 1 | tf_op jit(solution)/shard_map/first_rows/pallas_call | solution.py:430
  1.7 0.1 collective-permute-start
  1.8 0.0 copy-done.3
  1.8 0.0 copy-done.2
  1.8 0.1 copy-done.1
  1.9 0.1 copy-done
  2.0 0.0 copy-start.4
  2.0 0.5 %edges_pack.1 = (f32[288,128]{1,0:T(8,128)S(1)}, f32[280,128]{1,0:T(8,128)S(1)}, f32[40,128]{1,0:T(8,128)S(1)}, f32[48,128]{1,0:T(8,128)S(1)}, f32[80,128]{1,0:T...) custom-call(f32[640,128]{1,0:T(8,128)S(1)} %bitcast.8, f32[640,128]{1,0:T(8,128)S(1)} %bitcast.10, ...), custom_call_target="tpu_custom_call" | custom-call | flops 1 | bytes 1 | tf_op jit(solution)/shard_map/edges_pack/pallas_call | solution.py:446
  2.6 1.5 %collective-permute-start.1 = (f32[288,128]{1,0:T(8,128)S(1)}, f32[288,128]{1,0:T(8,128)S(1)}, u32[]{:S(2)}, u32[]{:S(2)}) collective-permute-start(f32[288,128]{1,0:T(8,128)S(1)} %get-tuple-element.35), channel_id=1, source_target_pairs={{8,16},{16,8},{9,17},{17,9},{10,18},{18,10},{11,19},{19,11},{12,20... | collective-permute-start | bytes 442376 | tf_op jit(solution)/shard_map/ppermute | solution.py:463
  4.1 2.8 %collective-permute-start.4 = (f32[48,128]{1,0:T(8,128)S(1)}, f32[48,128]{1,0:T(8,128)S(1)}, u32[]{:S(2)}, u32[]{:S(2)}) collective-permute-start(f32[48,128]{1,0:T(8,128)S(1)} %get-tuple-element.39), channel_id=1, source_target_pairs={{1,2},{2,1},{3,4},{4,3},{5,6},{6,5},{7,0},{0,7},{9,10},{10,9},{11,... | collective-permute-start | bytes 73736 | tf_op jit(solution)/shard_map/ppermute | solution.py:465
  6.9 1.0 %collective-permute-start.2 = (f32[280,128]{1,0:T(8,128)S(1)}, f32[280,128]{1,0:T(8,128)S(1)}, u32[]{:S(2)}, u32[]{:S(2)}) collective-permute-start(f32[280,128]{1,0:T(8,128)S(1)} %get-tuple-element.36), channel_id=1, source_target_pairs={{16,24},{24,16},{17,25},{25,17},{18,26},{26,18},{19,27},{27,19},{2... | collective-permute-start | bytes 430088 | tf_op jit(solution)/shard_map/ppermute | solution.py:464
  7.8 0.0 collective-permute-start.3
  7.8 0.0 copy-done.4
  7.8 0.2 %columns.1 = (f32[3,640,128]{2,1,0:T(8,128)S(1)}, f32[16,128]{1,0:T(8,128)S(1)}) custom-call(f32[640,128]{1,0:T(8,128)S(1)} %bitcast.16, s32[16,128]{1,0:T(8,128)S(1)} %get-tuple-element.29.levels), custom_call_target="tpu_custom_call" | custom-call | flops 1 | bytes 1 | tf_op jit(solution)/shard_map/columns/pallas_call | solution.py:467
  8.1 1.5 %interior.1 = (f32[3,640,128]{2,1,0:T(8,128)S(1)}, f32[3,640,128]{2,1,0:T(8,128)S(1)}) custom-call(f32[640,128]{1,0:T(8,128)S(1)} %bitcast.9, f32[640,128]{1,0:T(8,128)S(1)} %bitcast.11, f32[640,128]{1,0:T(8,128)S(1)} %bitcast.13, s32[640,128]{1,0:T(8,128)S(1)} %bitcast.15, f32[16,128]{1,0:T(8,128)S(1)} %get-tuple-element.23.inv_dx, ...), custom_call_target="tpu_custom_call" | custom-call | flops 1 | bytes 1 | tf_op jit(solution)/shard_map/interior/pallas_call | solution.py:476
  9.5 0.0 collective-permute-done.3.other
  9.5 0.4 %columns_ghosts.1.packed = f32[96,128]{1,0:T(8,128)S(1)} custom-call(f32[80,128]{1,0:T(8,128)S(1)} %get-tuple-element.37.edges, f32[40,128]{1,0:T(8,128)S(1)} %collective-permute-done.3.other, f32[16,128]{1,0:T(8,128)S(1)} %get-tuple-element.23.inv_dx, f32[16,128]{1,0:T(8,128)S(1)} %get-tuple-element.25.spread), custom_call_target="tpu_custom_call" | custom-call | flops 1 | bytes 1 | tf_op jit(solution)/shard_map/columns_ghosts/pallas_call | solution.py:485
  9.9 0.0 collective-permute-done.4.other
  9.9 2.0 %collective-permute-done.2.got2 = f32[280,128]{1,0:T(8,128)S(1)} collective-permute-done((f32[280,128]{1,0:T(8,128)S(1)}, f32[280,128]{1,0:T(8,128)S(1)}, u32[]{:S(2)}, u32[]{:S(2)}) %collective-permute-start.2) | collective-permute-done | bytes 143392 | tf_op jit(solution)/shard_map/ppermute | solution.py:464
  12.0 0.0 collective-permute-done.got0
  12.0 0.0 collective-permute-done.1.got1
  12.0 1.7 %finish.1 = (f32[640,128]{1,0:T(8,128)}, f32[640,128]{1,0:T(8,128)}, f32[640,128]{1,0:T(8,128)}, f32[3,640,128]{2,1,0:T(8,128)S(1)}) custom-call(f32[3,640,128]{2,1,0:T(8,128)S(1)} %get-tuple-element.27.prov, f32[3,640,128]{2,1,0:T(8,128)S(1)} %get-tuple-element.28.extra_in, ...), custom_call_target="tpu_custom_call", output_to_operand_aliasing={{3}: (1, {})} | custom-call | flops 1 | bytes 1 | tf_op jit(solution)/shard_map/finish/pallas_call | solution.py:504
  (1 shorter events, 0.0 us)
Async XLA Ops:
  0.6 1.2 %copy-start.3 = (s32[40,16,128]{2,1,0:T(8,128)S(1)}, s32[40,16,128]{2,1,0:T(8,128)}, u32[]{:S(2)}) copy-start(s32[40,16,128]{2,1,0:T(8,128)} %mask.1) | copy-start | bytes 983044
  0.6 1.2 %copy-start.2 = (f32[40,16,128]{2,1,0:T(8,128)S(1)}, f32[40,16,128]{2,1,0:T(8,128)}, u32[]{:S(2)}) copy-start(f32[40,16,128]{2,1,0:T(8,128)} %vvel.1) | copy-start | bytes 983044
  0.7 1.3 %copy-start.1 = (f32[40,16,128]{2,1,0:T(8,128)S(1)}, f32[40,16,128]{2,1,0:T(8,128)}, u32[]{:S(2)}) copy-start(f32[40,16,128]{2,1,0:T(8,128)} %uvel.1) | copy-start | bytes 983044
  0.7 1.4 %copy-start = (f32[40,16,128]{2,1,0:T(8,128)S(1)}, f32[40,16,128]{2,1,0:T(8,128)}, u32[]{:S(2)}) copy-start(f32[40,16,128]{2,1,0:T(8,128)} %temp.1) | copy-start | bytes 983044
  1.7 10.3 %collective-permute-start = (f32[288,128]{1,0:T(8,128)S(1)}, f32[288,128]{1,0:T(8,128)S(1)}, u32[]{:S(2)}, u32[]{:S(2)}) collective-permute-start(f32[288,128]{1,0:T(8,128)S(1)} %get-tuple-element.32.after), channel_id=1, source_target_pairs={{0,8},{8,0},{1,9},{9,1},{2,10},{10,2},{3,11},{11,3},{4,12},{12,4},... | collective-permute-start | bytes 442376 | tf_op jit(solution)/shard_map/ppermute | solution.py:442
  2.0 5.8 %copy-start.4 = (f32[40,16,128]{2,1,0:T(8,128)S(1)}, f32[40,16,128]{2,1,0:T(8,128)}, u32[]{:S(2)}) copy-start(f32[40,16,128]{2,1,0:T(8,128)} %param.13) | copy-start | bytes 983044
  2.6 9.4 %collective-permute-start.1 = (f32[288,128]{1,0:T(8,128)S(1)}, f32[288,128]{1,0:T(8,128)S(1)}, u32[]{:S(2)}, u32[]{:S(2)}) collective-permute-start(f32[288,128]{1,0:T(8,128)S(1)} %get-tuple-element.35), channel_id=1, source_target_pairs={{8,16},{16,8},{9,17},{17,9},{10,18},{18,10},{11,19},{19,11},{12,20... | collective-permute-start | bytes 442376 | tf_op jit(solution)/shard_map/ppermute | solution.py:463
  4.1 5.9 %collective-permute-start.4 = (f32[48,128]{1,0:T(8,128)S(1)}, f32[48,128]{1,0:T(8,128)S(1)}, u32[]{:S(2)}, u32[]{:S(2)}) collective-permute-start(f32[48,128]{1,0:T(8,128)S(1)} %get-tuple-element.39), channel_id=1, source_target_pairs={{1,2},{2,1},{3,4},{4,3},{5,6},{6,5},{7,0},{0,7},{9,10},{10,9},{11,... | collective-permute-start | bytes 73736 | tf_op jit(solution)/shard_map/ppermute | solution.py:465
  6.9 5.1 %collective-permute-start.2 = (f32[280,128]{1,0:T(8,128)S(1)}, f32[280,128]{1,0:T(8,128)S(1)}, u32[]{:S(2)}, u32[]{:S(2)}) collective-permute-start(f32[280,128]{1,0:T(8,128)S(1)} %get-tuple-element.36), channel_id=1, source_target_pairs={{16,24},{24,16},{17,25},{25,17},{18,26},{26,18},{19,27},{27,19},{2... | collective-permute-start | bytes 430088 | tf_op jit(solution)/shard_map/ppermute | solution.py:464
  7.8 1.7 %collective-permute-start.3 = (f32[40,128]{1,0:T(8,128)S(1)}, f32[40,128]{1,0:T(8,128)S(1)}, u32[]{:S(2)}, u32[]{:S(2)}) collective-permute-start(f32[40,128]{1,0:T(8,128)S(1)} %get-tuple-element.38), channel_id=1, source_target_pairs={{0,1},{1,0},{2,3},{3,2},{4,5},{5,4},{6,7},{7,6},{8,9},{9,8},{10,11... | collective-permute-start | bytes 61448 | tf_op jit(solution)/shard_map/ppermute | solution.py:466

commit v12 on v10

--- a/solution.py
+++ b/solution.py
@@ -138,7 +138,10 @@
     middle[...] = 1.0 / (1.0 - chains[0] * chains[1])
 
 
-def interior_kernel(temp, uvel, vvel, mask, inv_dx, inv_dy, spread, coriolis, prov, zeros):
+def interior_kernel(
+    temp, uvel, vvel, mask, inv_dx, inv_dy, spread, coriolis, mixing, levels, prov, zeros, solve, middle_out
+):
+    columns_kernel(mixing, levels, solve, middle_out)
     depth = temp.shape[0] // ROWS
     lane = lane_index(ROWS)
     row = lax.broadcasted_iota(jnp.int32, (ROWS, LANES), 0)
@@ -460,24 +463,15 @@
     got2 = lax.ppermute(sent2, both, meridional[2])
     second = lax.ppermute(zonal2, both, zonal_second)
     first = lax.ppermute(zonal1, both, zonal_first)
-    solve, middle = pl.pallas_call(
-        columns_kernel,
-        name="columns",
-        out_shape=(f32(3, flat, lanes), f32(rows, lanes)),
-        in_specs=[VMEM] * 2,
-        out_specs=(VMEM,) * 2,
+    prov, zeros, solve, middle = pl.pallas_call(
+        interior_kernel,
+        name="interior",
+        out_shape=(f32(3, flat, lanes),) * 3 + (f32(rows, lanes),),
+        in_specs=[VMEM] * 10,
+        out_specs=(VMEM,) * 4,
         compiler_params=limit,
         cost_estimate=cheap,
-    )(vert_mixing, levels)
-    prov, zeros = pl.pallas_call(
-        interior_kernel,
-        name="interior",
-        out_shape=(f32(3, flat, lanes),) * 2,
-        in_specs=[VMEM] * 8,
-        out_specs=(VMEM,) * 2,
-        compiler_params=limit,
-        cost_estimate=cheap,
-    )(temp, uvel, vvel, wet_mask, inv_dx, inv_dy, horiz_mixing, coriolis)
+    )(temp, uvel, vvel, wet_mask, inv_dx, inv_dy, horiz_mixing, coriolis, vert_mixing, levels)
     packed = pl.pallas_call(
         columns_ghosts_kernel,
         name="columns_ghosts",

time: 13.8 us -> 13.9 us (level)
    pallas_call x1 -> x0, Pallas kernels: 0.2 us -> none  [per_device(): pl.pallas_call(columns_kernel, name='columns', out_shape=(f32(3, flat, la...]
    pallas_call x1, Pallas kernels: 1.48 us -> 1.63 us  [per_device(): pl.pallas_call(interior_kernel, name='interior', out_shape=(f32(3, flat,...]
where the time goes in v12:
time: 13.9 us; the launch traced here: 13.8 us
  Pallas kernels  5.4 us (39%)
  starting transfers between devices  5.3 us (38%)
  waiting for transfers between devices  2.09 us (15%)
  between operations  0.73 us (5%)
  local copies, waits for them, and re-layouts  0.22 us (2%)
    ppermute x1, starting transfers between devices, per_device(): second = lax.ppermute(zonal2, both, zonal_second)  2.81 us
    ppermute x1, waiting for transfers between devices, per_device(): got2 = lax.ppermute(sent2, both, meridional[2])  2.08 us
    pallas_call x1, Pallas kernels, per_device(): pl.pallas_call(finish_kernel, name='finish', out_shape=(f32(flat, lanes),...  1.8 us
    pallas_call x1, Pallas kernels, per_device(): pl.pallas_call(interior_kernel, name='interior', out_shape=(f32(3, flat,...  1.63 us
    ppermute x1, starting transfers between devices, per_device(): got1 = lax.ppermute(sent1, both, meridional[1])  1.45 us
    pallas_call x1, Pallas kernels, per_device(): pl.pallas_call(first_rows_kernel, name='first_rows', out_shape=(f32(7 * d...  1.04 us
    ppermute x1, starting transfers between devices, per_device(): got2 = lax.ppermute(sent2, both, meridional[2])  0.97 us
    pallas_call x1, Pallas kernels, per_device(): pl.pallas_call(edges_pack_kernel, name='edges_pack', out_shape=(f32(7 * d...  0.55 us
  transfers between devices with their start and end apart: 5, of which 1 were waited for; matrix products, arithmetic and copies ran while one was open for 0% of the time, Pallas kernels for 19%

profile of v12, /device:TPU:4, one launch (start us, length us, event | category | flops | bytes accessed | tf_op | source)
XLA Modules:
  0.0 13.8 jit_solution(16639072434946799106)
XLA Ops:
  0.6 0.0 copy-start.3
  0.6 0.0 copy-start.2
  0.7 0.0 copy-start.1
  0.7 0.0 copy-start
  0.7 1.0 %first_rows.1 = (f32[288,128]{1,0:T(8,128)S(1)}, f32[16,128]{1,0:T(8,128)S(1)}, f32[16,128]{1,0:T(8,128)S(1)}, f32[16,128]{1,0:T(8,128)S(1)}, f32[16,128]{1,0:T(8,128)S(1)}, /*index=5*/s32[16,128]{1,0:T(8,128)S(1)}) custom-call(f32[40,16,128]{2,1,0:T(8,128)} %temp.1, f32[40,16,128]{2,1,0:T(8,128)} %uvel.1, f32[40,16,128]{2,1,0:T(8,128)} %vvel.1, ...), custom_call_target="tpu_custom_call" | custom-call | flops 1 | bytes 1 | tf_op jit(solution)/shard_map/first_rows/pallas_call | solution.py:429
  1.7 0.1 collective-permute-start
  1.8 0.0 copy-done.3
  1.8 0.0 copy-done.2
  1.8 0.1 copy-done.1
  1.9 0.1 copy-done
  2.0 0.0 copy-start.4
  2.0 0.6 %edges_pack.1 = (f32[288,128]{1,0:T(8,128)S(1)}, f32[280,128]{1,0:T(8,128)S(1)}, f32[48,128]{1,0:T(8,128)S(1)}, f32[56,128]{1,0:T(8,128)S(1)}, f32[80,128]{1,0:T...) custom-call(f32[640,128]{1,0:T(8,128)S(1)} %bitcast.8, f32[640,128]{1,0:T(8,128)S(1)} %bitcast.10, ...), custom_call_target="tpu_custom_call" | custom-call | flops 1 | bytes 1 | tf_op jit(solution)/shard_map/edges_pack/pallas_call | solution.py:445
  2.6 1.5 %collective-permute-start.1 = (f32[288,128]{1,0:T(8,128)S(1)}, f32[288,128]{1,0:T(8,128)S(1)}, u32[]{:S(2)}, u32[]{:S(2)}) collective-permute-start(f32[288,128]{1,0:T(8,128)S(1)} %get-tuple-element.35), channel_id=1, source_target_pairs={{8,16},{16,8},{9,17},{17,9},{10,18},{18,10},{11,19},{19,11},{12,20... | collective-permute-start | bytes 442376 | tf_op jit(solution)/shard_map/ppermute | solution.py:462
  4.0 2.8 %collective-permute-start.4 = (f32[56,128]{1,0:T(8,128)S(1)}, f32[56,128]{1,0:T(8,128)S(1)}, u32[]{:S(2)}, u32[]{:S(2)}) collective-permute-start(f32[56,128]{1,0:T(8,128)S(1)} %get-tuple-element.39), channel_id=1, source_target_pairs={{1,2},{2,1},{3,4},{4,3},{5,6},{6,5},{7,0},{0,7},{9,10},{10,9},{11,... | collective-permute-start | bytes 86024 | tf_op jit(solution)/shard_map/ppermute | solution.py:464
  6.8 1.0 %collective-permute-start.2 = (f32[280,128]{1,0:T(8,128)S(1)}, f32[280,128]{1,0:T(8,128)S(1)}, u32[]{:S(2)}, u32[]{:S(2)}) collective-permute-start(f32[280,128]{1,0:T(8,128)S(1)} %get-tuple-element.36), channel_id=1, source_target_pairs={{16,24},{24,16},{17,25},{25,17},{18,26},{26,18},{19,27},{27,19},{2... | collective-permute-start | bytes 430088 | tf_op jit(solution)/shard_map/ppermute | solution.py:463
  7.8 0.0 collective-permute-start.3
  7.8 0.0 copy-done.4
  7.8 1.6 %interior.1 = (f32[3,640,128]{2,1,0:T(8,128)S(1)}, f32[3,640,128]{2,1,0:T(8,128)S(1)}, f32[3,640,128]{2,1,0:T(8,128)S(1)}, f32[16,128]{1,0:T(8,128)S(1)}) custom-call(f32[640,128]{1,0:T(8,128)S(1)} %bitcast.9, f32[640,128]{1,0:T(8,128)S(1)} %bitcast.11, f32[640,128]{1,0:T(8,128)S(1)} %bitcast.13, s32[640,128]{1,0:T(8,128)S(1)} %bitcast.15, ...), custom_call_target="tpu_custom_call" | custom-call | flops 1 | bytes 1 | tf_op jit(solution)/shard_map/interior/pallas_call | solution.py:466
  9.4 0.0 collective-permute-done.3.other
  9.5 0.4 %columns_ghosts.1.packed = f32[96,128]{1,0:T(8,128)S(1)} custom-call(f32[80,128]{1,0:T(8,128)S(1)} %get-tuple-element.37.edges, f32[48,128]{1,0:T(8,128)S(1)} %collective-permute-done.3.other, f32[16,128]{1,0:T(8,128)S(1)} %get-tuple-element.23.inv_dx, f32[16,128]{1,0:T(8,128)S(1)} %get-tuple-element.25.spread), custom_call_target="tpu_custom_call" | custom-call | flops 1 | bytes 1 | tf_op jit(solution)/shard_map/columns_ghosts/pallas_call | solution.py:475
  9.8 0.0 collective-permute-done.4.other
  9.9 2.1 %collective-permute-done.2.got2 = f32[280,128]{1,0:T(8,128)S(1)} collective-permute-done((f32[280,128]{1,0:T(8,128)S(1)}, f32[280,128]{1,0:T(8,128)S(1)}, u32[]{:S(2)}, u32[]{:S(2)}) %collective-permute-start.2) | collective-permute-done | bytes 143392 | tf_op jit(solution)/shard_map/ppermute | solution.py:463
  11.9 0.0 collective-permute-done.got0
  11.9 0.0 collective-permute-done.1.got1
  11.9 1.8 %finish.1 = (f32[640,128]{1,0:T(8,128)}, f32[640,128]{1,0:T(8,128)}, f32[640,128]{1,0:T(8,128)}, f32[3,640,128]{2,1,0:T(8,128)S(1)}) custom-call(f32[3,640,128]{2,1,0:T(8,128)S(1)} %get-tuple-element.28.prov, f32[3,640,128]{2,1,0:T(8,128)S(1)} %get-tuple-element.29.extra_in, ...), custom_call_target="tpu_custom_call", output_to_operand_aliasing={{3}: (1, {})} | custom-call | flops 1 | bytes 1 | tf_op jit(solution)/shard_map/finish/pallas_call | solution.py:494
  (1 shorter events, 0.0 us)
Async XLA Ops:
  0.6 1.2 %copy-start.3 = (s32[40,16,128]{2,1,0:T(8,128)S(1)}, s32[40,16,128]{2,1,0:T(8,128)}, u32[]{:S(2)}) copy-start(s32[40,16,128]{2,1,0:T(8,128)} %mask.1) | copy-start | bytes 983044
  0.6 1.2 %copy-start.2 = (f32[40,16,128]{2,1,0:T(8,128)S(1)}, f32[40,16,128]{2,1,0:T(8,128)}, u32[]{:S(2)}) copy-start(f32[40,16,128]{2,1,0:T(8,128)} %vvel.1) | copy-start | bytes 983044
  0.7 1.3 %copy-start.1 = (f32[40,16,128]{2,1,0:T(8,128)S(1)}, f32[40,16,128]{2,1,0:T(8,128)}, u32[]{:S(2)}) copy-start(f32[40,16,128]{2,1,0:T(8,128)} %uvel.1) | copy-start | bytes 983044
  0.7 1.4 %copy-start = (f32[40,16,128]{2,1,0:T(8,128)S(1)}, f32[40,16,128]{2,1,0:T(8,128)}, u32[]{:S(2)}) copy-start(f32[40,16,128]{2,1,0:T(8,128)} %temp.1) | copy-start | bytes 983044
  1.7 10.2 %collective-permute-start = (f32[288,128]{1,0:T(8,128)S(1)}, f32[288,128]{1,0:T(8,128)S(1)}, u32[]{:S(2)}, u32[]{:S(2)}) collective-permute-start(f32[288,128]{1,0:T(8,128)S(1)} %get-tuple-element.32.after), channel_id=1, source_target_pairs={{0,8},{8,0},{1,9},{9,1},{2,10},{10,2},{3,11},{11,3},{4,12},{12,4},... | collective-permute-start | bytes 442376 | tf_op jit(solution)/shard_map/ppermute | solution.py:441
  2.0 5.8 %copy-start.4 = (f32[40,16,128]{2,1,0:T(8,128)S(1)}, f32[40,16,128]{2,1,0:T(8,128)}, u32[]{:S(2)}) copy-start(f32[40,16,128]{2,1,0:T(8,128)} %param.13) | copy-start | bytes 983044
  2.6 9.4 %collective-permute-start.1 = (f32[288,128]{1,0:T(8,128)S(1)}, f32[288,128]{1,0:T(8,128)S(1)}, u32[]{:S(2)}, u32[]{:S(2)}) collective-permute-start(f32[288,128]{1,0:T(8,128)S(1)} %get-tuple-element.35), channel_id=1, source_target_pairs={{8,16},{16,8},{9,17},{17,9},{10,18},{18,10},{11,19},{19,11},{12,20... | collective-permute-start | bytes 442376 | tf_op jit(solution)/shard_map/ppermute | solution.py:462
  4.0 5.8 %collective-permute-start.4 = (f32[56,128]{1,0:T(8,128)S(1)}, f32[56,128]{1,0:T(8,128)S(1)}, u32[]{:S(2)}, u32[]{:S(2)}) collective-permute-start(f32[56,128]{1,0:T(8,128)S(1)} %get-tuple-element.39), channel_id=1, source_target_pairs={{1,2},{2,1},{3,4},{4,3},{5,6},{6,5},{7,0},{0,7},{9,10},{10,9},{11,... | collective-permute-start | bytes 86024 | tf_op jit(solution)/shard_map/ppermute | solution.py:464
  6.8 5.1 %collective-permute-start.2 = (f32[280,128]{1,0:T(8,128)S(1)}, f32[280,128]{1,0:T(8,128)S(1)}, u32[]{:S(2)}, u32[]{:S(2)}) collective-permute-start(f32[280,128]{1,0:T(8,128)S(1)} %get-tuple-element.36), channel_id=1, source_target_pairs={{16,24},{24,16},{17,25},{25,17},{18,26},{26,18},{19,27},{27,19},{2... | collective-permute-start | bytes 430088 | tf_op jit(solution)/shard_map/ppermute | solution.py:463
  7.8 1.6 %collective-permute-start.3 = (f32[48,128]{1,0:T(8,128)S(1)}, f32[48,128]{1,0:T(8,128)S(1)}, u32[]{:S(2)}, u32[]{:S(2)}) collective-permute-start(f32[48,128]{1,0:T(8,128)S(1)} %get-tuple-element.38), channel_id=1, source_target_pairs={{0,1},{1,0},{2,3},{3,2},{4,5},{5,4},{6,7},{7,6},{8,9},{9,8},{10,11... | collective-permute-start | bytes 73736 | tf_op jit(solution)/shard_map/ppermute | solution.py:465
